TPU v7x, 32 devices: a whole 2x2x4 slice. The times are simulated.
32 devices in a mesh: ctx: 8 (over y, x, core), head: 4 (over z).
Axes of the slice: x: 2, y: 2, z: 4, core: 2. Of those that a mesh axis runs over, the one named last changes fastest.
Arguments:
- inputs: bfloat16 [4096, 2048], P('ctx'), may hold values from -6 to 6
- w_query: bfloat16 [2048, 2048], P(None, 'head'), may hold values from -0.125 to 0.125
- w_key: bfloat16 [2048, 2048], P(None, 'head'), may hold values from -0.125 to 0.125
- w_value: bfloat16 [2048, 4096], P(None, 'head'), may hold values from -0.125 to 0.125
- w_gate_out: bfloat16 [2048, 4096], P(None, 'head'), may hold values from -0.125 to 0.125
- conv_query: float32 [4, 2048], P(None, 'head'), may hold values from -3 to 3
- conv_key: float32 [4, 2048], P(None, 'head'), may hold values from -3 to 3
- conv_value: float32 [4, 4096], P(None, 'head'), may hold values from -3 to 3
- decay_log: float32 [32, 4096], P('head', 'ctx'), may hold values from -1 to 0, as said below
- write_rate: float32 [32, 4096], P('head', 'ctx'), may hold values from 0 to 1, as said below
- w_out: bfloat16 [4096, 2048], P('head'), may hold values from -0.09375 to 0.09375
Outputs:
- mixed: bfloat16 [4096, 2048], P(('ctx', 'head'))
Inputs may be any that keep to these rules, and one draw needn't show every extreme that they name: `decay_log`: Negative. `write_rate`: Positive.
All inputs are finite; a program needn't handle non-finite values.
Results may differ from a plain program's by a relative error of at most 0.015.
Values may be sent and summed in bfloat16 or wider, within the bound.
No kernel may reach another device: no remote copies, remote signals or barrier semaphores. Data moves between devices by JAX's collectives and lax.ppermute only.
A program may use at most 128 MiB of HBM per device.

v0:
```python
import jax
import jax.numpy as jnp
from jax import lax
from jax.sharding import PartitionSpec as P

HD = 128
GROUP = 64


highest = lax.Precision.HIGHEST


def passed_along(value, axis, steps):
    count = lax.axis_size(axis)
    first, last = (max(0, -steps), min(count, count - steps))
    return lax.ppermute(value, axis, [(source, source + steps) for source in range(first, last)])


def causal_conv(projected, conv_rims, weights):
    kernel_len = weights.shape[0]
    row_count = projected.shape[0]
    padded = jnp.concatenate([conv_rims, projected], axis=0).astype(jnp.float32)
    summed = weights[0] * padded[0:row_count]
    for offset in range(1, kernel_len):
        summed = summed + weights[offset] * padded[offset : offset + row_count]
    return jax.nn.silu(summed)


def unit_rows(values, factor):
    return values * lax.rsqrt(jnp.sum(values * values, axis=-1, keepdims=True) + 1e-06) * factor


def head_inputs(
    proj_query,
    proj_key,
    proj_value,
    conv_query,
    conv_key,
    conv_value,
    rims_query,
    rims_key,
    rims_value,
    head_dim,
):
    row_count = proj_query.shape[0]
    key_heads = proj_query.shape[1] // head_dim
    value_heads = proj_value.shape[1] // head_dim
    ratio_heads = value_heads // key_heads
    conv_q = causal_conv(proj_query, rims_query, conv_query).reshape(row_count, key_heads, head_dim)
    conv_k = causal_conv(proj_key, rims_key, conv_key).reshape(row_count, key_heads, head_dim)
    conv_v = causal_conv(proj_value, rims_value, conv_value).reshape(
        row_count, value_heads, head_dim
    )
    queries = unit_rows(conv_q, head_dim ** (-0.5))
    keys_all = unit_rows(conv_k, 1.0)
    queries = jnp.repeat(queries, ratio_heads, axis=1)
    keys_all = jnp.repeat(keys_all, ratio_heads, axis=1)
    return (queries, keys_all, conv_v)


def to_groups(arrays, group_len):
    row_count, heads_count, feat = arrays.shape
    return arrays.reshape(row_count // group_len, group_len, heads_count, feat).transpose(
        0, 2, 1, 3
    )


def gates_to_groups(arrays, group_len):
    heads_count, row_count = arrays.shape
    return arrays.reshape(heads_count, row_count // group_len, group_len).transpose(1, 0, 2)


def group_pieces(query_blk, key_blk, value_blk, decay_blk, write_blk):
    group_len = decay_blk.shape[-1]
    key_len = key_blk.shape[-1]
    cumulative = jnp.cumsum(decay_blk, axis=-1)
    row_ids = lax.broadcasted_iota(jnp.int32, (group_len, group_len), 0)
    col_ids = lax.broadcasted_iota(jnp.int32, (group_len, group_len), 1)
    differ = cumulative[:, :, None] - cumulative[:, None, :]
    decay_mat = jnp.where(row_ids >= col_ids, jnp.exp(jnp.minimum(differ, 0.0)), 0.0)
    key_inner = jnp.einsum("hcd,hed->hce", key_blk, key_blk, precision=highest)
    strict_low = jnp.where(row_ids > col_ids, write_blk[:, :, None] * key_inner * decay_mat, 0.0)
    system = strict_low + jnp.eye(group_len, dtype=jnp.float32)
    scaled = jnp.exp(cumulative)
    right_side = jnp.concatenate(
        [key_blk * (write_blk * scaled)[:, :, None], value_blk * write_blk[:, :, None]], axis=-1
    )
    solved = lax.linalg.triangular_solve(
        system, right_side, left_side=True, lower=True, unit_diagonal=True
    )
    wy_keys = solved[..., :key_len]
    wy_values = solved[..., key_len:]
    scores = jnp.einsum("hcd,hed->hce", query_blk, key_blk, precision=highest) * decay_mat
    q_eff = query_blk * scaled[:, :, None] - jnp.einsum(
        "hce,hed->hcd", scores, wy_keys, precision=highest
    )
    group_end = cumulative[:, -1]
    k_eff = key_blk * jnp.exp(group_end[:, None] - cumulative)[:, :, None]
    carry_decay = jnp.exp(group_end)
    local_out = jnp.einsum("hce,hef->hcf", scores, wy_values, precision=highest)
    local_state = jnp.einsum("hcd,hcf->hdf", k_eff, wy_values, precision=highest)
    return (q_eff, k_eff, wy_keys, carry_decay, local_out, local_state)


def propagate(k_eff, wy_keys, carry_decay, state_now):
    removed = jnp.einsum("hcd,hdf->hcf", wy_keys, state_now, precision=highest)
    return carry_decay[:, None, None] * state_now - jnp.einsum(
        "hcd,hcf->hdf", k_eff, removed, precision=highest
    )


def apply_map(linear_part, state_now):
    return jnp.einsum("hij,hjf->hif", linear_part, state_now, precision=highest)


def gated_norm(attended, gate_in):
    row_count = attended.shape[0]
    gating = gate_in.astype(jnp.float32).reshape(attended.shape)
    scaled = attended * lax.rsqrt(jnp.mean(attended * attended, axis=-1, keepdims=True) + 1e-06)
    return (scaled * jax.nn.silu(gating)).astype(jnp.bfloat16).reshape(row_count, -1)


def shards(
    inputs,
    w_query,
    w_key,
    w_value,
    w_gate_out,
    conv_query,
    conv_key,
    conv_value,
    decay_log,
    write_rate,
    w_out,
):
    proj_query = jnp.dot(inputs, w_query, preferred_element_type=jnp.float32).astype(jnp.bfloat16)
    proj_key = jnp.dot(inputs, w_key, preferred_element_type=jnp.float32).astype(jnp.bfloat16)
    proj_value = jnp.dot(inputs, w_value, preferred_element_type=jnp.float32).astype(jnp.bfloat16)
    gate_in = jnp.dot(inputs, w_gate_out, preferred_element_type=jnp.float32).astype(jnp.bfloat16)
    rim_len = conv_query.shape[0] - 1
    width_q = proj_query.shape[1]
    width_k = proj_key.shape[1]
    tails = jnp.concatenate(
        [proj_query[-rim_len:], proj_key[-rim_len:], proj_value[-rim_len:]], axis=1
    )
    conv_rims = passed_along(tails, "ctx", 1)
    rims_query = conv_rims[:, :width_q]
    rims_key = conv_rims[:, width_q : width_q + width_k]
    rims_value = conv_rims[:, width_q + width_k :]
    queries, keys_all, values_all = head_inputs(
        proj_query,
        proj_key,
        proj_value,
        conv_query,
        conv_key,
        conv_value,
        rims_query,
        rims_key,
        rims_value,
        HD,
    )
    row_count, heads_local, head_dim = values_all.shape
    blocks = (
        to_groups(queries, GROUP),
        to_groups(keys_all, GROUP),
        to_groups(values_all, GROUP),
        gates_to_groups(decay_log, GROUP),
        gates_to_groups(write_rate, GROUP),
    )
    zero_state = jnp.zeros((heads_local, head_dim, head_dim), jnp.float32)
    identity = jnp.broadcast_to(
        jnp.eye(head_dim, dtype=jnp.float32), (heads_local, head_dim, head_dim)
    )

    def first_pass(carried, block_set):
        state_now, linear_now = carried
        q_eff, k_eff, wy_keys, carry_decay, local_out, local_state = group_pieces(*block_set)
        out_blk = local_out + jnp.einsum("hcd,hdf->hcf", q_eff, state_now, precision=highest)
        state_next = propagate(k_eff, wy_keys, carry_decay, state_now) + local_state
        linear_next = propagate(k_eff, wy_keys, carry_decay, linear_now)
        return ((state_next, linear_next), (out_blk, q_eff, k_eff, wy_keys, carry_decay))

    (local_final, linear_map), (outs_local, q_effs, k_effs, wy_all, decay_all) = lax.scan(
        first_pass, (zero_state, identity), blocks
    )

    def relay(turn_index, incoming_now):
        outgoing = apply_map(linear_map, incoming_now) + local_final
        return passed_along(outgoing, "ctx", 1)

    incoming = lax.fori_loop(0, lax.axis_size("ctx") - 1, relay, zero_state)

    def second_pass(state_now, block_set):
        q_eff, k_eff, wy_keys, carry_decay = block_set
        added = jnp.einsum("hcd,hdf->hcf", q_eff, state_now, precision=highest)
        return (propagate(k_eff, wy_keys, carry_decay, state_now), added)

    end_state, added_all = lax.scan(second_pass, incoming, (q_effs, k_effs, wy_all, decay_all))
    attended = (
        (outs_local + added_all).transpose(0, 2, 1, 3).reshape(row_count, heads_local, head_dim)
    )
    normed = gated_norm(attended, gate_in)
    return lax.psum_scatter(
        jnp.dot(normed, w_out, preferred_element_type=jnp.float32).astype(jnp.bfloat16),
        "head",
        scatter_dimension=0,
        tiled=True,
    )


def solution(mesh):
    return jax.shard_map(
        shards,
        mesh=mesh,
        in_specs=(
            P("ctx", None),
            P(None, "head"),
            P(None, "head"),
            P(None, "head"),
            P(None, "head"),
            P(None, "head"),
            P(None, "head"),
            P(None, "head"),
            P("head", "ctx"),
            P("head", "ctx"),
            P("head", None),
        ),
        out_specs=P(("ctx", "head"), None),
        check_vma=False,
    )
```

profile of v0, /device:TPU:0, one launch (start us, length us, event | category | flops | bytes accessed | tf_op | source)
XLA Modules:
  0.0 771.3 jit_solution(6824629090182038145)
XLA Ops:
  8.1 4.7 convolution_convert_fusion.2
  23.3 2.6 reshape.116
  50.9 496.0 %while.47 = (s32[]{:T(128)}, f32[8,128,128]{2,1,0:T(8,128)S(1)}, f32[8,128,128]{2,1,0:T(8,128)}, f32[8,8,64,128]{3,2,1,0:T(8,128)}, f32[8,8,64,128]{3,2,1,0:T(8,...) while((s32[]{:T(128)}, f32[8,128,128]{2,1,0:T(8,128)S(1)}, ...), condition=%wide.region_4.5_spmd.clone, body=%wide.region_2.4_spmd.clone.sunk | while | flops 908227136 | bytes 23152092 | solution.py:183
  55.1 40.0 %custom-call.7 = f32[8,1,64,64]{2,3,1,0:T(8,128)} custom-call(f32[8,1,64,64]{3,2,1,0:T(8,128)S(1)} %fusion.170), custom_call_target="InvertDiagBlocksLowerTriangular" | custom-call | tf_op jit(solution)/shard_map/while/body/eval_jaxpr/triangular_solve | solution.py:88
  109.1 2.9 convolution_subtract_fusion.9
  117.1 40.0 %custom-call.7 = f32[8,1,64,64]{2,3,1,0:T(8,128)} custom-call(f32[8,1,64,64]{3,2,1,0:T(8,128)S(1)} %fusion.170), custom_call_target="InvertDiagBlocksLowerTriangular" | custom-call | tf_op jit(solution)/shard_map/while/body/eval_jaxpr/triangular_solve | solution.py:88
  171.2 2.9 convolution_subtract_fusion.9
  179.2 40.0 %custom-call.7 = f32[8,1,64,64]{2,3,1,0:T(8,128)} custom-call(f32[8,1,64,64]{3,2,1,0:T(8,128)S(1)} %fusion.170), custom_call_target="InvertDiagBlocksLowerTriangular" | custom-call | tf_op jit(solution)/shard_map/while/body/eval_jaxpr/triangular_solve | solution.py:88
  233.2 2.9 convolution_subtract_fusion.9
  241.2 40.0 %custom-call.7 = f32[8,1,64,64]{2,3,1,0:T(8,128)} custom-call(f32[8,1,64,64]{3,2,1,0:T(8,128)S(1)} %fusion.170), custom_call_target="InvertDiagBlocksLowerTriangular" | custom-call | tf_op jit(solution)/shard_map/while/body/eval_jaxpr/triangular_solve | solution.py:88
  295.2 2.9 convolution_subtract_fusion.9
  303.2 40.0 %custom-call.7 = f32[8,1,64,64]{2,3,1,0:T(8,128)} custom-call(f32[8,1,64,64]{3,2,1,0:T(8,128)S(1)} %fusion.170), custom_call_target="InvertDiagBlocksLowerTriangular" | custom-call | tf_op jit(solution)/shard_map/while/body/eval_jaxpr/triangular_solve | solution.py:88
  357.2 2.9 convolution_subtract_fusion.9
  365.2 40.0 %custom-call.7 = f32[8,1,64,64]{2,3,1,0:T(8,128)} custom-call(f32[8,1,64,64]{3,2,1,0:T(8,128)S(1)} %fusion.170), custom_call_target="InvertDiagBlocksLowerTriangular" | custom-call | tf_op jit(solution)/shard_map/while/body/eval_jaxpr/triangular_solve | solution.py:88
  419.1 2.9 convolution_subtract_fusion.9
  427.1 40.0 %custom-call.7 = f32[8,1,64,64]{2,3,1,0:T(8,128)} custom-call(f32[8,1,64,64]{3,2,1,0:T(8,128)S(1)} %fusion.170), custom_call_target="InvertDiagBlocksLowerTriangular" | custom-call | tf_op jit(solution)/shard_map/while/body/eval_jaxpr/triangular_solve | solution.py:88
  481.1 2.9 convolution_subtract_fusion.9
  489.2 40.0 %custom-call.7 = f32[8,1,64,64]{2,3,1,0:T(8,128)} custom-call(f32[8,1,64,64]{3,2,1,0:T(8,128)S(1)} %fusion.170), custom_call_target="InvertDiagBlocksLowerTriangular" | custom-call | tf_op jit(solution)/shard_map/while/body/eval_jaxpr/triangular_solve | solution.py:88
  543.2 2.9 convolution_subtract_fusion.9
  547.0 87.7 %while.45 = (s32[]{:T(128)}, f32[8,128,128]{2,1,0:T(8,128)S(1)}, f32[8,128,128]{2,1,0:T(8,128)}, f32[8,128,128]{2,1,0:T(8,128)S(1)}, s32[]{:T(128)}) while((s32[]{:T(128)}, f32[8,128,128]{2,1,0:T(8,128)S(1)}, f32[8,128,128]{2,1,0:T(8,128)}, f32[8,128,128]{2,1,0:T(8,128)S(1)}, s32[]{:T(128)}) %tuple.85), condition=%wide.region_6.7_spmd, body=%wide.region_5.6_spmd.sunk | while | flops 201457664 | bytes 4194405 | solution.py:191
  549.5 4.6 collective-permute-start
  558.2 8.9 %collective-permute-start = (f32[8,128,128]{2,1,0:T(8,128)}, f32[8,128,128]{2,1,0:T(8,128)S(1)}, u32[]{:S(2)}, u32[]{:S(2)}) collective-permute-start(f32[8,128,128]{2,1,0:T(8,128)} %convolution_add_fusion.5), channel_id=1, source_target_pairs={{0,4},{4,8},{8,12},{12,16},{16,20},{20,24},{24,28},{1,5},{5,9},{9,... | collective-permute-start | bytes 1572872 | tf_op jit(solution)/shard_map/while/body/eval_jaxpr/ppermute | solution.py:16
  571.3 9.0 %collective-permute-start = (f32[8,128,128]{2,1,0:T(8,128)}, f32[8,128,128]{2,1,0:T(8,128)S(1)}, u32[]{:S(2)}, u32[]{:S(2)}) collective-permute-start(f32[8,128,128]{2,1,0:T(8,128)} %convolution_add_fusion.5), channel_id=1, source_target_pairs={{0,4},{4,8},{8,12},{12,16},{16,20},{20,24},{24,28},{1,5},{5,9},{9,... | collective-permute-start | bytes 1572872 | tf_op jit(solution)/shard_map/while/body/eval_jaxpr/ppermute | solution.py:16
  584.5 9.0 %collective-permute-start = (f32[8,128,128]{2,1,0:T(8,128)}, f32[8,128,128]{2,1,0:T(8,128)S(1)}, u32[]{:S(2)}, u32[]{:S(2)}) collective-permute-start(f32[8,128,128]{2,1,0:T(8,128)} %convolution_add_fusion.5), channel_id=1, source_target_pairs={{0,4},{4,8},{8,12},{12,16},{16,20},{20,24},{24,28},{1,5},{5,9},{9,... | collective-permute-start | bytes 1572872 | tf_op jit(solution)/shard_map/while/body/eval_jaxpr/ppermute | solution.py:16
  597.7 9.0 %collective-permute-start = (f32[8,128,128]{2,1,0:T(8,128)}, f32[8,128,128]{2,1,0:T(8,128)S(1)}, u32[]{:S(2)}, u32[]{:S(2)}) collective-permute-start(f32[8,128,128]{2,1,0:T(8,128)} %convolution_add_fusion.5), channel_id=1, source_target_pairs={{0,4},{4,8},{8,12},{12,16},{16,20},{20,24},{24,28},{1,5},{5,9},{9,... | collective-permute-start | bytes 1572872 | tf_op jit(solution)/shard_map/while/body/eval_jaxpr/ppermute | solution.py:16
  610.9 9.0 %collective-permute-start = (f32[8,128,128]{2,1,0:T(8,128)}, f32[8,128,128]{2,1,0:T(8,128)S(1)}, u32[]{:S(2)}, u32[]{:S(2)}) collective-permute-start(f32[8,128,128]{2,1,0:T(8,128)} %convolution_add_fusion.5), channel_id=1, source_target_pairs={{0,4},{4,8},{8,12},{12,16},{16,20},{20,24},{24,28},{1,5},{5,9},{9,... | collective-permute-start | bytes 1572872 | tf_op jit(solution)/shard_map/while/body/eval_jaxpr/ppermute | solution.py:16
  624.1 9.0 %collective-permute-start = (f32[8,128,128]{2,1,0:T(8,128)}, f32[8,128,128]{2,1,0:T(8,128)S(1)}, u32[]{:S(2)}, u32[]{:S(2)}) collective-permute-start(f32[8,128,128]{2,1,0:T(8,128)} %convolution_add_fusion.5), channel_id=1, source_target_pairs={{0,4},{4,8},{8,12},{12,16},{16,20},{20,24},{24,28},{1,5},{5,9},{9,... | collective-permute-start | bytes 1572872 | tf_op jit(solution)/shard_map/while/body/eval_jaxpr/ppermute | solution.py:16
  636.3 47.4 %while.46 = (s32[]{:T(128)}, f32[8,128,128]{2,1,0:T(8,128)S(1)}, f32[8,8,64,128]{3,2,1,0:T(8,128)}, f32[8,8]{1,0:T(8,128)S(1)}, f32[8,8,64,128]{3,2,1,0:T(8,128)...) while((s32[]{:T(128)}, f32[8,128,128]{2,1,0:T(8,128)S(1)}, ...), condition=%wide.region_8.9_spmd, body=%wide.region_7.8_spmd.sunk | while | flops 302252032 | bytes 3672249 | solution.py:198
  683.7 4.0 multiply_reduce_fusion
  687.9 4.1 copy.41
  693.9 11.1 %convolution_convert_fusion = bf16[512,2048]{1,0:T(8,128)(2,1)} fusion(bf16[1024,2048]{1,0:T(8,128)(2,1)} %param.27, f32[64,8,8,128]{3,2,1,0:T(8,128)} %bitcast.196, f32[64,8,8,128]{3,2,1,0:T(8,128)} %bitcast.197, bf16[512,2048]{1,0:T(8,128)(2,1)S(1)} %copy-done, bf16[2048,1024]{1,0:T(8,128)(2,1)} %param.21), kind=kOutput, calls=%fused_computation.93 | convolution fusion | flops 4300734464 | bytes 16777216 | tf_op jit(solution)/shard_map/dot_general | solution.py:204
  705.1 59.4 %reduce-scatter.2.cloned.1.call-done = bf16[128,2048]{1,0:T(8,128)(2,1)} async-done(((bf16[512,2048]{1,0:T(8,128)(2,1)}), bf16[128,2048]{1,0:T(8,128)(2,1)}) %reduce-scatter.2.cloned.1.call-update) | async-done | bytes 524304 | tf_op jit(solution)/shard_map/reduce_scatter | solution.py:203
  (332 shorter events, 268.5 us)
Async XLA Ops:
  6.5 1.6 copy-start
  6.5 757.9 %reduce-scatter.2.cloned.1.call-start = ((), (), s32[]{:S(2)}) async-start(), calls=%async_computation.1 | async-start | bytes 2621440 | tf_op jit(solution)/shard_map/reduce_scatter | solution.py:203
  8.1 4.7 copy-start.14
  12.8 1.3 copy-start.6
  12.8 2.0 copy-start.15
  14.8 3.7 copy-start.12
  14.8 3.7 copy-start.13
  14.8 3.7 copy-start.11
  14.8 3.8 copy-start.9
  14.8 3.9 copy-start.10
  16.1 2.5 copy-start.8
  16.1 3.2 collective-permute-start.1
  25.8 2.0 copy-start.3
  27.8 1.8 copy-start.2
  33.8 2.0 copy-start.4
  35.8 1.2 copy-start.7
  39.0 1.7 copy-start.5
  101.5 3.0 copy-start.1
  163.5 3.0 copy-start.1
  225.6 3.0 copy-start.1
  287.6 3.0 copy-start.1
  349.6 3.0 copy-start.1
  411.6 3.0 copy-start.1
  473.5 3.0 copy-start.1
  535.6 3.0 copy-start.1
  549.5 6.3 collective-permute-start
  558.2 10.6 %collective-permute-start = (f32[8,128,128]{2,1,0:T(8,128)}, f32[8,128,128]{2,1,0:T(8,128)S(1)}, u32[]{:S(2)}, u32[]{:S(2)}) collective-permute-start(f32[8,128,128]{2,1,0:T(8,128)} %convolution_add_fusion.5), channel_id=1, source_target_pairs={{0,4},{4,8},{8,12},{12,16},{16,20},{20,24},{24,28},{1,5},{5,9},{9,... | collective-permute-start | bytes 1572872 | tf_op jit(solution)/shard_map/while/body/eval_jaxpr/ppermute | solution.py:16
  571.3 10.7 %collective-permute-start = (f32[8,128,128]{2,1,0:T(8,128)}, f32[8,128,128]{2,1,0:T(8,128)S(1)}, u32[]{:S(2)}, u32[]{:S(2)}) collective-permute-start(f32[8,128,128]{2,1,0:T(8,128)} %convolution_add_fusion.5), channel_id=1, source_target_pairs={{0,4},{4,8},{8,12},{12,16},{16,20},{20,24},{24,28},{1,5},{5,9},{9,... | collective-permute-start | bytes 1572872 | tf_op jit(solution)/shard_map/while/body/eval_jaxpr/ppermute | solution.py:16
  584.5 10.7 %collective-permute-start = (f32[8,128,128]{2,1,0:T(8,128)}, f32[8,128,128]{2,1,0:T(8,128)S(1)}, u32[]{:S(2)}, u32[]{:S(2)}) collective-permute-start(f32[8,128,128]{2,1,0:T(8,128)} %convolution_add_fusion.5), channel_id=1, source_target_pairs={{0,4},{4,8},{8,12},{12,16},{16,20},{20,24},{24,28},{1,5},{5,9},{9,... | collective-permute-start | bytes 1572872 | tf_op jit(solution)/shard_map/while/body/eval_jaxpr/ppermute | solution.py:16
  597.7 10.7 %collective-permute-start = (f32[8,128,128]{2,1,0:T(8,128)}, f32[8,128,128]{2,1,0:T(8,128)S(1)}, u32[]{:S(2)}, u32[]{:S(2)}) collective-permute-start(f32[8,128,128]{2,1,0:T(8,128)} %convolution_add_fusion.5), channel_id=1, source_target_pairs={{0,4},{4,8},{8,12},{12,16},{16,20},{20,24},{24,28},{1,5},{5,9},{9,... | collective-permute-start | bytes 1572872 | tf_op jit(solution)/shard_map/while/body/eval_jaxpr/ppermute | solution.py:16
  610.9 10.7 %collective-permute-start = (f32[8,128,128]{2,1,0:T(8,128)}, f32[8,128,128]{2,1,0:T(8,128)S(1)}, u32[]{:S(2)}, u32[]{:S(2)}) collective-permute-start(f32[8,128,128]{2,1,0:T(8,128)} %convolution_add_fusion.5), channel_id=1, source_target_pairs={{0,4},{4,8},{8,12},{12,16},{16,20},{20,24},{24,28},{1,5},{5,9},{9,... | collective-permute-start | bytes 1572872 | tf_op jit(solution)/shard_map/while/body/eval_jaxpr/ppermute | solution.py:16
  624.1 10.7 %collective-permute-start = (f32[8,128,128]{2,1,0:T(8,128)}, f32[8,128,128]{2,1,0:T(8,128)S(1)}, u32[]{:S(2)}, u32[]{:S(2)}) collective-permute-start(f32[8,128,128]{2,1,0:T(8,128)} %convolution_add_fusion.5), channel_id=1, source_target_pairs={{0,4},{4,8},{8,12},{12,16},{16,20},{20,24},{24,28},{1,5},{5,9},{9,... | collective-permute-start | bytes 1572872 | tf_op jit(solution)/shard_map/while/body/eval_jaxpr/ppermute | solution.py:16
Sparse Core Ops, SparseCore 0:
  705.2 59.2 reduce-scatter.1
where the time goes:
time: 775 us; the launch traced here: 771 us
  other arithmetic  361 us (47%)
  matrix products  225 us (29%)
  waiting for transfers between devices  71.8 us (9%)
  starting transfers between devices  60.8 us (8%)
  local copies, waits for them, and re-layouts  37.3 us (5%)
  between operations  13.7 us (2%)
    another operation x32, other arithmetic, group_pieces(): lax.linalg.triangular_solve(system, right_side, left_side=True, lower=Tru...  320 us
    ppermute x8, starting transfers between devices, passed_along(): lax.ppermute(value, axis, [(source, source + steps) for source in range(f...  60.8 us
    reduce_scatter x1, waiting for transfers between devices, shards(): lax.psum_scatter(jnp.dot(normed, w_out, preferred_element_type=jnp.float3...  59.4 us
    dot_general x24, matrix products, propagate(): jnp.einsum('hcd,hcf->hdf', k_eff, removed, precision=highest)  49 us
    dot_general x24, matrix products, propagate(): removed = jnp.einsum('hcd,hdf->hcf', wy_keys, state_now, precision=highest)  29.9 us
    dot_general x8, matrix products, first_pass(): jnp.einsum('hcd,hdf->hcf', q_eff, state_now, precision=highest)  19.1 us
    dot_general x8, matrix products, second_pass(): added = jnp.einsum('hcd,hdf->hcf', q_eff, state_now, precision=highest)  18.1 us
    dot_general x7, matrix products, apply_map(): return jnp.einsum('hij,hjf->hif', linear_part, state_now, precision=highest)  17.3 us
  transfers between devices with their start and end apart: 9, of which 9 were waited for; matrix products, arithmetic and copies ran while one was open for 0% of the time, Pallas kernels for 0%

commit v1 on v0

v1 whole, which is shorter than its diff:
```python
import functools

import jax
import jax.numpy as jnp
from jax import lax
from jax.experimental import pallas as pl
from jax.experimental.pallas import tpu as pltpu
from jax.sharding import PartitionSpec as P

HD = 128
CHUNK = 128
RIM = 16
BF = jnp.bfloat16
F32 = jnp.float32
EXACT = lax.Precision.HIGHEST


def mm(left, right):
    return jnp.dot(left.astype(BF), right.astype(BF), preferred_element_type=F32)


def mm_nt(left, right):
    return lax.dot_general(
        left.astype(BF), right.astype(BF), (((1,), (1,)), ((), ())), preferred_element_type=F32
    )


def silu(values):
    return values / (1.0 + jnp.exp(-values))


def unit_rows(values, factor):
    return values * (lax.rsqrt(jnp.sum(values * values, axis=-1, keepdims=True) + 1e-06) * factor)


def stage_rows(stage, rims_ref, rows_ref):
    stage[0:8] = rims_ref[RIM - 8 : RIM].astype(F32)
    stage[8:] = rows_ref[...].astype(F32)


def conv_chunk(stage, taps, chunk):
    taps_len = taps.shape[0]
    start = 8 - (taps_len - 1) + chunk * CHUNK
    total = taps[0:1] * stage[start : start + CHUNK]
    for offset in range(1, taps_len):
        total = total + taps[offset : offset + 1] * stage[start + offset : start + offset + CHUNK]
    return silu(total)


def grid_ids():
    row_ids = lax.broadcasted_iota(jnp.int32, (CHUNK, CHUNK), 0)
    col_ids = lax.broadcasted_iota(jnp.int32, (CHUNK, CHUNK), 1)
    return row_ids, col_ids


def cumulated(decay):
    row_ids, col_ids = grid_ids()
    lower = jnp.where(row_ids >= col_ids, 1.0, 0.0)
    dims = (((1,), (1,)), ((), ()))
    as_rows = lax.dot_general(decay, lower, dims, precision=EXACT, preferred_element_type=F32)
    as_cols = lax.dot_general(lower, decay, dims, precision=EXACT, preferred_element_type=F32)
    return as_rows, as_cols


def inverted(systems):
    row_ids, col_ids = grid_ids()
    same = row_ids // 2 == col_ids // 2
    eye = jnp.where(row_ids == col_ids, 1.0, 0.0)
    inverses = [eye - jnp.where(same, system, 0.0) for system in systems]
    size = 2
    while size < CHUNK:
        cross = (row_ids // (2 * size) == col_ids // (2 * size)) & (
            row_ids // size != col_ids // size
        )
        links = [jnp.where(cross, system, 0.0).astype(BF) for system in systems]
        halves = [inverse.astype(BF) for inverse in inverses]
        if size < 8:
            inner = [mm(link, half) for link, half in zip(links, halves)]
            outer = [mm(half, part) for half, part in zip(halves, inner)]
            inverses = [inverse - part for inverse, part in zip(inverses, outer)]
        else:
            starts = range(size, CHUNK, 2 * size)
            odd = [
                jnp.concatenate([inverse[s : s + size] for s in starts], axis=0)
                for inverse in inverses
            ]
            inner = [mm(part, link) for part, link in zip(odd, links)]
            outer = [mm(part, half) for part, half in zip(inner, halves)]
            odd = [part - update for part, update in zip(odd, outer)]
            inverses = [
                jnp.concatenate(
                    [
                        piece
                        for at, s in enumerate(starts)
                        for piece in (
                            inverse[s - size : s],
                            part[at * size : (at + 1) * size],
                        )
                    ],
                    axis=0,
                )
                for inverse, part in zip(inverses, odd)
            ]
        size *= 2
    return inverses


def local_kernel(
    ratio,
    chunks,
    keys_ref,
    values_ref,
    rims_k_ref,
    rims_v_ref,
    taps_k_ref,
    taps_v_ref,
    decay_ref,
    write_ref,
    keys_out,
    wy_out,
    starts_out,
    map_out,
    stage_k,
    stage_v,
):
    row_ids, col_ids = grid_ids()
    stage_rows(stage_k, rims_k_ref, keys_ref)
    stage_rows(stage_v, rims_v_ref, values_ref)
    decay_rows, decay_cols = cumulated(decay_ref[0])
    write_cols = lax.dot_general(
        jnp.where(row_ids == col_ids, 1.0, 0.0),
        write_ref[0],
        (((1,), (1,)), ((), ())),
        precision=EXACT,
        preferred_element_type=F32,
    )
    taps_k = taps_k_ref[...]
    taps_v = taps_v_ref[...]
    keys = []
    flipped = []
    values = []
    inner = []
    for chunk in range(chunks):
        key = unit_rows(conv_chunk(stage_k, taps_k, chunk), 1.0)
        keys_out[chunk * CHUNK : (chunk + 1) * CHUNK] = key.astype(BF)
        keys.append(key)
        flipped.append(key.T)
        inner.append(mm(key, flipped[-1]))
        values.append(conv_chunk(stage_v, taps_v, chunk))
    units = [(head, chunk) for head in range(ratio) for chunk in range(chunks)]
    systems = []
    for head, chunk in units:
        at = head * chunks + chunk
        fading = jnp.exp(
            jnp.minimum(decay_cols[:, at : at + 1] - decay_rows[at : at + 1], 0.0)
        )
        systems.append(
            jnp.where(
                row_ids > col_ids, write_cols[:, at : at + 1] * inner[chunk] * fading, 0.0
            )
        )
    inverses = inverted(systems)
    maps = []
    for (head, chunk), inverse in zip(units, inverses):
        at = head * chunks + chunk
        col = decay_cols[:, at : at + 1]
        write = write_cols[:, at : at + 1]
        value = values[chunk][:, head * HD : (head + 1) * HD]
        right = jnp.concatenate([keys[chunk] * (write * jnp.exp(col)), value * write], axis=1)
        solved = mm(inverse, right).astype(BF)
        wy_out[head, chunk * CHUNK : (chunk + 1) * CHUNK] = solved
        row = decay_rows[at : at + 1]
        end = row[:, CHUNK - 1 : CHUNK]
        maps.append((mm(flipped[chunk] * jnp.exp(end - row), solved), jnp.exp(end)))
    eye = jnp.where(row_ids == col_ids, 1.0, 0.0)
    for head in range(ratio):
        state = None
        for chunk in range(chunks):
            product, end = maps[head * chunks + chunk]
            linear = eye * end - product[:, :HD]
            added = product[:, HD:]
            if state is None:
                state = jnp.concatenate([linear, added], axis=1)
            else:
                starts_out[head, chunk - 1] = state.astype(BF)
                moved = mm(linear, state)
                state = jnp.concatenate([moved[:, :HD], moved[:, HD:] + added], axis=1)
        map_out[head] = state.astype(BF)


def output_kernel(
    ratio,
    chunks,
    query_ref,
    rims_ref,
    taps_ref,
    keys_ref,
    wy_ref,
    starts_ref,
    decay_ref,
    parts_out,
    stage,
):
    row_ids, col_ids = grid_ids()
    stage_rows(stage, rims_ref, query_ref)
    decay_rows, decay_cols = cumulated(decay_ref[0])
    taps = taps_ref[...]
    for chunk in range(chunks):
        rows = slice(chunk * CHUNK, (chunk + 1) * CHUNK)
        query = unit_rows(conv_chunk(stage, taps, chunk), HD ** (-0.5))
        scores = mm_nt(query, keys_ref[rows])
        for head in range(ratio):
            at = head * chunks + chunk
            col = decay_cols[:, at : at + 1]
            fading = jnp.exp(jnp.minimum(col - decay_rows[at : at + 1], 0.0))
            weights = jnp.where(row_ids >= col_ids, scores * fading, 0.0)
            scaled = query * jnp.exp(col)
            wy = wy_ref[head, rows]
            if chunk == 0:
                whole = mm(weights, wy)
                linear = scaled - whole[:, :HD]
                local = whole[:, HD:]
            else:
                state = starts_ref[head, chunk - 1]
                removed = mm(wy[:, :HD], state)
                left = jnp.concatenate([scaled, weights], axis=1)
                rest = jnp.concatenate(
                    [-removed[:, :HD], wy[:, HD:].astype(F32) - removed[:, HD:]], axis=1
                ).astype(BF)
                whole = mm(left, jnp.concatenate([state, rest], axis=0))
                linear = whole[:, :HD]
                local = whole[:, HD:]
            parts_out[head, rows, :HD] = linear.astype(BF)
            parts_out[head, rows, HD:] = local.astype(BF)


def final_kernel(heads, parts_ref, state_ref, gate_ref, weight_ref, out_ref, normed):
    for head in range(heads):
        lanes = slice(head * HD, (head + 1) * HD)
        attended = parts_ref[head, :, HD:].astype(F32) + mm(
            parts_ref[head, :, :HD], state_ref[head]
        )
        spread = lax.rsqrt(jnp.mean(attended * attended, axis=-1, keepdims=True) + 1e-06)
        normed[:, lanes] = (attended * spread * silu(gate_ref[:, lanes].astype(F32))).astype(BF)
    out_ref[...] = jnp.dot(normed[...], weight_ref[...], preferred_element_type=F32).astype(BF)


def exchanged(value, axis, bit):
    count = lax.axis_size(axis)
    return lax.ppermute(value, axis, [(source, source ^ bit) for source in range(count)])


def after(later, earlier):
    moved = jnp.einsum(
        "hij,hjf->hif", later[..., :HD].astype(BF), earlier.astype(BF), preferred_element_type=F32
    )
    return moved.at[..., HD:].add(later[..., HD:])


def incoming_state(total, axis):
    count = lax.axis_size(axis)
    index = lax.axis_index(axis)
    heads = total.shape[0]
    total = total.astype(F32)
    eye = jnp.broadcast_to(jnp.eye(HD, dtype=F32), (heads, HD, HD))
    before = jnp.concatenate([eye, jnp.zeros_like(eye)], axis=-1)
    bit = 1
    while bit < count:
        other = exchanged(total.astype(BF), axis, bit).astype(F32)
        high = (index & bit) != 0
        before = jnp.where(high, after(before, other), before)
        if 2 * bit < count:
            total = after(jnp.where(high, total, other), jnp.where(high, other, total))
        bit *= 2
    return before[..., HD:]


def scattered_sum(value, axis):
    count = lax.axis_size(axis)
    index = lax.axis_index(axis)
    parts = value.reshape(count, value.shape[0] // count, value.shape[1])

    def take(at):
        return lax.dynamic_index_in_dim(parts, jnp.clip(at, 0, count - 1), 0, keepdims=False)

    up = down = None
    for step in range(count - 1):
        send_up = take(count - 1 - step + index)
        send_down = take(step - (count - 1 - index))
        if up is not None:
            send_up = (send_up.astype(F32) + up.astype(F32)).astype(BF)
            send_down = (send_down.astype(F32) + down.astype(F32)).astype(BF)
        up = lax.ppermute(send_up, axis, [(z, z + 1) for z in range(step + 1)])
        down = lax.ppermute(
            send_down, axis, [(count - 1 - z, count - 2 - z) for z in range(step + 1)]
        )
    own = take(index).astype(F32)
    return (own + up.astype(F32) + down.astype(F32)).astype(BF)


def shards(
    inputs,
    w_query,
    w_key,
    w_value,
    w_gate_out,
    conv_query,
    conv_key,
    conv_value,
    decay_log,
    write_rate,
    w_out,
):
    def project(weights):
        return jnp.dot(inputs, weights, preferred_element_type=F32).astype(BF)

    proj_key = project(w_key)
    proj_value = project(w_value)
    proj_query = project(w_query)
    rows = inputs.shape[0]
    key_width = proj_key.shape[1]
    key_heads = key_width // HD
    heads = proj_value.shape[1] // HD
    ratio = heads // key_heads
    chunks = rows // CHUNK
    tails = jnp.concatenate(
        [proj_key[-RIM:], proj_value[-RIM:], proj_query[-RIM:]], axis=1
    )
    count = lax.axis_size("ctx")
    rims = lax.ppermute(tails, "ctx", [(at, at + 1) for at in range(count - 1)])
    gate_in = project(w_gate_out)
    rims_k = rims[:, :key_width]
    rims_v = rims[:, key_width : key_width + heads * HD]
    rims_q = rims[:, key_width + heads * HD :]
    decay = decay_log.reshape(key_heads, ratio * chunks, CHUNK)
    write = write_rate.reshape(key_heads, ratio * chunks, CHUNK)

    def cols(length, width):
        return pl.BlockSpec((length, width), lambda h: (0, h))

    gate_spec = pl.BlockSpec((1, ratio * chunks, CHUNK), lambda h: (h, 0, 0))
    wy_spec = pl.BlockSpec((ratio, rows, 2 * HD), lambda h: (h, 0, 0))
    starts_spec = pl.BlockSpec((ratio, chunks - 1, HD, 2 * HD), lambda h: (h, 0, 0, 0))
    taps_len = conv_key.shape[0]
    keys, wy, starts, total = pl.pallas_call(
        functools.partial(local_kernel, ratio, chunks),
        grid=(key_heads,),
        in_specs=[
            cols(rows, HD),
            cols(rows, ratio * HD),
            cols(RIM, HD),
            cols(RIM, ratio * HD),
            cols(taps_len, HD),
            cols(taps_len, ratio * HD),
            gate_spec,
            gate_spec,
        ],
        out_specs=[
            cols(rows, HD),
            wy_spec,
            starts_spec,
            pl.BlockSpec((ratio, HD, 2 * HD), lambda h: (h, 0, 0)),
        ],
        out_shape=[
            jax.ShapeDtypeStruct((rows, key_width), BF),
            jax.ShapeDtypeStruct((heads, rows, 2 * HD), BF),
            jax.ShapeDtypeStruct((heads, chunks - 1, HD, 2 * HD), BF),
            jax.ShapeDtypeStruct((heads, HD, 2 * HD), BF),
        ],
        scratch_shapes=[
            pltpu.VMEM((rows + 8, HD), F32),
            pltpu.VMEM((rows + 8, ratio * HD), F32),
        ],
        name="local",
    )(proj_key, proj_value, rims_k, rims_v, conv_key, conv_value, decay, write)
    parts = pl.pallas_call(
        functools.partial(output_kernel, ratio, chunks),
        grid=(key_heads,),
        in_specs=[
            cols(rows, HD),
            cols(RIM, HD),
            cols(taps_len, HD),
            cols(rows, HD),
            wy_spec,
            starts_spec,
            gate_spec,
        ],
        out_specs=wy_spec,
        out_shape=jax.ShapeDtypeStruct((heads, rows, 2 * HD), BF),
        scratch_shapes=[pltpu.VMEM((rows + 8, HD), F32)],
        name="outputs",
    )(proj_query, rims_q, conv_query, keys, wy, starts, decay)
    state = incoming_state(total, "ctx").astype(BF)
    width_out = w_out.shape[1]
    partial_out = pl.pallas_call(
        functools.partial(final_kernel, heads),
        grid=(chunks,),
        in_specs=[
            pl.BlockSpec((heads, CHUNK, 2 * HD), lambda c: (0, c, 0)),
            pl.BlockSpec((heads, HD, HD), lambda c: (0, 0, 0)),
            pl.BlockSpec((CHUNK, heads * HD), lambda c: (c, 0)),
            pl.BlockSpec((heads * HD, width_out), lambda c: (0, 0)),
        ],
        out_specs=pl.BlockSpec((CHUNK, width_out), lambda c: (c, 0)),
        out_shape=jax.ShapeDtypeStruct((rows, width_out), BF),
        scratch_shapes=[pltpu.VMEM((CHUNK, heads * HD), BF)],
        name="final",
    )(parts, state, gate_in, w_out)
    return scattered_sum(partial_out, "head")


def solution(mesh):
    return jax.shard_map(
        shards,
        mesh=mesh,
        in_specs=(
            P("ctx", None),
            P(None, "head"),
            P(None, "head"),
            P(None, "head"),
            P(None, "head"),
            P(None, "head"),
            P(None, "head"),
            P(None, "head"),
            P("head", "ctx"),
            P("head", "ctx"),
            P("head", None),
        ),
        out_specs=P(("ctx", "head"), None),
        check_vma=False,
    )
```

time: 775 us -> 150 us (0.19)
  other arithmetic: 361 us -> 9.84 us
  matrix products: 225 us -> 13.7 us
  starting transfers between devices: 60.8 us -> 26.5 us
  Pallas kernels: 0 us -> 30.9 us
  local copies, waits for them, and re-layouts: 37.3 us -> 7.07 us
  between operations: 13.7 us -> 0.39 us
  waiting for transfers between devices: 71.8 us -> 61 us
    another operation x40 -> x1, other arithmetic: 322 us -> 0.78 us  [the longest x32 320 us: group_pieces(): lax.linalg.triangular_solve(system, right_side, left_side=True, lower=Tru...]
    dot_general x115 -> x9, matrix products: 212 us -> 13.7 us  [the longest x4 12.2 us: project(): return jnp.dot(inputs, weights, preferred_element_type=F32).astype(BF)]
    reduce_scatter x1 -> x0, waiting for transfers between devices: 59.4 us -> none  [shards(): lax.psum_scatter(jnp.dot(normed, w_out, preferred_element_type=jnp.float3...]
    ppermute x8 -> x10, waiting for transfers between devices: 12.4 us -> 61 us  [the longest x3 24.1 us: scattered_sum(): up = lax.ppermute(send_up, axis, [(z, z + 1) for z in range(step + 1)])]
    ppermute x8 -> x10, starting transfers between devices: 60.8 us -> 26.5 us  [the longest x3 12.9 us: scattered_sum(): up = lax.ppermute(send_up, axis, [(z, z + 1) for z in range(step + 1)])]
    pallas_call x0 -> x3, Pallas kernels: none -> 30.9 us  [the longest x1 15.8 us: shards(): pl.pallas_call(functools.partial(local_kernel, ratio, chunks), grid=(key_...]
    mul x12 -> x0, other arithmetic: 20 us -> none  [the longest x8 15.5 us: group_pieces(): key_blk * (write_blk * scaled)[:, :, None]]
    another operation x8 -> x0, matrix products: 13.3 us -> none  [group_pieces(): lax.linalg.triangular_solve(system, right_side, left_side=True, lower=Tru...]
  transfers between devices with their start and end apart: 9 -> 10, of which waited for: 9 -> 6; matrix products, arithmetic and copies ran while one was open for 0% -> 7% of each run, Pallas kernels for 0% -> 5%
where the time goes in v1:
time: 150 us; the launch traced here: 149 us
  waiting for transfers between devices  61 us (41%)
  Pallas kernels  30.9 us (21%)
  starting transfers between devices  26.5 us (18%)
  matrix products  13.7 us (9%)
  other arithmetic  9.84 us (7%)
  local copies, waits for them, and re-layouts  7.07 us (5%)
    ppermute x3, waiting for transfers between devices, scattered_sum(): up = lax.ppermute(send_up, axis, [(z, z + 1) for z in range(step + 1)])  24.1 us
    ppermute x3, waiting for transfers between devices, exchanged(): lax.ppermute(value, axis, [(source, source ^ bit) for source in range(cou...  23.2 us
    pallas_call x1, Pallas kernels, shards(): pl.pallas_call(functools.partial(local_kernel, ratio, chunks), grid=(key_...  15.8 us
    ppermute x3, waiting for transfers between devices, scattered_sum(): lax.ppermute(send_down, axis, [(count - 1 - z, count - 2 - z) for z in ra...  13.6 us
    ppermute x3, starting transfers between devices, scattered_sum(): up = lax.ppermute(send_up, axis, [(z, z + 1) for z in range(step + 1)])  12.9 us
    dot_general x4, matrix products, project(): return jnp.dot(inputs, weights, preferred_element_type=F32).astype(BF)  12.2 us
    pallas_call x1, Pallas kernels, shards(): pl.pallas_call(functools.partial(final_kernel, heads), grid=(chunks,), in...  7.87 us
    ppermute x3, starting transfers between devices, exchanged(): lax.ppermute(value, axis, [(source, source ^ bit) for source in range(cou...  7.57 us
  transfers between devices with their start and end apart: 10, of which 6 were waited for; matrix products, arithmetic and copies ran while one was open for 7% of the time, Pallas kernels for 5%

profile of v1, /device:TPU:0, one launch (start us, length us, event | category | flops | bytes accessed | tf_op | source)
XLA Modules:
  0.0 149.4 jit_solution(12508284831544772574)
XLA Ops:
  0.0 1.6 %copy-done = bf16[512,2048]{1,0:T(8,128)(2,1)S(1)} copy-done((bf16[512,2048]{1,0:T(8,128)(2,1)S(1)}, bf16[512,2048]{1,0:T(8,128)(2,1)}, u32[]{:S(2)}) %copy-start) | copy-done | bytes 2097176
  1.6 3.1 %convolution_convert_fusion.3.query_ref = bf16[512,512]{1,0:T(8,128)(2,1)S(1)} fusion(bf16[512,2048]{1,0:T(8,128)(2,1)S(1)} %copy-done, bf16[2048,512]{1,0:T(8,128)(2,1)} %param.22), kind=kOutput, calls=%fused_computation.7 | convolution fusion | flops 1074003968 | bytes 4718592 | tf_op jit(solution)/shard_map/dot_general | solution.py:315
  4.7 2.4 %convolution_convert_fusion.1.values_ref = bf16[512,1024]{1,0:T(8,128)(2,1)S(1)} fusion(bf16[512,2048]{1,0:T(8,128)(2,1)S(1)} %copy-done, bf16[2048,1024]{1,0:T(8,128)(2,1)S(1)} %copy-done.7), kind=kOutput, calls=%fused_computation.1 | convolution fusion | flops 2148007936 | bytes 7340032 | tf_op jit(solution)/shard_map/dot_general | solution.py:315
  7.2 1.2 convolution_convert_fusion.2.keys_ref
  8.5 0.8 copy-done.3
  9.2 2.5 %collective-permute-start = (bf16[16,2048]{1,0:T(8,128)(2,1)S(1)}, bf16[16,2048]{1,0:T(8,128)(2,1)S(1)}, u32[]{:S(2)}, u32[]{:S(2)}) collective-permute-start(bf16[16,2048]{1,0:T(8,128)(2,1)S(1)} %pad_maximum_fusion), channel_id=1, source_target_pairs={{0,4},{4,8},{8,12},{12,16},{16,20},{20,24},{24,28},{1,5},{5,9},{9,... | collective-permute-start | bytes 196616 | tf_op jit(solution)/shard_map/ppermute | solution.py:330
  13.7 0.6 slice.192.rims_v_ref
  14.3 15.8 %local.1 = (bf16[512,512]{1,0:T(8,128)(2,1)}, bf16[8,512,256]{2,1,0:T(8,128)(2,1)}, bf16[8,3,128,256]{3,2,1,0:T(8,128)(2,1)}, bf16[8,128,256]{2,1,0:T(8,128)(2,1)}) custom-call(bf16[512,512]{1,0:T(8,128)(2,1)} %copy-done.3, bf16[512,1024]{1,0:T(8,128)(2,1)} %copy-done.2, bf16[16,512]{1,0:T(8,128)(2,1)} %get-tuple-element.77.rims_k_ref, ...), custom_call_target="tpu_custom_call" | custom-call | tf_op jit(solution)/shard_map/local/pallas_call | solution.py:345
  30.1 2.7 %collective-permute-start.1 = (bf16[8,128,256]{2,1,0:T(8,128)(2,1)}, bf16[8,128,256]{2,1,0:T(8,128)(2,1)S(1)}, u32[]{:S(2)}, u32[]{:S(2)}) collective-permute-start(bf16[8,128,256]{2,1,0:T(8,128)(2,1)} %get-tuple-element.72), channel_id=1, source_target_pairs={{0,4},{4,0},{8,12},{12,8},{16,20},{20,16},{24,28},{28,24},{1,5},{5... | collective-permute-start | bytes 1572872 | tf_op jit(solution)/shard_map/ppermute | solution.py:250
  32.8 5.5 %convolution_convert_fusion.gate_ref = bf16[512,1024]{1,0:T(8,128)(2,1)} fusion(bf16[512,2048]{1,0:T(8,128)(2,1)S(1)} %copy-done, bf16[2048,1024]{1,0:T(8,128)(2,1)} %param.25), kind=kOutput, calls=%fused_computation | convolution fusion | flops 2148007936 | bytes 7340032 | tf_op jit(solution)/shard_map/dot_general | solution.py:315
  38.3 7.3 %outputs.1.parts_ref = bf16[8,512,256]{2,1,0:T(8,128)(2,1)} custom-call(bf16[512,512]{1,0:T(8,128)(2,1)} %copy-done.4, bf16[16,512]{1,0:T(8,128)(2,1)} %get-tuple-element.78.rims_ref, f32[4,512]{1,0:T(4,128)} %taps_ref.1, bf16[512,512]{1,0:T(8,128)(2,1)} %get-tuple-element.69.keys_ref, bf16[8,512,256]{2,1,0:T(8,128)(2,1)} %get-tuple-element.70.wy_ref, ...), custom_call_target="tpu_custom_call" | custom-call | tf_op jit(solution)/shard_map/outputs/pallas_call | solution.py:376
  46.2 2.2 %collective-permute-start.2 = (bf16[8,128,256]{2,1,0:T(8,128)(2,1)S(1)}, bf16[8,128,256]{2,1,0:T(8,128)(2,1)S(1)}, u32[]{:S(2)}, u32[]{:S(2)}) collective-permute-start(bf16[8,128,256]{2,1,0:T(8,128)(2,1)S(1)} %convert_element_type.123), channel_id=1, source_target_pairs={{0,8},{4,12},{8,0},{12,4},{16,24},{20,28},{24,16},{28,20},{1,9},{5... | collective-permute-start | bytes 1572872 | tf_op jit(solution)/shard_map/ppermute | solution.py:250
  48.9 12.0 %collective-permute-done.2 = bf16[8,128,256]{2,1,0:T(8,128)(2,1)S(1)} collective-permute-done((bf16[8,128,256]{2,1,0:T(8,128)(2,1)S(1)}, bf16[8,128,256]{2,1,0:T(8,128)(2,1)S(1)}, u32[]{:S(2)}, u32[]{:S(2)}) %collective-permute-start.2) | collective-permute-done | bytes 524320 | tf_op jit(solution)/shard_map/ppermute | solution.py:250
  61.6 2.7 %collective-permute-start.3 = (bf16[8,128,256]{2,1,0:T(8,128)(2,1)S(1)}, bf16[8,128,256]{2,1,0:T(8,128)(2,1)S(1)}, u32[]{:S(2)}, u32[]{:S(2)}) collective-permute-start(bf16[8,128,256]{2,1,0:T(8,128)(2,1)S(1)} %convert_element_type.126), channel_id=1, source_target_pairs={{0,16},{4,20},{8,24},{12,28},{16,0},{20,4},{24,8},{28,12},{1,17},{... | collective-permute-start | bytes 1572872 | tf_op jit(solution)/shard_map/ppermute | solution.py:250
  64.9 11.2 %collective-permute-done.3 = bf16[8,128,256]{2,1,0:T(8,128)(2,1)S(1)} collective-permute-done((bf16[8,128,256]{2,1,0:T(8,128)(2,1)S(1)}, bf16[8,128,256]{2,1,0:T(8,128)(2,1)S(1)}, u32[]{:S(2)}, u32[]{:S(2)}) %collective-permute-start.3) | collective-permute-done | bytes 524320 | tf_op jit(solution)/shard_map/ppermute | solution.py:250
  76.5 0.8 fusion.12.state_ref
  77.3 7.9 %final.1 = bf16[512,2048]{1,0:T(8,128)(2,1)} custom-call(bf16[8,512,256]{2,1,0:T(8,128)(2,1)} %outputs.1.parts_ref, bf16[8,128,128]{2,1,0:T(8,128)(2,1)} %fusion.12.state_ref, bf16[512,1024]{1,0:T(8,128)(2,1)} %convolution_convert_fusion.gate_ref, bf16[1024,2048]{1,0:T(8,128)(2,1)} %weight_ref.1), custom_call_target="tpu_custom_call" | custom-call | tf_op jit(solution)/shard_map/final/pallas_call | solution.py:395
  85.2 2.1 %dynamic-slice_bitcast_fusion.1 = (bf16[128,2048]{1,0:T(8,128)(2,1)S(1)}, bf16[128,2048]{1,0:T(8,128)(2,1)}) fusion(bf16[4,128,2048]{2,1,0:T(8,128)(2,1)} %bitcast.31, s32[]{:T(128)S(6)} %min.25, s32[]{:T(128)S(6)} %min.28), kind=kLoop, calls=%fused_computation.40 | loop fusion | bytes 2097160 | tf_op jit(solution)/shard_map/jit(dynamic_index_in_dim)/squeeze | solution.py:284
  87.2 3.5 %collective-permute-start.4 = (bf16[128,2048]{1,0:T(8,128)(2,1)S(1)}, bf16[128,2048]{1,0:T(8,128)(2,1)S(1)}, u32[]{:S(2)}, u32[]{:S(2)}) collective-permute-start(bf16[128,2048]{1,0:T(8,128)(2,1)S(1)} %get-tuple-element.75), channel_id=1, source_target_pairs={{0,1},{4,5},{8,9},{12,13},{16,17},{20,21},{24,25},{28,29}} | collective-permute-start | bytes 1572872 | tf_op jit(solution)/shard_map/ppermute | solution.py:293
  90.8 1.5 collective-permute-start.7
  92.2 9.0 %collective-permute-done.4 = bf16[128,2048]{1,0:T(8,128)(2,1)S(1)} collective-permute-done((bf16[128,2048]{1,0:T(8,128)(2,1)S(1)}, bf16[128,2048]{1,0:T(8,128)(2,1)S(1)}, u32[]{:S(2)}, u32[]{:S(2)}) %collective-permute-start.4) | collective-permute-done | bytes 524320 | tf_op jit(solution)/shard_map/ppermute | solution.py:293
  101.2 1.2 fusion.4
  102.4 4.4 %collective-permute-start.5 = (bf16[128,2048]{1,0:T(8,128)(2,1)S(1)}, bf16[128,2048]{1,0:T(8,128)(2,1)S(1)}, u32[]{:S(2)}, u32[]{:S(2)}) collective-permute-start(bf16[128,2048]{1,0:T(8,128)(2,1)S(1)} %fusion.4), channel_id=1, source_target_pairs={{0,1},{1,2},{4,5},{5,6},{8,9},{9,10},{12,13},{13,14},{16,17},{17,1... | collective-permute-start | bytes 1572872 | tf_op jit(solution)/shard_map/ppermute | solution.py:293
  106.8 9.5 %collective-permute-done.5 = bf16[128,2048]{1,0:T(8,128)(2,1)S(1)} collective-permute-done((bf16[128,2048]{1,0:T(8,128)(2,1)S(1)}, bf16[128,2048]{1,0:T(8,128)(2,1)S(1)}, u32[]{:S(2)}, u32[]{:S(2)}) %collective-permute-start.5) | collective-permute-done | bytes 524320 | tf_op jit(solution)/shard_map/ppermute | solution.py:293
  116.3 2.7 %fusion.5 = (bf16[128,2048]{1,0:T(8,128)(2,1)}, bf16[128,2048]{1,0:T(8,128)(2,1)}) fusion(bf16[128,2048]{1,0:T(8,128)(2,1)S(1)} %collective-permute-done.5, bf16[4,128,2048]{2,1,0:T(8,128)(2,1)} %bitcast.33, s32[]{:T(128)S(6)} %min.23, bf16[128,2048]{1,0:T(8,128)(2,1)} %collective-permute-done.7, s32[]{:T(128)S(6)} %min.27), kind=kLoop, calls=%fused_computation.17 | loop fusion | flops 2097152 | bytes 3145736 | tf_op jit(solution)/shard_map/convert_element_type | solution.py:291
  119.1 0.7 collective-permute-start.8
  119.7 5.0 %collective-permute-start.6 = (bf16[128,2048]{1,0:T(8,128)(2,1)}, bf16[128,2048]{1,0:T(8,128)(2,1)S(1)}, u32[]{:S(2)}, u32[]{:S(2)}) collective-permute-start(bf16[128,2048]{1,0:T(8,128)(2,1)} %get-tuple-element.73), channel_id=1, source_target_pairs={{0,1},{1,2},{2,3},{4,5},{5,6},{6,7},{8,9},{9,10},{10,11},{12,13},{... | collective-permute-start | bytes 1572872 | tf_op jit(solution)/shard_map/ppermute | solution.py:293
  124.8 2.0 %fusion.3 = bf16[128,2048]{1,0:T(8,128)(2,1)} fusion(bf16[128,2048]{1,0:T(8,128)(2,1)S(1)} %collective-permute-done.8, bf16[4,128,2048]{2,1,0:T(8,128)(2,1)} %bitcast.34, s32[]{:T(128)S(6)} %min.26), kind=kLoop, calls=%fused_computation.13 | loop fusion | flops 1048576 | bytes 1572868 | tf_op jit(solution)/shard_map/convert_element_type | solution.py:292
  126.8 1.3 collective-permute-start.9
  128.0 5.7 %collective-permute-done.6 = bf16[128,2048]{1,0:T(8,128)(2,1)S(1)} collective-permute-done((bf16[128,2048]{1,0:T(8,128)(2,1)}, bf16[128,2048]{1,0:T(8,128)(2,1)S(1)}, u32[]{:S(2)}, u32[]{:S(2)}) %collective-permute-start.6) | collective-permute-done | bytes 524320 | tf_op jit(solution)/shard_map/ppermute | solution.py:293
  133.7 13.6 %collective-permute-done.9 = bf16[128,2048]{1,0:T(8,128)(2,1)S(1)} collective-permute-done((bf16[128,2048]{1,0:T(8,128)(2,1)}, bf16[128,2048]{1,0:T(8,128)(2,1)S(1)}, u32[]{:S(2)}, u32[]{:S(2)}) %collective-permute-start.9) | collective-permute-done | bytes 524320 | tf_op jit(solution)/shard_map/ppermute | solution.py:294
  147.3 2.1 %fusion.7 = bf16[128,2048]{1,0:T(8,128)(2,1)} fusion(bf16[128,2048]{1,0:T(8,128)(2,1)S(1)} %collective-permute-done.9, bf16[128,2048]{1,0:T(8,128)(2,1)S(1)} %collective-permute-done.6, bf16[4,128,2048]{2,1,0:T(8,128)(2,1)} %bitcast.35, s32[]{:T(128)S(6)} %min.22), kind=kLoop, calls=%fused_computation.20 | loop fusion | flops 1572864 | bytes 2097156 | tf_op jit(solution)/shard_map/convert_element_type | solution.py:298
  (47 shorter events, 4.6 us)
Async XLA Ops:
  0.0 1.6 %copy-start = (bf16[512,2048]{1,0:T(8,128)(2,1)S(1)}, bf16[512,2048]{1,0:T(8,128)(2,1)}, u32[]{:S(2)}) copy-start(bf16[512,2048]{1,0:T(8,128)(2,1)} %param.21) | copy-start | bytes 6291460
  0.0 4.7 %copy-start.7 = (bf16[2048,1024]{1,0:T(8,128)(2,1)S(1)}, bf16[2048,1024]{1,0:T(8,128)(2,1)}, u32[]{:S(2)}) copy-start(bf16[2048,1024]{1,0:T(8,128)(2,1)} %param.24) | copy-start | bytes 12582916
  4.7 2.4 %copy-start.4 = (bf16[512,512]{1,0:T(8,128)(2,1)}, bf16[512,512]{1,0:T(8,128)(2,1)S(1)}, u32[]{:S(2)}) copy-start(bf16[512,512]{1,0:T(8,128)(2,1)S(1)} %convolution_convert_fusion.3.query_ref) | copy-start | bytes 1572868
  4.7 2.4 %copy-start.8 = (bf16[2048,512]{1,0:T(8,128)(2,1)S(1)}, bf16[2048,512]{1,0:T(8,128)(2,1)}, u32[]{:S(2)}) copy-start(bf16[2048,512]{1,0:T(8,128)(2,1)} %param.23) | copy-start | bytes 6291460
  7.1 1.3 copy-start.2
  7.1 2.1 %slice-start = ((bf16[512,512]{1,0:T(8,128)(2,1)}), bf16[16,512]{1,0:T(8,128)(2,1)S(1)}, s32[]{:S(2)}) async-start(bf16[512,512]{1,0:T(8,128)(2,1)} %copy-done.4), calls=%async_computation | async-start | bytes 32768 | tf_op jit(solution)/shard_map/slice | solution.py:327
  7.2 4.7 %copy-start.5 = (f32[8,512]{1,0:T(8,128)S(1)}, f32[8,512]{1,0:T(8,128)}, u32[]{:S(2)}) copy-start(f32[8,512]{1,0:T(8,128)} %param.29) | copy-start | bytes 49156
  7.2 5.3 %copy-start.6 = (f32[8,512]{1,0:T(8,128)S(1)}, f32[8,512]{1,0:T(8,128)}, u32[]{:S(2)}) copy-start(f32[8,512]{1,0:T(8,128)} %param.30) | copy-start | bytes 49156
  8.4 0.8 copy-start.3
  9.2 3.8 %collective-permute-start = (bf16[16,2048]{1,0:T(8,128)(2,1)S(1)}, bf16[16,2048]{1,0:T(8,128)(2,1)S(1)}, u32[]{:S(2)}, u32[]{:S(2)}) collective-permute-start(bf16[16,2048]{1,0:T(8,128)(2,1)S(1)} %pad_maximum_fusion), channel_id=1, source_target_pairs={{0,4},{4,8},{8,12},{12,16},{16,20},{20,24},{24,28},{1,5},{5,9},{9,... | collective-permute-start | bytes 196616 | tf_op jit(solution)/shard_map/ppermute | solution.py:330
  30.1 15.4 %collective-permute-start.1 = (bf16[8,128,256]{2,1,0:T(8,128)(2,1)}, bf16[8,128,256]{2,1,0:T(8,128)(2,1)S(1)}, u32[]{:S(2)}, u32[]{:S(2)}) collective-permute-start(bf16[8,128,256]{2,1,0:T(8,128)(2,1)} %get-tuple-element.72), channel_id=1, source_target_pairs={{0,4},{4,0},{8,12},{12,8},{16,20},{20,16},{24,28},{28,24},{1,5},{5... | collective-permute-start | bytes 1572872 | tf_op jit(solution)/shard_map/ppermute | solution.py:250
  38.3 7.3 %copy-start.1 = (bf16[8,128,256]{2,1,0:T(8,128)(2,1)S(1)}, bf16[8,128,256]{2,1,0:T(8,128)(2,1)}, u32[]{:S(2)}) copy-start(bf16[8,128,256]{2,1,0:T(8,128)(2,1)} %get-tuple-element.72) | copy-start | bytes 1572868
  46.2 14.8 %collective-permute-start.2 = (bf16[8,128,256]{2,1,0:T(8,128)(2,1)S(1)}, bf16[8,128,256]{2,1,0:T(8,128)(2,1)S(1)}, u32[]{:S(2)}, u32[]{:S(2)}) collective-permute-start(bf16[8,128,256]{2,1,0:T(8,128)(2,1)S(1)} %convert_element_type.123), channel_id=1, source_target_pairs={{0,8},{4,12},{8,0},{12,4},{16,24},{20,28},{24,16},{28,20},{1,9},{5... | collective-permute-start | bytes 1572872 | tf_op jit(solution)/shard_map/ppermute | solution.py:250
  61.6 14.5 %collective-permute-start.3 = (bf16[8,128,256]{2,1,0:T(8,128)(2,1)S(1)}, bf16[8,128,256]{2,1,0:T(8,128)(2,1)S(1)}, u32[]{:S(2)}, u32[]{:S(2)}) collective-permute-start(bf16[8,128,256]{2,1,0:T(8,128)(2,1)S(1)} %convert_element_type.126), channel_id=1, source_target_pairs={{0,16},{4,20},{8,24},{12,28},{16,0},{20,4},{24,8},{28,12},{1,17},{... | collective-permute-start | bytes 1572872 | tf_op jit(solution)/shard_map/ppermute | solution.py:250
  87.2 14.0 %collective-permute-start.4 = (bf16[128,2048]{1,0:T(8,128)(2,1)S(1)}, bf16[128,2048]{1,0:T(8,128)(2,1)S(1)}, u32[]{:S(2)}, u32[]{:S(2)}) collective-permute-start(bf16[128,2048]{1,0:T(8,128)(2,1)S(1)} %get-tuple-element.75), channel_id=1, source_target_pairs={{0,1},{4,5},{8,9},{12,13},{16,17},{20,21},{24,25},{28,29}} | collective-permute-start | bytes 1572872 | tf_op jit(solution)/shard_map/ppermute | solution.py:293
  90.8 16.1 %collective-permute-start.7 = (bf16[128,2048]{1,0:T(8,128)(2,1)}, bf16[128,2048]{1,0:T(8,128)(2,1)}, u32[]{:S(2)}, u32[]{:S(2)}) collective-permute-start(bf16[128,2048]{1,0:T(8,128)(2,1)} %get-tuple-element.76), channel_id=1, source_target_pairs={{3,2},{7,6},{11,10},{15,14},{19,18},{23,22},{27,26},{31,30}} | collective-permute-start | bytes 1572872 | tf_op jit(solution)/shard_map/ppermute | solution.py:294
  102.4 14.0 %collective-permute-start.5 = (bf16[128,2048]{1,0:T(8,128)(2,1)S(1)}, bf16[128,2048]{1,0:T(8,128)(2,1)S(1)}, u32[]{:S(2)}, u32[]{:S(2)}) collective-permute-start(bf16[128,2048]{1,0:T(8,128)(2,1)S(1)} %fusion.4), channel_id=1, source_target_pairs={{0,1},{1,2},{4,5},{5,6},{8,9},{9,10},{12,13},{13,14},{16,17},{17,1... | collective-permute-start | bytes 1572872 | tf_op jit(solution)/shard_map/ppermute | solution.py:293
  119.1 5.7 %collective-permute-start.8 = (bf16[128,2048]{1,0:T(8,128)(2,1)}, bf16[128,2048]{1,0:T(8,128)(2,1)S(1)}, u32[]{:S(2)}, u32[]{:S(2)}) collective-permute-start(bf16[128,2048]{1,0:T(8,128)(2,1)} %get-tuple-element.74), channel_id=1, source_target_pairs={{3,2},{2,1},{7,6},{6,5},{11,10},{10,9},{15,14},{14,13},{19,18},{18... | collective-permute-start | bytes 1572872 | tf_op jit(solution)/shard_map/ppermute | solution.py:294
  119.7 13.9 %collective-permute-start.6 = (bf16[128,2048]{1,0:T(8,128)(2,1)}, bf16[128,2048]{1,0:T(8,128)(2,1)S(1)}, u32[]{:S(2)}, u32[]{:S(2)}) collective-permute-start(bf16[128,2048]{1,0:T(8,128)(2,1)} %get-tuple-element.73), channel_id=1, source_target_pairs={{0,1},{1,2},{2,3},{4,5},{5,6},{6,7},{8,9},{9,10},{10,11},{12,13},{... | collective-permute-start | bytes 1572872 | tf_op jit(solution)/shard_map/ppermute | solution.py:293
  126.8 20.6 %collective-permute-start.9 = (bf16[128,2048]{1,0:T(8,128)(2,1)}, bf16[128,2048]{1,0:T(8,128)(2,1)S(1)}, u32[]{:S(2)}, u32[]{:S(2)}) collective-permute-start(bf16[128,2048]{1,0:T(8,128)(2,1)} %fusion.3), channel_id=1, source_target_pairs={{3,2},{2,1},{1,0},{7,6},{6,5},{5,4},{11,10},{10,9},{9,8},{15,14},{... | collective-permute-start | bytes 1572872 | tf_op jit(solution)/shard_map/ppermute | solution.py:294

commit v2 on v1

--- a/solution.py
+++ b/solution.py
@@ -60,6 +60,19 @@
     as_rows = lax.dot_general(decay, lower, dims, precision=EXACT, preferred_element_type=F32)
     as_cols = lax.dot_general(lower, decay, dims, precision=EXACT, preferred_element_type=F32)
     return as_rows, as_cols
+
+
+def head_rows(ref, ratio, chunks):
+    start = pl.program_id(0) * ratio
+    rows = [ref[pl.ds(start + head, 1), :] for head in range(ratio)]
+    return jnp.concatenate(
+        [
+            row[:, chunk * CHUNK : (chunk + 1) * CHUNK]
+            for chunk in range(chunks)
+            for row in rows
+        ],
+        axis=0,
+    )
 
 
 def inverted(systems):
@@ -126,10 +139,10 @@
     row_ids, col_ids = grid_ids()
     stage_rows(stage_k, rims_k_ref, keys_ref)
     stage_rows(stage_v, rims_v_ref, values_ref)
-    decay_rows, decay_cols = cumulated(decay_ref[0])
+    decay_rows, decay_cols = cumulated(head_rows(decay_ref, ratio, chunks))
     write_cols = lax.dot_general(
         jnp.where(row_ids == col_ids, 1.0, 0.0),
-        write_ref[0],
+        head_rows(write_ref, ratio, chunks),
         (((1,), (1,)), ((), ())),
         precision=EXACT,
         preferred_element_type=F32,
@@ -150,7 +163,7 @@
     units = [(head, chunk) for head in range(ratio) for chunk in range(chunks)]
     systems = []
     for head, chunk in units:
-        at = head * chunks + chunk
+        at = chunk * ratio + head
         fading = jnp.exp(
             jnp.minimum(decay_cols[:, at : at + 1] - decay_rows[at : at + 1], 0.0)
         )
@@ -162,7 +175,7 @@
     inverses = inverted(systems)
     maps = []
     for (head, chunk), inverse in zip(units, inverses):
-        at = head * chunks + chunk
+        at = chunk * ratio + head
         col = decay_cols[:, at : at + 1]
         write = write_cols[:, at : at + 1]
         value = values[chunk][:, head * HD : (head + 1) * HD]
@@ -203,14 +216,14 @@
 ):
     row_ids, col_ids = grid_ids()
     stage_rows(stage, rims_ref, query_ref)
-    decay_rows, decay_cols = cumulated(decay_ref[0])
+    decay_rows, decay_cols = cumulated(head_rows(decay_ref, ratio, chunks))
     taps = taps_ref[...]
     for chunk in range(chunks):
         rows = slice(chunk * CHUNK, (chunk + 1) * CHUNK)
         query = unit_rows(conv_chunk(stage, taps, chunk), HD ** (-0.5))
         scores = mm_nt(query, keys_ref[rows])
         for head in range(ratio):
-            at = head * chunks + chunk
+            at = chunk * ratio + head
             col = decay_cols[:, at : at + 1]
             fading = jnp.exp(jnp.minimum(col - decay_rows[at : at + 1], 0.0))
             weights = jnp.where(row_ids >= col_ids, scores * fading, 0.0)
@@ -234,15 +247,41 @@
             parts_out[head, rows, HD:] = local.astype(BF)
 
 
-def final_kernel(heads, parts_ref, state_ref, gate_ref, weight_ref, out_ref, normed):
+def final_kernel(heads, first, plan_ref, parts_ref, kept_ref, got_ref, gate_ref, weight_ref, out_ref, normed):
+    swap = plan_ref[0] != 0
+    half = heads // 2
     for head in range(heads):
         lanes = slice(head * HD, (head + 1) * HD)
-        attended = parts_ref[head, :, HD:].astype(F32) + mm(
-            parts_ref[head, :, :HD], state_ref[head]
-        )
+        kept, got = kept_ref[head % half], got_ref[head % half]
+        state = jnp.where(swap, got, kept) if head < half else jnp.where(swap, kept, got)
+        attended = parts_ref[head, :, HD:].astype(F32) + mm(parts_ref[head, :, :HD], state)
         spread = lax.rsqrt(jnp.mean(attended * attended, axis=-1, keepdims=True) + 1e-06)
         normed[:, lanes] = (attended * spread * silu(gate_ref[:, lanes].astype(F32))).astype(BF)
-    out_ref[...] = jnp.dot(normed[...], weight_ref[...], preferred_element_type=F32).astype(BF)
+    out_ref[0] = jnp.dot(normed[...], weight_ref[...], preferred_element_type=F32).astype(BF)
+
+
+def final_rows(first, count, plan, parts, kept, got, gate_in, w_out, length):
+    heads = parts.shape[0]
+    width = w_out.shape[1]
+    return pl.pallas_call(
+        functools.partial(final_kernel, heads, first),
+        grid_spec=pltpu.PrefetchScalarGridSpec(
+            num_scalar_prefetch=1,
+            grid=(count,),
+            in_specs=[
+                pl.BlockSpec((heads, length, 2 * HD), lambda c, plan: (0, plan[1 + first + c], 0)),
+                pl.BlockSpec(memory_space=pltpu.VMEM),
+                pl.BlockSpec(memory_space=pltpu.VMEM),
+                pl.BlockSpec((length, heads * HD), lambda c, plan: (plan[1 + first + c], 0)),
+                pl.BlockSpec(memory_space=pltpu.VMEM),
+            ],
+            out_specs=pl.BlockSpec((1, length, width), lambda c, plan: (c, 0, 0)),
+            scratch_shapes=[pltpu.VMEM((length, heads * HD), BF)],
+        ),
+        out_shape=jax.ShapeDtypeStruct((count, length, width), BF),
+        compiler_params=pltpu.CompilerParams(vmem_limit_bytes=16 << 20),
+        name="final",
+    )(plan, parts, kept, got, gate_in, w_out)
 
 
 def exchanged(value, axis, bit):
@@ -254,31 +293,78 @@
     moved = jnp.einsum(
         "hij,hjf->hif", later[..., :HD].astype(BF), earlier.astype(BF), preferred_element_type=F32
     )
-    return moved.at[..., HD:].add(later[..., HD:])
-
-
-def incoming_state(total, axis):
+    if earlier.shape[-1] == HD:
+        return moved + later[..., HD:].astype(F32)
+    return jnp.concatenate([moved[..., :HD], moved[..., HD:] + later[..., HD:].astype(F32)], axis=-1)
+
+
+def incoming_state(total, axis, covers):
+    covers = list(covers)
     count = lax.axis_size(axis)
     index = lax.axis_index(axis)
-    heads = total.shape[0]
-    total = total.astype(F32)
-    eye = jnp.broadcast_to(jnp.eye(HD, dtype=F32), (heads, HD, HD))
-    before = jnp.concatenate([eye, jnp.zeros_like(eye)], axis=-1)
-    bit = 1
+
+    def cover(value):
+        for at, work in enumerate(covers):
+            if work is not None:
+                value, work = lax.optimization_barrier((value, work))
+                done.append(work)
+                covers[at] = None
+                break
+        return value
+
+    done = []
+    odd = (index & 1) != 0
+    half = total.shape[0] // 2
+    mine = jnp.where(odd, total[half:], total[:half])
+    other = exchanged(jnp.where(odd, total[:half], total[half:]), axis, 1)
+    first = jnp.where(odd, other, mine)
+    second = jnp.where(odd, mine, other)
+    total = after(second, first).astype(BF)
+    before_map = before_state = None
+    bit = 2
     while bit < count:
-        other = exchanged(total.astype(BF), axis, bit).astype(F32)
         high = (index & bit) != 0
-        before = jnp.where(high, after(before, other), before)
-        if 2 * bit < count:
-            total = after(jnp.where(high, total, other), jnp.where(high, other, total))
+        last = 2 * bit >= count
+        if last and before_map is not None:
+            pairs = [(at, at ^ bit) for at in range(count) if not at & bit]
+            state = cover(lax.ppermute(total[..., HD:], axis, pairs))
+            moved = after(jnp.concatenate([before_map, before_state], axis=-1), state)
+            before_state = jnp.where(high, moved, before_state.astype(F32))
+        else:
+            other = cover(exchanged(total, axis, bit))
+            if before_map is None:
+                eye = jnp.broadcast_to(jnp.eye(HD, dtype=BF), (half, HD, HD))
+                before_map = jnp.where(high, other[..., :HD], eye)
+                before_state = jnp.where(high, other[..., HD:], jnp.zeros((), BF))
+            else:
+                before = jnp.concatenate([before_map, before_state], axis=-1)
+                moved = jnp.where(high, after(before, other), before.astype(F32)).astype(BF)
+                before_map, before_state = moved[..., :HD], moved[..., HD:]
+            if not last:
+                total = after(
+                    jnp.where(high, total, other), jnp.where(high, other, total)
+                ).astype(BF)
         bit *= 2
-    return before[..., HD:]
-
-
-def scattered_sum(value, axis):
+    if before_state is None:
+        before_state = jnp.zeros((half, HD, HD), F32)
+    before_state = before_state.astype(BF)
+    passed = after(first, before_state).astype(BF)
+    kept = jnp.where(odd, passed, before_state)
+    got = exchanged(jnp.where(odd, before_state, passed), axis, 1)
+    done.extend(work for work in covers if work is not None)
+    return kept, got, done
+
+
+def summed(*values):
+    total = values[0].astype(F32)
+    for value in values[1:]:
+        total = total + value.astype(F32)
+    return total.astype(BF)
+
+
+def line_sum(parts, axis):
     count = lax.axis_size(axis)
     index = lax.axis_index(axis)
-    parts = value.reshape(count, value.shape[0] // count, value.shape[1])
 
     def take(at):
         return lax.dynamic_index_in_dim(parts, jnp.clip(at, 0, count - 1), 0, keepdims=False)
@@ -288,14 +374,30 @@
         send_up = take(count - 1 - step + index)
         send_down = take(step - (count - 1 - index))
         if up is not None:
-            send_up = (send_up.astype(F32) + up.astype(F32)).astype(BF)
-            send_down = (send_down.astype(F32) + down.astype(F32)).astype(BF)
+            send_up = summed(send_up, up)
+            send_down = summed(send_down, down)
         up = lax.ppermute(send_up, axis, [(z, z + 1) for z in range(step + 1)])
         down = lax.ppermute(
             send_down, axis, [(count - 1 - z, count - 2 - z) for z in range(step + 1)]
         )
-    own = take(index).astype(F32)
-    return (own + up.astype(F32) + down.astype(F32)).astype(BF)
+    return summed(take(index), up, down)
+
+
+def swapped_sum(far, rest, axis):
+    pass_far, pass_near, own = rest
+    width = far.shape[-1] // 2
+    across = []
+    for piece in (slice(0, width), slice(width, 2 * width)):
+        paired = summed(pass_far[:, piece], exchanged(far[:, piece], axis, 1))
+        across.append(exchanged(paired, axis, 2))
+    near = exchanged(pass_near, axis, 1)
+    return jnp.concatenate(
+        [
+            summed(own[:, at * width : (at + 1) * width], near[:, at * width : (at + 1) * width], part)
+            for at, part in enumerate(across)
+        ],
+        axis=-1,
+    )
 
 
 def shards(
@@ -329,16 +431,10 @@
     count = lax.axis_size("ctx")
     rims = lax.ppermute(tails, "ctx", [(at, at + 1) for at in range(count - 1)])
     gate_in = project(w_gate_out)
-    rims_k = rims[:, :key_width]
-    rims_v = rims[:, key_width : key_width + heads * HD]
-    rims_q = rims[:, key_width + heads * HD :]
-    decay = decay_log.reshape(key_heads, ratio * chunks, CHUNK)
-    write = write_rate.reshape(key_heads, ratio * chunks, CHUNK)
-
-    def cols(length, width):
-        return pl.BlockSpec((length, width), lambda h: (0, h))
-
-    gate_spec = pl.BlockSpec((1, ratio * chunks, CHUNK), lambda h: (h, 0, 0))
+    def cols(length, width, start=0):
+        return pl.BlockSpec((length, width), lambda h: (0, h + start // width))
+
+    gate_spec = pl.BlockSpec((heads, rows), lambda h: (0, 0))
     wy_spec = pl.BlockSpec((ratio, rows, 2 * HD), lambda h: (h, 0, 0))
     starts_spec = pl.BlockSpec((ratio, chunks - 1, HD, 2 * HD), lambda h: (h, 0, 0, 0))
     taps_len = conv_key.shape[0]
@@ -349,7 +445,7 @@
             cols(rows, HD),
             cols(rows, ratio * HD),
             cols(RIM, HD),
-            cols(RIM, ratio * HD),
+            cols(RIM, ratio * HD, key_width),
             cols(taps_len, HD),
             cols(taps_len, ratio * HD),
             gate_spec,
@@ -371,14 +467,15 @@
             pltpu.VMEM((rows + 8, HD), F32),
             pltpu.VMEM((rows + 8, ratio * HD), F32),
         ],
+        compiler_params=pltpu.CompilerParams(vmem_limit_bytes=24 << 20),
         name="local",
-    )(proj_key, proj_value, rims_k, rims_v, conv_key, conv_value, decay, write)
+    )(proj_key, proj_value, rims, rims, conv_key, conv_value, decay_log, write_rate)
     parts = pl.pallas_call(
         functools.partial(output_kernel, ratio, chunks),
         grid=(key_heads,),
         in_specs=[
             cols(rows, HD),
-            cols(RIM, HD),
+            cols(RIM, HD, key_width + heads * HD),
             cols(taps_len, HD),
             cols(rows, HD),
             wy_spec,
@@ -388,25 +485,25 @@
         out_specs=wy_spec,
         out_shape=jax.ShapeDtypeStruct((heads, rows, 2 * HD), BF),
         scratch_shapes=[pltpu.VMEM((rows + 8, HD), F32)],
+        compiler_params=pltpu.CompilerParams(vmem_limit_bytes=20 << 20),
         name="outputs",
-    )(proj_query, rims_q, conv_query, keys, wy, starts, decay)
-    state = incoming_state(total, "ctx").astype(BF)
-    width_out = w_out.shape[1]
-    partial_out = pl.pallas_call(
-        functools.partial(final_kernel, heads),
-        grid=(chunks,),
-        in_specs=[
-            pl.BlockSpec((heads, CHUNK, 2 * HD), lambda c: (0, c, 0)),
-            pl.BlockSpec((heads, HD, HD), lambda c: (0, 0, 0)),
-            pl.BlockSpec((CHUNK, heads * HD), lambda c: (c, 0)),
-            pl.BlockSpec((heads * HD, width_out), lambda c: (0, 0)),
-        ],
-        out_specs=pl.BlockSpec((CHUNK, width_out), lambda c: (c, 0)),
-        out_shape=jax.ShapeDtypeStruct((rows, width_out), BF),
-        scratch_shapes=[pltpu.VMEM((CHUNK, heads * HD), BF)],
-        name="final",
-    )(parts, state, gate_in, w_out)
-    return scattered_sum(partial_out, "head")
+    )(proj_query, rims, conv_query, keys, wy, starts, decay_log)
+    kept, got, (parts, gate_in) = incoming_state(total, "ctx", (parts, gate_in))
+    spread = lax.axis_size("head")
+    place = lax.axis_index("head")
+    length = rows // spread
+    swap = lax.axis_index("ctx") & 1
+    if spread == 4:
+        order = [place ^ 3, place ^ 2, place ^ 1, place]
+    else:
+        order = list(range(spread))
+    plan = jnp.stack([jnp.int32(at) for at in [swap] + order])
+    shared = (plan, parts, kept, got, gate_in, w_out, length)
+    if spread == 4:
+        far = final_rows(0, 1, *shared)
+        rest = final_rows(1, 3, *shared)
+        return swapped_sum(far[0], rest, "head")
+    return line_sum(final_rows(0, spread, *shared), "head")
 
 
 def solution(mesh):

time: 150 us -> 106 us (0.71)
  waiting for transfers between devices: 61 us -> 32.1 us
  starting transfers between devices: 26.5 us -> 19 us
  other arithmetic: 9.84 us -> 3.2 us
  Pallas kernels: 30.9 us -> 25 us
  local copies, waits for them, and re-layouts: 7.07 us -> 12.9 us
    ppermute x6 -> x1, waiting for transfers between devices: 37.8 us -> 0.01 us  [incoming_state(): state = cover(lax.ppermute(total[..., HD:], axis, pairs))]
    ppermute x6 -> x1, starting transfers between devices: 16.4 us -> 4.09 us  [incoming_state(): state = cover(lax.ppermute(total[..., HD:], axis, pairs))]
    unnamed x18 -> x44, local copies, waits for them, and re-layouts: 2.41 us -> 12.7 us
    ppermute x3 -> x8, waiting for transfers between devices: 23.2 us -> 31.2 us  [exchanged(): lax.ppermute(value, axis, [(source, source ^ bit) for source in range(cou...]
    convert_element_type x8 -> x3, other arithmetic: 8.06 us -> 0.47 us  [the longest x2 0.46 us: summed(): return total.astype(BF)]
    ppermute x3 -> x8, starting transfers between devices: 7.57 us -> 12.5 us  [exchanged(): lax.ppermute(value, axis, [(source, source ^ bit) for source in range(cou...]
    dot_general x4, matrix products: 12.2 us -> 9.07 us  [project(): return jnp.dot(inputs, weights, preferred_element_type=F32).astype(BF)]
    dot_general x5 -> x4, matrix products: 1.46 us -> 4.05 us  [after(): jnp.einsum('hij,hjf->hif', later[..., :HD].astype(BF), earlier.astype(BF)...]
  transfers between devices with their start and end apart: 10 -> 10, of which waited for: 6 -> 8; matrix products, arithmetic and copies ran while one was open for 7% -> 3% of each run, Pallas kernels for 5% -> 9%
where the time goes in v2:
time: 106 us
  waiting for transfers between devices  32.1 us (30%)
  Pallas kernels  25 us (24%)
  starting transfers between devices  19 us (18%)
  matrix products  13.1 us (12%)
  local copies, waits for them, and re-layouts  12.9 us (12%)
  other arithmetic  3.2 us (3%)
    ppermute x8, waiting for transfers between devices, exchanged(): lax.ppermute(value, axis, [(source, source ^ bit) for source in range(cou...  31.2 us
    pallas_call x1, Pallas kernels, shards(): pl.pallas_call(functools.partial(local_kernel, ratio, chunks), grid=(key_...  14.2 us
    unnamed x44, local copies, waits for them, and re-layouts  12.7 us
    ppermute x8, starting transfers between devices, exchanged(): lax.ppermute(value, axis, [(source, source ^ bit) for source in range(cou...  12.5 us
    dot_general x4, matrix products, project(): return jnp.dot(inputs, weights, preferred_element_type=F32).astype(BF)  9.07 us
    pallas_call x2, Pallas kernels, final_rows(): pl.pallas_call(functools.partial(final_kernel, heads, first), grid_spec=p...  5.7 us
    pallas_call x1, Pallas kernels, shards(): pl.pallas_call(functools.partial(output_kernel, ratio, chunks), grid=(key...  5.01 us
    ppermute x1, starting transfers between devices, incoming_state(): state = cover(lax.ppermute(total[..., HD:], axis, pairs))  4.09 us
  transfers between devices with their start and end apart: 10, of which 8 were waited for; matrix products, arithmetic and copies ran while one was open for 3% of the time, Pallas kernels for 9%

profile of v2, /device:TPU:0, one launch (start us, length us, event | category | flops | bytes accessed | tf_op | source)
XLA Modules:
  0.0 105.6 jit_solution(7151891491321199075)
XLA Ops:
  0.0 1.6 %copy-done = bf16[512,2048]{1,0:T(8,128)(2,1)S(1)} copy-done((bf16[512,2048]{1,0:T(8,128)(2,1)S(1)}, bf16[512,2048]{1,0:T(8,128)(2,1)}, u32[]{:S(2)}) %copy-start) | copy-done | bytes 2097176
  1.6 3.1 %convolution_convert_fusion.3.keys_ref = bf16[512,512]{1,0:T(8,128)(2,1)S(1)} fusion(bf16[512,2048]{1,0:T(8,128)(2,1)S(1)} %copy-done, bf16[2048,512]{1,0:T(8,128)(2,1)} %param.13), kind=kOutput, calls=%fused_computation.3 | convolution fusion | flops 1074003968 | bytes 4718592 | tf_op jit(solution)/shard_map/dot_general | solution.py:417
  4.7 2.4 %convolution_convert_fusion.1.values_ref = bf16[512,1024]{1,0:T(8,128)(2,1)S(1)} fusion(bf16[512,2048]{1,0:T(8,128)(2,1)S(1)} %copy-done, bf16[2048,1024]{1,0:T(8,128)(2,1)S(1)} %copy-done.19), kind=kOutput, calls=%fused_computation.1 | convolution fusion | flops 2148007936 | bytes 7340032 | tf_op jit(solution)/shard_map/dot_general | solution.py:417
  7.2 1.2 %convolution_convert_fusion.2.query_ref = bf16[512,512]{1,0:T(8,128)(2,1)S(1)} fusion(bf16[512,2048]{1,0:T(8,128)(2,1)S(1)} %copy-done, bf16[2048,512]{1,0:T(8,128)(2,1)S(1)} %copy-done.21), kind=kOutput, calls=%fused_computation.2 | convolution fusion | flops 1074003968 | bytes 4718592 | tf_op jit(solution)/shard_map/dot_general | solution.py:417
  9.2 2.4 %collective-permute-start = (bf16[16,2048]{1,0:T(8,128)(2,1)S(1)}, bf16[16,2048]{1,0:T(8,128)(2,1)S(1)}, u32[]{:S(2)}, u32[]{:S(2)}) collective-permute-start(bf16[16,2048]{1,0:T(8,128)(2,1)S(1)} %pad_maximum_fusion.2), channel_id=1, source_target_pairs={{0,4},{4,8},{8,12},{12,16},{16,20},{20,24},{24,28},{1,5},{5,9},{9,... | collective-permute-start | bytes 196616 | tf_op jit(solution)/shard_map/ppermute | solution.py:432
  12.5 1.0 copy-done.9
  13.6 14.2 %local.1 = (bf16[512,512]{1,0:T(8,128)(2,1)S(1)}, bf16[8,512,256]{2,1,0:T(8,128)(2,1)S(1)}, bf16[8,3,128,256]{3,2,1,0:T(8,128)(2,1)S(1)}, bf16[8,128,256]{2,1,0:T(8,128)(2,1)S(1)}) custom-call(bf16[512,512]{1,0:T(8,128)(2,1)S(1)} %copy-done.9, bf16[512,1024]{1,0:T(8,128)(2,1)S(1)} %convolution_convert_fusion.1.values_ref, ...), custom_call_target="tpu_custom_call" | custom-call | tf_op jit(solution)/shard_map/local/pallas_call | solution.py:441
  27.9 3.1 %collective-permute-start.1 = (bf16[4,128,256]{2,1,0:T(8,128)(2,1)S(1)}, bf16[4,128,256]{2,1,0:T(8,128)(2,1)S(1)}, u32[]{:S(2)}, u32[]{:S(2)}) collective-permute-start(bf16[4,128,256]{2,1,0:T(8,128)(2,1)S(1)} %broadcast_select_fusion.3), channel_id=1, source_target_pairs={{0,4},{4,0},{8,12},{12,8},{16,20},{20,16},{24,28},{28,24},{1,5},{5... | collective-permute-start | bytes 786440 | tf_op jit(solution)/shard_map/ppermute | solution.py:289
  31.0 1.2 %collective-permute-done.1 = bf16[4,128,256]{2,1,0:T(8,128)(2,1)S(1)} collective-permute-done((bf16[4,128,256]{2,1,0:T(8,128)(2,1)S(1)}, bf16[4,128,256]{2,1,0:T(8,128)(2,1)S(1)}, u32[]{:S(2)}, u32[]{:S(2)}) %collective-permute-start.1) | collective-permute-done | bytes 262176 | tf_op jit(solution)/shard_map/ppermute | solution.py:289
  33.3 2.7 %collective-permute-start.2 = (bf16[4,128,256]{2,1,0:T(8,128)(2,1)}, bf16[4,128,256]{2,1,0:T(8,128)(2,1)}, u32[]{:S(2)}, u32[]{:S(2)}) collective-permute-start(bf16[4,128,256]{2,1,0:T(8,128)(2,1)} %pad_maximum_fusion.1), channel_id=1, source_target_pairs={{0,8},{4,12},{8,0},{12,4},{16,24},{20,28},{24,16},{28,20},{1,9},{5... | collective-permute-start | bytes 786440 | tf_op jit(solution)/shard_map/ppermute | solution.py:289
  35.9 1.6 %copy-done.5 = bf16[8,512,256]{2,1,0:T(8,128)(2,1)S(1)} copy-done((bf16[8,512,256]{2,1,0:T(8,128)(2,1)S(1)}, bf16[8,512,256]{2,1,0:T(8,128)(2,1)}, u32[]{:S(2)}) %copy-start.5) | copy-done | bytes 2097176
  37.5 1.4 %copy-done.7 = bf16[8,3,128,256]{3,2,1,0:T(8,128)(2,1)S(1)} copy-done((bf16[8,3,128,256]{3,2,1,0:T(8,128)(2,1)S(1)}, bf16[8,3,128,256]{3,2,1,0:T(8,128)(2,1)}, u32[]{:S(2)}) %copy-start.7) | copy-done | bytes 1572888
  38.9 1.0 copy-done.13
  40.0 5.0 %outputs.1.parts_ref = bf16[8,512,256]{2,1,0:T(8,128)(2,1)S(1)} custom-call(bf16[512,512]{1,0:T(8,128)(2,1)S(1)} %copy-done.11, bf16[16,2048]{1,0:T(8,128)(2,1)S(1)} %collective-permute-done.rims_k_ref.rims_v_ref.rims_ref, f32[4,512]{1,0:T(4,128)S(1)} %copy-done.18, bf16[512,512]{1,0:T(8,128)(2,1)S(1)} %copy-done.13, bf16[8,512,256]{2,1,0:T(8,128)(2,1)S(1)} %copy-done.5, ...), custom_call_target="tpu_custom_call" | custom-call | tf_op jit(solution)/shard_map/outputs/pallas_call | solution.py:473
  45.0 1.4 %copy-done.1 = bf16[8,512,256]{2,1,0:T(8,128)(2,1)} copy-done((bf16[8,512,256]{2,1,0:T(8,128)(2,1)}, bf16[8,512,256]{2,1,0:T(8,128)(2,1)S(1)}, u32[]{:S(2)}) %copy-start.1) | copy-done | bytes 2097176
  47.4 1.7 %fusion.3 = bf16[4,128,128]{2,1,0:T(8,128)(2,1)} fusion(bf16[4,128,128]{2,1,0:T(8,128)(2,1)S(1)} %slice.179, bf16[4,128,128]{2,1,0:T(8,128)(2,1)S(1)} %fusion.4, bf16[4,128,256]{2,1,0:T(8,128)(2,1)S(1)} %broadcast_select_fusion, pred[]{:T(512)S(6)} %ne.11, bf16[4,128,256]{2,1,0:T(8,128)(2,1)} %collective-permute-done.2), kind=kOutput, calls=%fused_computation.10 | convolution fusion | flops 17301504 | bytes 786433 | tf_op jit(solution)/shard_map/hij,hjf->hif/dot_general | solution.py:293
  49.2 4.1 %collective-permute-start.3 = (bf16[4,128,128]{2,1,0:T(8,128)(2,1)}, bf16[4,128,128]{2,1,0:T(8,128)(2,1)}, u32[]{:S(2)}, u32[]{:S(2)}) collective-permute-start(bf16[4,128,128]{2,1,0:T(8,128)(2,1)} %fusion.3), channel_id=1, source_target_pairs={{0,16},{4,20},{8,24},{12,28},{1,17},{5,21},{9,25},{13,29},{2,18},{... | collective-permute-start | bytes 393224 | tf_op jit(solution)/shard_map/ppermute | solution.py:330
  53.3 2.4 %convolution_convert_fusion.gate_ref = bf16[512,1024]{1,0:T(8,128)(2,1)S(1)} fusion(bf16[512,2048]{1,0:T(8,128)(2,1)S(1)} %copy-done, bf16[2048,1024]{1,0:T(8,128)(2,1)S(1)} %copy-done.20), kind=kOutput, calls=%fused_computation | convolution fusion | flops 2148007936 | bytes 7340032 | tf_op jit(solution)/shard_map/dot_general | solution.py:417
  55.7 1.2 %fusion.1 = bf16[4,128,128]{2,1,0:T(8,128)(2,1)S(1)} fusion(bf16[4,128,128]{2,1,0:T(8,128)(2,1)} %collective-permute-done.3, bf16[4,128,256]{2,1,0:T(8,128)(2,1)} %collective-permute-done.2, pred[]{:T(512)S(6)} %ne.11, pred[]{:T(512)S(6)} %ne.10, bf16[128,128]{1,0:T(8,128)(2,1)S(1)} %fusion.18), kind=kOutput, calls=%fused_computation.8 | convolution fusion | flops 17170432 | bytes 558592 | tf_op jit(solution)/shard_map/hij,hjf->hif/dot_general | solution.py:293
  57.9 1.5 %collective-permute-done.4.got_ref = bf16[4,128,128]{2,1,0:T(8,128)(2,1)S(1)} collective-permute-done((bf16[4,128,128]{2,1,0:T(8,128)(2,1)}, bf16[4,128,128]{2,1,0:T(8,128)(2,1)S(1)}, u32[]{:S(2)}, u32[]{:S(2)}) %collective-permute-start.4) | collective-permute-done | bytes 131104 | tf_op jit(solution)/shard_map/ppermute | solution.py:289
  59.3 1.6 %copy-done.2 = bf16[8,512,256]{2,1,0:T(8,128)(2,1)S(1)} copy-done((bf16[8,512,256]{2,1,0:T(8,128)(2,1)S(1)}, bf16[8,512,256]{2,1,0:T(8,128)(2,1)}, u32[]{:S(2)}) %copy-start.2) | copy-done | bytes 2097176
  60.9 2.2 %copy-done.3 = bf16[1024,2048]{1,0:T(8,128)(2,1)S(1)} copy-done((bf16[1024,2048]{1,0:T(8,128)(2,1)S(1)}, bf16[1024,2048]{1,0:T(8,128)(2,1)}, u32[]{:S(2)}) %copy-start.3) | copy-done | bytes 4194328
  63.1 1.7 %final.3 = bf16[1,128,2048]{2,1,0:T(8,128)(2,1)S(1)} custom-call(s32[5]{0:T(128)S(1)} %stack.23.plan_ref, bf16[8,512,256]{2,1,0:T(8,128)(2,1)S(1)} %copy-done.2, bf16[4,128,128]{2,1,0:T(8,128)(2,1)S(1)} %get-tuple-element.33.kept_ref, bf16[4,128,128]{2,1,0:T(8,128)(2,1)S(1)} %collective-permute-done.4.got_ref, ...), custom_call_target="tpu_custom_call" | custom-call | tf_op jit(solution)/shard_map/final/pallas_call | solution.py:266
  64.8 1.6 %collective-permute-start.6 = (bf16[128,1024]{1,0:T(8,128)(2,1)S(1)}, bf16[128,1024]{1,0:T(8,128)(2,1)S(1)}, u32[]{:S(2)}, u32[]{:S(2)}) collective-permute-start(bf16[128,1024]{1,0:T(8,128)(2,1)S(1)} %get-tuple-element.30), channel_id=1, source_target_pairs={{0,1},{1,0},{2,3},{3,2},{4,5},{5,4},{6,7},{7,6},{8,9},{9,8},{10,11... | collective-permute-start | bytes 786440 | tf_op jit(solution)/shard_map/ppermute | solution.py:289
  66.9 4.0 %final.2 = bf16[3,128,2048]{2,1,0:T(8,128)(2,1)S(1)} custom-call(s32[5]{0:T(128)S(1)} %stack.23.plan_ref, bf16[8,512,256]{2,1,0:T(8,128)(2,1)S(1)} %copy-done.2, bf16[4,128,128]{2,1,0:T(8,128)(2,1)S(1)} %get-tuple-element.33.kept_ref, bf16[4,128,128]{2,1,0:T(8,128)(2,1)S(1)} %collective-permute-done.4.got_ref, ...), custom_call_target="tpu_custom_call" | custom-call | tf_op jit(solution)/shard_map/final/pallas_call | solution.py:266
  71.1 1.6 %collective-permute-start.5 = (bf16[128,2048]{1,0:T(8,128)(2,1)S(1)}, bf16[128,2048]{1,0:T(8,128)(2,1)S(1)}, u32[]{:S(2)}, u32[]{:S(2)}) collective-permute-start(bf16[128,2048]{1,0:T(8,128)(2,1)S(1)} %get-tuple-element.23), channel_id=1, source_target_pairs={{0,1},{1,0},{2,3},{3,2},{4,5},{5,4},{6,7},{7,6},{8,9},{9,8},{10,11... | collective-permute-start | bytes 1572872 | tf_op jit(solution)/shard_map/ppermute | solution.py:289
  72.7 1.3 %collective-permute-done.6 = bf16[128,1024]{1,0:T(8,128)(2,1)S(1)} collective-permute-done((bf16[128,1024]{1,0:T(8,128)(2,1)S(1)}, bf16[128,1024]{1,0:T(8,128)(2,1)S(1)}, u32[]{:S(2)}, u32[]{:S(2)}) %collective-permute-start.6) | collective-permute-done | bytes 262176 | tf_op jit(solution)/shard_map/ppermute | solution.py:289
  74.0 5.6 %collective-permute-done.8 = bf16[128,1024]{1,0:T(8,128)(2,1)S(1)} collective-permute-done((bf16[128,1024]{1,0:T(8,128)(2,1)S(1)}, bf16[128,1024]{1,0:T(8,128)(2,1)S(1)}, u32[]{:S(2)}, u32[]{:S(2)}) %collective-permute-start.8) | collective-permute-done | bytes 262176 | tf_op jit(solution)/shard_map/ppermute | solution.py:289
  79.9 2.6 %collective-permute-start.7 = (bf16[128,1024]{1,0:T(8,128)(2,1)S(1)}, bf16[128,1024]{1,0:T(8,128)(2,1)S(1)}, u32[]{:S(2)}, u32[]{:S(2)}) collective-permute-start(bf16[128,1024]{1,0:T(8,128)(2,1)S(1)} %get-tuple-element.28), channel_id=1, source_target_pairs={{0,2},{1,3},{2,0},{3,1},{4,6},{5,7},{6,4},{7,5},{8,10},{9,11},{10,... | collective-permute-start | bytes 786440 | tf_op jit(solution)/shard_map/ppermute | solution.py:289
  82.8 12.8 %collective-permute-done.7 = bf16[128,1024]{1,0:T(8,128)(2,1)S(1)} collective-permute-done((bf16[128,1024]{1,0:T(8,128)(2,1)S(1)}, bf16[128,1024]{1,0:T(8,128)(2,1)S(1)}, u32[]{:S(2)}, u32[]{:S(2)}) %collective-permute-start.7) | collective-permute-done | bytes 262176 | tf_op jit(solution)/shard_map/ppermute | solution.py:289
  95.6 4.7 %collective-permute-done.5 = bf16[128,2048]{1,0:T(8,128)(2,1)S(1)} collective-permute-done((bf16[128,2048]{1,0:T(8,128)(2,1)S(1)}, bf16[128,2048]{1,0:T(8,128)(2,1)S(1)}, u32[]{:S(2)}, u32[]{:S(2)}) %collective-permute-start.5) | collective-permute-done | bytes 524320 | tf_op jit(solution)/shard_map/ppermute | solution.py:289
  100.3 4.1 %collective-permute-done.9 = bf16[128,1024]{1,0:T(8,128)(2,1)S(1)} collective-permute-done((bf16[128,1024]{1,0:T(8,128)(2,1)S(1)}, bf16[128,1024]{1,0:T(8,128)(2,1)S(1)}, u32[]{:S(2)}, u32[]{:S(2)}) %collective-permute-start.9) | collective-permute-done | bytes 262176 | tf_op jit(solution)/shard_map/ppermute | solution.py:289
  (61 shorter events, 7.1 us)
Async XLA Ops:
  0.0 1.6 %copy-start = (bf16[512,2048]{1,0:T(8,128)(2,1)S(1)}, bf16[512,2048]{1,0:T(8,128)(2,1)}, u32[]{:S(2)}) copy-start(bf16[512,2048]{1,0:T(8,128)(2,1)} %param.11) | copy-start | bytes 6291460
  0.0 4.7 %copy-start.19 = (bf16[2048,1024]{1,0:T(8,128)(2,1)S(1)}, bf16[2048,1024]{1,0:T(8,128)(2,1)}, u32[]{:S(2)}) copy-start(bf16[2048,1024]{1,0:T(8,128)(2,1)} %param.14) | copy-start | bytes 12582916
  4.7 4.5 %copy-start.8 = (bf16[512,512]{1,0:T(8,128)(2,1)}, bf16[512,512]{1,0:T(8,128)(2,1)S(1)}, u32[]{:S(2)}) copy-start(bf16[512,512]{1,0:T(8,128)(2,1)S(1)} %convolution_convert_fusion.3.keys_ref) | copy-start | bytes 1572868
  4.7 2.4 %copy-start.21 = (bf16[2048,512]{1,0:T(8,128)(2,1)S(1)}, bf16[2048,512]{1,0:T(8,128)(2,1)}, u32[]{:S(2)}) copy-start(bf16[2048,512]{1,0:T(8,128)(2,1)} %param.12) | copy-start | bytes 6291460
  7.1 5.4 %copy-start.14 = (f32[8,512]{1,0:T(8,128)S(1)}, f32[8,512]{1,0:T(8,128)}, u32[]{:S(2)}) copy-start(f32[8,512]{1,0:T(8,128)} %decay_ref.3) | copy-start | bytes 49156
  7.1 5.4 %copy-start.15 = (f32[4,1024]{1,0:T(4,128)S(1)}, f32[4,1024]{1,0:T(4,128)}, u32[]{:S(2)}) copy-start(f32[4,1024]{1,0:T(4,128)} %taps_v_ref.1) | copy-start | bytes 49156
  7.1 5.4 %copy-start.16 = (f32[8,512]{1,0:T(8,128)S(1)}, f32[8,512]{1,0:T(8,128)}, u32[]{:S(2)}) copy-start(f32[8,512]{1,0:T(8,128)} %write_ref.1) | copy-start | bytes 49156
  7.1 5.4 %copy-start.17 = (f32[4,512]{1,0:T(4,128)S(1)}, f32[4,512]{1,0:T(4,128)}, u32[]{:S(2)}) copy-start(f32[4,512]{1,0:T(4,128)} %taps_k_ref.1) | copy-start | bytes 24580
  8.4 0.8 copy-start.10
  9.2 3.3 %collective-permute-start = (bf16[16,2048]{1,0:T(8,128)(2,1)S(1)}, bf16[16,2048]{1,0:T(8,128)(2,1)S(1)}, u32[]{:S(2)}, u32[]{:S(2)}) collective-permute-start(bf16[16,2048]{1,0:T(8,128)(2,1)S(1)} %pad_maximum_fusion.2), channel_id=1, source_target_pairs={{0,4},{4,8},{8,12},{12,16},{16,20},{20,24},{24,28},{1,5},{5,9},{9,... | collective-permute-start | bytes 196616 | tf_op jit(solution)/shard_map/ppermute | solution.py:432
  12.5 1.0 copy-start.9
  27.8 5.4 %copy-start.4 = (bf16[8,512,256]{2,1,0:T(8,128)(2,1)}, bf16[8,512,256]{2,1,0:T(8,128)(2,1)S(1)}, u32[]{:S(2)}) copy-start(bf16[8,512,256]{2,1,0:T(8,128)(2,1)S(1)} %get-tuple-element.15.wy_ref) | copy-start | bytes 6291460
  27.8 5.4 %copy-start.6 = (bf16[8,3,128,256]{3,2,1,0:T(8,128)(2,1)}, bf16[8,3,128,256]{3,2,1,0:T(8,128)(2,1)S(1)}, u32[]{:S(2)}) copy-start(bf16[8,3,128,256]{3,2,1,0:T(8,128)(2,1)S(1)} %get-tuple-element.16.starts_ref) | copy-start | bytes 4718596
  27.8 5.4 %copy-start.12 = (bf16[512,512]{1,0:T(8,128)(2,1)}, bf16[512,512]{1,0:T(8,128)(2,1)S(1)}, u32[]{:S(2)}) copy-start(bf16[512,512]{1,0:T(8,128)(2,1)S(1)} %get-tuple-element.14.keys_ref) | copy-start | bytes 1572868
  27.8 8.1 %copy-start.11 = (bf16[512,512]{1,0:T(8,128)(2,1)S(1)}, bf16[512,512]{1,0:T(8,128)(2,1)}, u32[]{:S(2)}) copy-start(bf16[512,512]{1,0:T(8,128)(2,1)} %copy-done.10) | copy-start | bytes 1572868
  27.8 8.1 %copy-start.18 = (f32[4,512]{1,0:T(4,128)S(1)}, f32[4,512]{1,0:T(4,128)}, u32[]{:S(2)}) copy-start(f32[4,512]{1,0:T(4,128)} %taps_ref.1) | copy-start | bytes 24580
  27.9 4.3 %collective-permute-start.1 = (bf16[4,128,256]{2,1,0:T(8,128)(2,1)S(1)}, bf16[4,128,256]{2,1,0:T(8,128)(2,1)S(1)}, u32[]{:S(2)}, u32[]{:S(2)}) collective-permute-start(bf16[4,128,256]{2,1,0:T(8,128)(2,1)S(1)} %broadcast_select_fusion.3), channel_id=1, source_target_pairs={{0,4},{4,0},{8,12},{12,8},{16,20},{20,16},{24,28},{28,24},{1,5},{5... | collective-permute-start | bytes 786440 | tf_op jit(solution)/shard_map/ppermute | solution.py:289
  33.3 13.1 %collective-permute-start.2 = (bf16[4,128,256]{2,1,0:T(8,128)(2,1)}, bf16[4,128,256]{2,1,0:T(8,128)(2,1)}, u32[]{:S(2)}, u32[]{:S(2)}) collective-permute-start(bf16[4,128,256]{2,1,0:T(8,128)(2,1)} %pad_maximum_fusion.1), channel_id=1, source_target_pairs={{0,8},{4,12},{8,0},{12,4},{16,24},{20,28},{24,16},{28,20},{1,9},{5... | collective-permute-start | bytes 786440 | tf_op jit(solution)/shard_map/ppermute | solution.py:289
  35.9 1.6 %copy-start.5 = (bf16[8,512,256]{2,1,0:T(8,128)(2,1)S(1)}, bf16[8,512,256]{2,1,0:T(8,128)(2,1)}, u32[]{:S(2)}) copy-start(bf16[8,512,256]{2,1,0:T(8,128)(2,1)} %copy-done.4) | copy-start | bytes 6291460
  37.5 1.4 %copy-start.7 = (bf16[8,3,128,256]{3,2,1,0:T(8,128)(2,1)S(1)}, bf16[8,3,128,256]{3,2,1,0:T(8,128)(2,1)}, u32[]{:S(2)}) copy-start(bf16[8,3,128,256]{3,2,1,0:T(8,128)(2,1)} %copy-done.6) | copy-start | bytes 4718596
  38.9 1.0 copy-start.13
  40.0 13.3 %copy-start.20 = (bf16[2048,1024]{1,0:T(8,128)(2,1)S(1)}, bf16[2048,1024]{1,0:T(8,128)(2,1)}, u32[]{:S(2)}) copy-start(bf16[2048,1024]{1,0:T(8,128)(2,1)} %param.15) | copy-start | bytes 12582916
  45.0 1.4 %copy-start.1 = (bf16[8,512,256]{2,1,0:T(8,128)(2,1)}, bf16[8,512,256]{2,1,0:T(8,128)(2,1)S(1)}, u32[]{:S(2)}) copy-start(bf16[8,512,256]{2,1,0:T(8,128)(2,1)S(1)} %outputs.1.parts_ref) | copy-start | bytes 6291460
  49.2 6.5 %collective-permute-start.3 = (bf16[4,128,128]{2,1,0:T(8,128)(2,1)}, bf16[4,128,128]{2,1,0:T(8,128)(2,1)}, u32[]{:S(2)}, u32[]{:S(2)}) collective-permute-start(bf16[4,128,128]{2,1,0:T(8,128)(2,1)} %fusion.3), channel_id=1, source_target_pairs={{0,16},{4,20},{8,24},{12,28},{1,17},{5,21},{9,25},{13,29},{2,18},{... | collective-permute-start | bytes 393224 | tf_op jit(solution)/shard_map/ppermute | solution.py:330
  57.8 1.6 %collective-permute-start.4 = (bf16[4,128,128]{2,1,0:T(8,128)(2,1)}, bf16[4,128,128]{2,1,0:T(8,128)(2,1)S(1)}, u32[]{:S(2)}, u32[]{:S(2)}) collective-permute-start(bf16[4,128,128]{2,1,0:T(8,128)(2,1)} %get-tuple-element.32), channel_id=1, source_target_pairs={{0,4},{4,0},{8,12},{12,8},{16,20},{20,16},{24,28},{28,24},{1,5},{5... | collective-permute-start | bytes 393224 | tf_op jit(solution)/shard_map/ppermute | solution.py:289
  59.3 1.6 %copy-start.2 = (bf16[8,512,256]{2,1,0:T(8,128)(2,1)S(1)}, bf16[8,512,256]{2,1,0:T(8,128)(2,1)}, u32[]{:S(2)}) copy-start(bf16[8,512,256]{2,1,0:T(8,128)(2,1)} %copy-done.1) | copy-start | bytes 6291460
  60.9 2.2 %copy-start.3 = (bf16[1024,2048]{1,0:T(8,128)(2,1)S(1)}, bf16[1024,2048]{1,0:T(8,128)(2,1)}, u32[]{:S(2)}) copy-start(bf16[1024,2048]{1,0:T(8,128)(2,1)} %weight_ref.3) | copy-start | bytes 12582916
  64.8 9.2 %collective-permute-start.6 = (bf16[128,1024]{1,0:T(8,128)(2,1)S(1)}, bf16[128,1024]{1,0:T(8,128)(2,1)S(1)}, u32[]{:S(2)}, u32[]{:S(2)}) collective-permute-start(bf16[128,1024]{1,0:T(8,128)(2,1)S(1)} %get-tuple-element.30), channel_id=1, source_target_pairs={{0,1},{1,0},{2,3},{3,2},{4,5},{5,4},{6,7},{7,6},{8,9},{9,8},{10,11... | collective-permute-start | bytes 786440 | tf_op jit(solution)/shard_map/ppermute | solution.py:289
  66.5 13.2 %collective-permute-start.8 = (bf16[128,1024]{1,0:T(8,128)(2,1)S(1)}, bf16[128,1024]{1,0:T(8,128)(2,1)S(1)}, u32[]{:S(2)}, u32[]{:S(2)}) collective-permute-start(bf16[128,1024]{1,0:T(8,128)(2,1)S(1)} %get-tuple-element.31), channel_id=1, source_target_pairs={{0,1},{1,0},{2,3},{3,2},{4,5},{5,4},{6,7},{7,6},{8,9},{9,8},{10,11... | collective-permute-start | bytes 786440 | tf_op jit(solution)/shard_map/ppermute | solution.py:289
  71.1 29.3 %collective-permute-start.5 = (bf16[128,2048]{1,0:T(8,128)(2,1)S(1)}, bf16[128,2048]{1,0:T(8,128)(2,1)S(1)}, u32[]{:S(2)}, u32[]{:S(2)}) collective-permute-start(bf16[128,2048]{1,0:T(8,128)(2,1)S(1)} %get-tuple-element.23), channel_id=1, source_target_pairs={{0,1},{1,0},{2,3},{3,2},{4,5},{5,4},{6,7},{7,6},{8,9},{9,8},{10,11... | collective-permute-start | bytes 1572872 | tf_op jit(solution)/shard_map/ppermute | solution.py:289
  79.9 15.8 %collective-permute-start.7 = (bf16[128,1024]{1,0:T(8,128)(2,1)S(1)}, bf16[128,1024]{1,0:T(8,128)(2,1)S(1)}, u32[]{:S(2)}, u32[]{:S(2)}) collective-permute-start(bf16[128,1024]{1,0:T(8,128)(2,1)S(1)} %get-tuple-element.28), channel_id=1, source_target_pairs={{0,2},{1,3},{2,0},{3,1},{4,6},{5,7},{6,4},{7,5},{8,10},{9,11},{10,... | collective-permute-start | bytes 786440 | tf_op jit(solution)/shard_map/ppermute | solution.py:289
  82.5 22.0 %collective-permute-start.9 = (bf16[128,1024]{1,0:T(8,128)(2,1)S(1)}, bf16[128,1024]{1,0:T(8,128)(2,1)S(1)}, u32[]{:S(2)}, u32[]{:S(2)}) collective-permute-start(bf16[128,1024]{1,0:T(8,128)(2,1)S(1)} %get-tuple-element.29), channel_id=1, source_target_pairs={{0,2},{1,3},{2,0},{3,1},{4,6},{5,7},{6,4},{7,5},{8,10},{9,11},{10,... | collective-permute-start | bytes 786440 | tf_op jit(solution)/shard_map/ppermute | solution.py:289

commit v3 on v2

--- a/solution.py
+++ b/solution.py
@@ -13,6 +13,17 @@
 BF = jnp.bfloat16
 F32 = jnp.float32
 EXACT = lax.Precision.HIGHEST
+WHOLE = pl.BlockSpec(memory_space=pltpu.VMEM)
+
+
+def cost(matmul_rows, exps, size):
+    return pl.CostEstimate(
+        flops=2 * HD * HD * matmul_rows, transcendentals=exps, bytes_accessed=size
+    )
+
+
+def in_hbm(array):
+    return pltpu.with_memory_space_constraint(array, pltpu.HBM)
 
 
 def mm(left, right):
@@ -62,8 +73,8 @@
     return as_rows, as_cols
 
 
-def head_rows(ref, ratio, chunks):
-    start = pl.program_id(0) * ratio
+def head_rows(ref, ratio, chunks, group=1, member=0):
+    start = (pl.program_id(0) * group + member) * ratio
     rows = [ref[pl.ds(start + head, 1), :] for head in range(ratio)]
     return jnp.concatenate(
         [
@@ -119,6 +130,7 @@
 
 
 def local_kernel(
+    group,
     ratio,
     chunks,
     keys_ref,
@@ -137,71 +149,97 @@
     stage_v,
 ):
     row_ids, col_ids = grid_ids()
+    eye = jnp.where(row_ids == col_ids, 1.0, 0.0)
     stage_rows(stage_k, rims_k_ref, keys_ref)
     stage_rows(stage_v, rims_v_ref, values_ref)
-    decay_rows, decay_cols = cumulated(head_rows(decay_ref, ratio, chunks))
-    write_cols = lax.dot_general(
-        jnp.where(row_ids == col_ids, 1.0, 0.0),
-        head_rows(write_ref, ratio, chunks),
-        (((1,), (1,)), ((), ())),
-        precision=EXACT,
-        preferred_element_type=F32,
-    )
     taps_k = taps_k_ref[...]
     taps_v = taps_v_ref[...]
-    keys = []
-    flipped = []
+    decays = []
+    writes = []
+    for member in range(group):
+        decays.append(cumulated(head_rows(decay_ref, ratio, chunks, group, member)))
+        writes.append(
+            lax.dot_general(
+                eye,
+                head_rows(write_ref, ratio, chunks, group, member),
+                (((1,), (1,)), ((), ())),
+                precision=EXACT,
+                preferred_element_type=F32,
+            )
+        )
+    keys = {}
+    flipped = {}
     values = []
-    inner = []
+    inner = {}
     for chunk in range(chunks):
-        key = unit_rows(conv_chunk(stage_k, taps_k, chunk), 1.0)
-        keys_out[chunk * CHUNK : (chunk + 1) * CHUNK] = key.astype(BF)
-        keys.append(key)
-        flipped.append(key.T)
-        inner.append(mm(key, flipped[-1]))
+        rows = slice(chunk * CHUNK, (chunk + 1) * CHUNK)
+        smoothed = conv_chunk(stage_k, taps_k, chunk)
         values.append(conv_chunk(stage_v, taps_v, chunk))
-    units = [(head, chunk) for head in range(ratio) for chunk in range(chunks)]
+        for member in range(group):
+            lanes = slice(member * HD, (member + 1) * HD)
+            key = unit_rows(smoothed[:, lanes], 1.0)
+            keys_out[rows, lanes] = key.astype(BF)
+            keys[member, chunk] = key
+            flipped[member, chunk] = key.T
+            inner[member, chunk] = mm(key, flipped[member, chunk])
+    units = [
+        (member, head, chunk)
+        for member in range(group)
+        for head in range(ratio)
+        for chunk in range(chunks)
+    ]
     systems = []
-    for head, chunk in units:
+    for member, head, chunk in units:
         at = chunk * ratio + head
+        decay_rows, decay_cols = decays[member]
         fading = jnp.exp(
             jnp.minimum(decay_cols[:, at : at + 1] - decay_rows[at : at + 1], 0.0)
         )
         systems.append(
             jnp.where(
-                row_ids > col_ids, write_cols[:, at : at + 1] * inner[chunk] * fading, 0.0
+                row_ids > col_ids,
+                writes[member][:, at : at + 1] * inner[member, chunk] * fading,
+                0.0,
             )
         )
     inverses = inverted(systems)
-    maps = []
-    for (head, chunk), inverse in zip(units, inverses):
+    maps = {}
+    for (member, head, chunk), inverse in zip(units, inverses):
         at = chunk * ratio + head
+        place = member * ratio + head
+        decay_rows, decay_cols = decays[member]
         col = decay_cols[:, at : at + 1]
-        write = write_cols[:, at : at + 1]
-        value = values[chunk][:, head * HD : (head + 1) * HD]
-        right = jnp.concatenate([keys[chunk] * (write * jnp.exp(col)), value * write], axis=1)
+        write = writes[member][:, at : at + 1]
+        value = values[chunk][:, place * HD : (place + 1) * HD]
+        right = jnp.concatenate(
+            [keys[member, chunk] * (write * jnp.exp(col)), value * write], axis=1
+        )
         solved = mm(inverse, right).astype(BF)
-        wy_out[head, chunk * CHUNK : (chunk + 1) * CHUNK] = solved
+        wy_out[place, chunk * CHUNK : (chunk + 1) * CHUNK] = solved
         row = decay_rows[at : at + 1]
         end = row[:, CHUNK - 1 : CHUNK]
-        maps.append((mm(flipped[chunk] * jnp.exp(end - row), solved), jnp.exp(end)))
-    eye = jnp.where(row_ids == col_ids, 1.0, 0.0)
-    for head in range(ratio):
-        state = None
-        for chunk in range(chunks):
-            product, end = maps[head * chunks + chunk]
+        maps[place, chunk] = (
+            mm(flipped[member, chunk] * jnp.exp(end - row), solved),
+            jnp.exp(end),
+        )
+    states = [None] * (group * ratio)
+    for chunk in range(chunks):
+        for place, state in enumerate(states):
+            product, end = maps[place, chunk]
             linear = eye * end - product[:, :HD]
             added = product[:, HD:]
             if state is None:
-                state = jnp.concatenate([linear, added], axis=1)
+                states[place] = jnp.concatenate([linear, added], axis=1)
             else:
-                starts_out[head, chunk - 1] = state.astype(BF)
+                starts_out[place, chunk - 1] = state.astype(BF)
                 moved = mm(linear, state)
-                state = jnp.concatenate([moved[:, :HD], moved[:, HD:] + added], axis=1)
-        map_out[head] = state.astype(BF)
+                states[place] = jnp.concatenate([moved[:, :HD], moved[:, HD:] + added], axis=1)
+    for place, state in enumerate(states):
+        map_out[place] = state.astype(BF)
 
 
 def output_kernel(
+    group,
     ratio,
     chunks,
     query_ref,
@@ -216,39 +254,53 @@
 ):
     row_ids, col_ids = grid_ids()
     stage_rows(stage, rims_ref, query_ref)
-    decay_rows, decay_cols = cumulated(head_rows(decay_ref, ratio, chunks))
+    decays = [
+        cumulated(head_rows(decay_ref, ratio, chunks, group, member)) for member in range(group)
+    ]
     taps = taps_ref[...]
     for chunk in range(chunks):
         rows = slice(chunk * CHUNK, (chunk + 1) * CHUNK)
-        query = unit_rows(conv_chunk(stage, taps, chunk), HD ** (-0.5))
-        scores = mm_nt(query, keys_ref[rows])
-        for head in range(ratio):
+        smoothed = conv_chunk(stage, taps, chunk)
+        places = range(group * ratio)
+        queries, scores = [], []
+        for member in range(group):
+            lanes = slice(member * HD, (member + 1) * HD)
+            queries.append(unit_rows(smoothed[:, lanes], HD ** (-0.5)))
+            scores.append(mm_nt(queries[-1], keys_ref[rows, lanes]))
+        if chunk > 0:
+            removed = [
+                mm(wy_ref[place, rows, :HD], starts_ref[place, chunk - 1]) for place in places
+            ]
+        for place in places:
+            member, head = divmod(place, ratio)
             at = chunk * ratio + head
+            decay_rows, decay_cols = decays[member]
             col = decay_cols[:, at : at + 1]
             fading = jnp.exp(jnp.minimum(col - decay_rows[at : at + 1], 0.0))
-            weights = jnp.where(row_ids >= col_ids, scores * fading, 0.0)
-            scaled = query * jnp.exp(col)
-            wy = wy_ref[head, rows]
+            weights = jnp.where(row_ids >= col_ids, scores[member] * fading, 0.0)
+            scaled = queries[member] * jnp.exp(col)
+            wy = wy_ref[place, rows]
             if chunk == 0:
                 whole = mm(weights, wy)
                 linear = scaled - whole[:, :HD]
                 local = whole[:, HD:]
             else:
-                state = starts_ref[head, chunk - 1]
-                removed = mm(wy[:, :HD], state)
+                gone = removed[place]
                 left = jnp.concatenate([scaled, weights], axis=1)
                 rest = jnp.concatenate(
-                    [-removed[:, :HD], wy[:, HD:].astype(F32) - removed[:, HD:]], axis=1
+                    [-gone[:, :HD], wy[:, HD:].astype(F32) - gone[:, HD:]], axis=1
                 ).astype(BF)
-                whole = mm(left, jnp.concatenate([state, rest], axis=0))
+                whole = mm(
+                    left, jnp.concatenate([starts_ref[place, chunk - 1], rest], axis=0)
+                )
                 linear = whole[:, :HD]
                 local = whole[:, HD:]
-            parts_out[head, rows, :HD] = linear.astype(BF)
-            parts_out[head, rows, HD:] = local.astype(BF)
-
-
-def final_kernel(heads, first, plan_ref, parts_ref, kept_ref, got_ref, gate_ref, weight_ref, out_ref, normed):
-    swap = plan_ref[0] != 0
+            parts_out[place, rows, :HD] = linear.astype(BF)
+            parts_out[place, rows, HD:] = local.astype(BF)
+
+
+def norm_kernel(heads, swap_ref, parts_ref, kept_ref, got_ref, gate_ref, normed_ref):
+    swap = swap_ref[0] != 0
     half = heads // 2
     for head in range(heads):
         lanes = slice(head * HD, (head + 1) * HD)
@@ -256,32 +308,35 @@
         state = jnp.where(swap, got, kept) if head < half else jnp.where(swap, kept, got)
         attended = parts_ref[head, :, HD:].astype(F32) + mm(parts_ref[head, :, :HD], state)
         spread = lax.rsqrt(jnp.mean(attended * attended, axis=-1, keepdims=True) + 1e-06)
-        normed[:, lanes] = (attended * spread * silu(gate_ref[:, lanes].astype(F32))).astype(BF)
-    out_ref[0] = jnp.dot(normed[...], weight_ref[...], preferred_element_type=F32).astype(BF)
+        normed_ref[:, lanes] = (
+            attended * spread * silu(gate_ref[:, lanes].astype(F32))
+        ).astype(BF)
 
 
 def final_rows(first, count, plan, parts, kept, got, gate_in, w_out, length):
     heads = parts.shape[0]
-    width = w_out.shape[1]
-    return pl.pallas_call(
-        functools.partial(final_kernel, heads, first),
+    normed = pl.pallas_call(
+        functools.partial(norm_kernel, heads),
         grid_spec=pltpu.PrefetchScalarGridSpec(
             num_scalar_prefetch=1,
             grid=(count,),
             in_specs=[
                 pl.BlockSpec((heads, length, 2 * HD), lambda c, plan: (0, plan[1 + first + c], 0)),
-                pl.BlockSpec(memory_space=pltpu.VMEM),
-                pl.BlockSpec(memory_space=pltpu.VMEM),
+                WHOLE,
+                WHOLE,
                 pl.BlockSpec((length, heads * HD), lambda c, plan: (plan[1 + first + c], 0)),
-                pl.BlockSpec(memory_space=pltpu.VMEM),
             ],
-            out_specs=pl.BlockSpec((1, length, width), lambda c, plan: (c, 0, 0)),
-            scratch_shapes=[pltpu.VMEM((length, heads * HD), BF)],
+            out_specs=pl.BlockSpec((length, heads * HD), lambda c, plan: (c, 0)),
         ),
-        out_shape=jax.ShapeDtypeStruct((count, length, width), BF),
+        out_shape=jax.ShapeDtypeStruct((count * length, heads * HD), BF),
         compiler_params=pltpu.CompilerParams(vmem_limit_bytes=16 << 20),
-        name="final",
-    )(plan, parts, kept, got, gate_in, w_out)
+        cost_estimate=cost(
+            heads * count * length, heads * count * length * HD, 8 * heads * count * length * HD
+        ),
+        name="normed",
+    )(plan, in_hbm(parts), kept, got, gate_in)
+    mixed = jnp.dot(normed, w_out, preferred_element_type=F32).astype(BF)
+    return mixed.reshape(count, length, w_out.shape[1])
 
 
 def exchanged(value, axis, bit):
@@ -383,18 +438,25 @@
     return summed(take(index), up, down)
 
 
-def swapped_sum(far, rest, axis):
-    pass_far, pass_near, own = rest
-    width = far.shape[-1] // 2
-    across = []
-    for piece in (slice(0, width), slice(width, 2 * width)):
-        paired = summed(pass_far[:, piece], exchanged(far[:, piece], axis, 1))
-        across.append(exchanged(paired, axis, 2))
-    near = exchanged(pass_near, axis, 1)
+def swapped_sum(rows_of, axis):
+    far = rows_of(0, 1, None)[0]
+    width = far.shape[-1] // 4
+    early, late = slice(0, width), slice(width, 4 * width)
+    first_in = exchanged(far[:, early], axis, 1)
+    passed = rows_of(1, 1, None)[0]
+    far_late, passed = lax.optimization_barrier((far[:, late], passed))
+    later_in = exchanged(far_late, axis, 1)
+    paired = summed(passed[:, early], first_in)
+    first = exchanged(paired, axis, 2)
+    rest = rows_of(2, 2, paired)
+    later_in, first = lax.optimization_barrier((later_in, first))
+    later = exchanged(summed(passed[:, late], later_in), axis, 2)
+    near = exchanged(rest[0], axis, 1)
+    own = rest[1]
     return jnp.concatenate(
         [
-            summed(own[:, at * width : (at + 1) * width], near[:, at * width : (at + 1) * width], part)
-            for at, part in enumerate(across)
+            summed(own[:, early], near[:, early], first),
+            summed(own[:, late], near[:, late], later),
         ],
         axis=-1,
     )
@@ -431,16 +493,18 @@
     count = lax.axis_size("ctx")
     rims = lax.ppermute(tails, "ctx", [(at, at + 1) for at in range(count - 1)])
     gate_in = project(w_gate_out)
+    group = 2 if key_heads % 2 == 0 else 1
+
     def cols(length, width, start=0):
-        return pl.BlockSpec((length, width), lambda h: (0, h + start // width))
+        return pl.BlockSpec((length, group * width), lambda h: (0, h + start // (group * width)))
 
     gate_spec = pl.BlockSpec((heads, rows), lambda h: (0, 0))
-    wy_spec = pl.BlockSpec((ratio, rows, 2 * HD), lambda h: (h, 0, 0))
-    starts_spec = pl.BlockSpec((ratio, chunks - 1, HD, 2 * HD), lambda h: (h, 0, 0, 0))
+    wy_spec = pl.BlockSpec((group * ratio, rows, 2 * HD), lambda h: (h, 0, 0))
+    starts_spec = pl.BlockSpec((group * ratio, chunks - 1, HD, 2 * HD), lambda h: (h, 0, 0, 0))
     taps_len = conv_key.shape[0]
     keys, wy, starts, total = pl.pallas_call(
-        functools.partial(local_kernel, ratio, chunks),
-        grid=(key_heads,),
+        functools.partial(local_kernel, group, ratio, chunks),
+        grid=(key_heads // group,),
         in_specs=[
             cols(rows, HD),
             cols(rows, ratio * HD),
@@ -455,24 +519,25 @@
             cols(rows, HD),
             wy_spec,
             starts_spec,
-            pl.BlockSpec((ratio, HD, 2 * HD), lambda h: (h, 0, 0)),
+            pl.BlockSpec((group * ratio, HD, 2 * HD), lambda h: (h, 0, 0)),
         ],
         out_shape=[
-            jax.ShapeDtypeStruct((rows, key_width), BF),
-            jax.ShapeDtypeStruct((heads, rows, 2 * HD), BF),
-            jax.ShapeDtypeStruct((heads, chunks - 1, HD, 2 * HD), BF),
+            pltpu.HBM((rows, key_width), BF),
+            pltpu.HBM((heads, rows, 2 * HD), BF),
+            pltpu.HBM((heads, chunks - 1, HD, 2 * HD), BF),
             jax.ShapeDtypeStruct((heads, HD, 2 * HD), BF),
         ],
         scratch_shapes=[
-            pltpu.VMEM((rows + 8, HD), F32),
-            pltpu.VMEM((rows + 8, ratio * HD), F32),
-        ],
-        compiler_params=pltpu.CompilerParams(vmem_limit_bytes=24 << 20),
+            pltpu.VMEM((rows + 8, group * HD), F32),
+            pltpu.VMEM((rows + 8, group * ratio * HD), F32),
+        ],
+        compiler_params=pltpu.CompilerParams(vmem_limit_bytes=32 << 20),
+        cost_estimate=cost(16 * heads * rows, 4 * heads * rows * HD, 12 * heads * rows * HD),
         name="local",
-    )(proj_key, proj_value, rims, rims, conv_key, conv_value, decay_log, write_rate)
+    )(in_hbm(proj_key), in_hbm(proj_value), rims, rims, conv_key, conv_value, decay_log, write_rate)
     parts = pl.pallas_call(
-        functools.partial(output_kernel, ratio, chunks),
-        grid=(key_heads,),
+        functools.partial(output_kernel, group, ratio, chunks),
+        grid=(key_heads // group,),
         in_specs=[
             cols(rows, HD),
             cols(RIM, HD, key_width + heads * HD),
@@ -483,11 +548,12 @@
             gate_spec,
         ],
         out_specs=wy_spec,
-        out_shape=jax.ShapeDtypeStruct((heads, rows, 2 * HD), BF),
-        scratch_shapes=[pltpu.VMEM((rows + 8, HD), F32)],
-        compiler_params=pltpu.CompilerParams(vmem_limit_bytes=20 << 20),
+        out_shape=pltpu.HBM((heads, rows, 2 * HD), BF),
+        scratch_shapes=[pltpu.VMEM((rows + 8, group * HD), F32)],
+        compiler_params=pltpu.CompilerParams(vmem_limit_bytes=24 << 20),
+        cost_estimate=cost(8 * heads * rows, 2 * heads * rows * HD, 12 * heads * rows * HD),
         name="outputs",
-    )(proj_query, rims, conv_query, keys, wy, starts, decay_log)
+    )(in_hbm(proj_query), rims, conv_query, in_hbm(keys), in_hbm(wy), in_hbm(starts), decay_log)
     kept, got, (parts, gate_in) = incoming_state(total, "ctx", (parts, gate_in))
     spread = lax.axis_size("head")
     place = lax.axis_index("head")
@@ -498,12 +564,16 @@
     else:
         order = list(range(spread))
     plan = jnp.stack([jnp.int32(at) for at in [swap] + order])
-    shared = (plan, parts, kept, got, gate_in, w_out, length)
+
+    def rows_of(first, amount, earlier):
+        steps = plan
+        if earlier is not None:
+            steps, _ = lax.optimization_barrier((plan, earlier))
+        return final_rows(first, amount, steps, parts, kept, got, gate_in, w_out, length)
+
     if spread == 4:
-        far = final_rows(0, 1, *shared)
-        rest = final_rows(1, 3, *shared)
-        return swapped_sum(far[0], rest, "head")
-    return line_sum(final_rows(0, spread, *shared), "head")
+        return swapped_sum(rows_of, "head")
+    return line_sum(rows_of(0, spread, None), "head")
 
 
 def solution(mesh):

time: 106 us -> 94.5 us (0.89)
  local copies, waits for them, and re-layouts: 12.9 us -> 1.85 us
  waiting for transfers between devices: 32.1 us -> 26.7 us
  matrix products: 13.1 us -> 17.2 us
  starting transfers between devices: 19 us -> 21 us
  other arithmetic: 3.2 us -> 1.43 us
    unnamed x44 -> x28, local copies, waits for them, and re-layouts: 12.7 us -> 1.66 us
    ppermute x8, waiting for transfers between devices: 31.2 us -> 25.8 us  [exchanged(): lax.ppermute(value, axis, [(source, source ^ bit) for source in range(cou...]
    dot_general x0 -> x3, matrix products: none -> 5.08 us  [final_rows(): mixed = jnp.dot(normed, w_out, preferred_element_type=F32).astype(BF)]
    ppermute x8, starting transfers between devices: 12.5 us -> 13.7 us  [exchanged(): lax.ppermute(value, axis, [(source, source ^ bit) for source in range(cou...]
    pallas_call x4 -> x5, Pallas kernels: 25 us -> 25.4 us  [the longest x1 12 us: shards(): pl.pallas_call(functools.partial(local_kernel, group, ratio, chunks), gri...]
  transfers between devices with their start and end apart: 10 -> 10, of which waited for: 8 -> 7; matrix products, arithmetic and copies ran while one was open for 3% -> 5% of each run, Pallas kernels for 9% -> 12%
where the time goes in v3:
time: 94.5 us; the launch traced here: 94 us
  waiting for transfers between devices  26.7 us (28%)
  Pallas kernels  25.4 us (27%)
  starting transfers between devices  21 us (22%)
  matrix products  17.2 us (18%)
  local copies, waits for them, and re-layouts  1.85 us (2%)
  other arithmetic  1.43 us (2%)
    ppermute x8, waiting for transfers between devices, exchanged(): lax.ppermute(value, axis, [(source, source ^ bit) for source in range(cou...  25.8 us
    ppermute x8, starting transfers between devices, exchanged(): lax.ppermute(value, axis, [(source, source ^ bit) for source in range(cou...  13.7 us
    pallas_call x1, Pallas kernels, shards(): pl.pallas_call(functools.partial(local_kernel, group, ratio, chunks), gri...  12 us
    dot_general x4, matrix products, project(): return jnp.dot(inputs, weights, preferred_element_type=F32).astype(BF)  9.03 us
    pallas_call x1, Pallas kernels, shards(): pl.pallas_call(functools.partial(output_kernel, group, ratio, chunks), gr...  6.84 us
    pallas_call x3, Pallas kernels, final_rows(): pl.pallas_call(functools.partial(norm_kernel, heads), grid_spec=pltpu.Pre...  6.56 us
    dot_general x3, matrix products, final_rows(): mixed = jnp.dot(normed, w_out, preferred_element_type=F32).astype(BF)  5.08 us
    ppermute x1, starting transfers between devices, incoming_state(): state = cover(lax.ppermute(total[..., HD:], axis, pairs))  4.98 us
  transfers between devices with their start and end apart: 10, of which 7 were waited for; matrix products, arithmetic and copies ran while one was open for 5% of the time, Pallas kernels for 12%

profile of v3, /device:TPU:0, one launch (start us, length us, event | category | flops | bytes accessed | tf_op | source)
XLA Modules:
  0.0 94.0 jit_solution(5684855727678601694)
XLA Ops:
  0.0 1.6 %copy-done = bf16[512,2048]{1,0:T(8,128)(2,1)S(1)} copy-done((bf16[512,2048]{1,0:T(8,128)(2,1)S(1)}, bf16[512,2048]{1,0:T(8,128)(2,1)}, u32[]{:S(2)}) %copy-start) | copy-done | bytes 2097176
  1.6 3.1 %convolution_convert_fusion.6.keys_ref = bf16[512,512]{1,0:T(8,128)(2,1)S(1)} fusion(bf16[512,2048]{1,0:T(8,128)(2,1)S(1)} %copy-done, bf16[2048,512]{1,0:T(8,128)(2,1)} %param.13), kind=kOutput, calls=%fused_computation.6 | convolution fusion | flops 1074003968 | bytes 4718592 | tf_op jit(solution)/shard_map/dot_general | solution.py:479
  4.7 2.4 %convolution_convert_fusion.4.values_ref = bf16[512,1024]{1,0:T(8,128)(2,1)S(1)} fusion(bf16[512,2048]{1,0:T(8,128)(2,1)S(1)} %copy-done, bf16[2048,1024]{1,0:T(8,128)(2,1)S(1)} %copy-done.11), kind=kOutput, calls=%fused_computation.4 | convolution fusion | flops 2148007936 | bytes 7340032 | tf_op jit(solution)/shard_map/dot_general | solution.py:479
  7.2 1.2 %convolution_convert_fusion.5.query_ref = bf16[512,512]{1,0:T(8,128)(2,1)S(1)} fusion(bf16[512,2048]{1,0:T(8,128)(2,1)S(1)} %copy-done, bf16[2048,512]{1,0:T(8,128)(2,1)S(1)} %copy-done.13), kind=kOutput, calls=%fused_computation.5 | convolution fusion | flops 1074003968 | bytes 4718592 | tf_op jit(solution)/shard_map/dot_general | solution.py:479
  8.5 2.4 %collective-permute-start = (bf16[16,2048]{1,0:T(8,128)(2,1)S(1)}, bf16[16,2048]{1,0:T(8,128)(2,1)S(1)}, u32[]{:S(2)}, u32[]{:S(2)}) collective-permute-start(bf16[16,2048]{1,0:T(8,128)(2,1)S(1)} %pad_maximum_fusion.2), channel_id=1, source_target_pairs={{0,4},{4,8},{8,12},{12,16},{16,20},{20,24},{24,28},{1,5},{5,9},{9,... | collective-permute-start | bytes 196616 | tf_op jit(solution)/shard_map/ppermute | solution.py:494
  10.9 0.9 collective-permute-done.rims_k_ref.rims_v_ref.rims_ref
  11.8 12.0 %local.1 = (bf16[512,512]{1,0:T(8,128)(2,1)}, bf16[8,512,256]{2,1,0:T(8,128)(2,1)}, bf16[8,3,128,256]{3,2,1,0:T(8,128)(2,1)}, bf16[8,128,256]{2,1,0:T(8,128)(2,1)S(1)}) custom-call(bf16[512,512]{1,0:T(8,128)(2,1)} %copy-done.10, bf16[512,1024]{1,0:T(8,128)(2,1)} %copy-done.9, bf16[16,2048]{1,0:T(8,128)(2,1)S(1)} %collective-permute-done.rims_k_ref.rims_v_ref.rims_ref, ...), custom_call_target="tpu_custom_call" | custom-call | flops 2147483648 | bytes 6291456 | tf_op jit(solution)/shard_map/local/pallas_call | solution.py:505
  23.8 3.1 %collective-permute-start.1 = (bf16[4,128,256]{2,1,0:T(8,128)(2,1)S(1)}, bf16[4,128,256]{2,1,0:T(8,128)(2,1)S(1)}, u32[]{:S(2)}, u32[]{:S(2)}) collective-permute-start(bf16[4,128,256]{2,1,0:T(8,128)(2,1)S(1)} %broadcast_select_fusion.3), channel_id=1, source_target_pairs={{0,4},{4,0},{8,12},{12,8},{16,20},{20,16},{24,28},{28,24},{1,5},{5... | collective-permute-start | bytes 786440 | tf_op jit(solution)/shard_map/ppermute | solution.py:344
  26.9 1.2 %collective-permute-done.1 = bf16[4,128,256]{2,1,0:T(8,128)(2,1)S(1)} collective-permute-done((bf16[4,128,256]{2,1,0:T(8,128)(2,1)S(1)}, bf16[4,128,256]{2,1,0:T(8,128)(2,1)S(1)}, u32[]{:S(2)}, u32[]{:S(2)}) %collective-permute-start.1) | collective-permute-done | bytes 262176 | tf_op jit(solution)/shard_map/ppermute | solution.py:344
  28.5 2.7 %collective-permute-start.2 = (bf16[4,128,256]{2,1,0:T(8,128)(2,1)S(1)}, bf16[4,128,256]{2,1,0:T(8,128)(2,1)S(1)}, u32[]{:S(2)}, u32[]{:S(2)}) collective-permute-start(bf16[4,128,256]{2,1,0:T(8,128)(2,1)S(1)} %pad_maximum_fusion.1), channel_id=1, source_target_pairs={{0,8},{4,12},{8,0},{12,4},{16,24},{20,28},{24,16},{28,20},{1,9},{5... | collective-permute-start | bytes 786440 | tf_op jit(solution)/shard_map/ppermute | solution.py:344
  31.1 6.8 %outputs.1.parts_ref = bf16[8,512,256]{2,1,0:T(8,128)(2,1)} custom-call(bf16[512,512]{1,0:T(8,128)(2,1)} %copy-done.7, bf16[16,2048]{1,0:T(8,128)(2,1)S(1)} %collective-permute-done.rims_k_ref.rims_v_ref.rims_ref, f32[4,512]{1,0:T(4,128)S(1)} %copy-done.2, bf16[512,512]{1,0:T(8,128)(2,1)} %get-tuple-element.19.keys_ref, ...), custom_call_target="tpu_custom_call" | custom-call | flops 1073741824 | bytes 6291456 | tf_op jit(solution)/shard_map/outputs/pallas_call | solution.py:538
  38.1 0.8 fusion.3
  38.9 5.0 %collective-permute-start.3 = (bf16[4,128,128]{2,1,0:T(8,128)(2,1)}, bf16[4,128,128]{2,1,0:T(8,128)(2,1)}, u32[]{:S(2)}, u32[]{:S(2)}) collective-permute-start(bf16[4,128,128]{2,1,0:T(8,128)(2,1)} %fusion.3), channel_id=1, source_target_pairs={{0,16},{4,20},{8,24},{12,28},{1,17},{5,21},{9,25},{13,29},{2,18},{... | collective-permute-start | bytes 393224 | tf_op jit(solution)/shard_map/ppermute | solution.py:385
  43.9 2.3 %convolution_convert_fusion.3.gate_ref = bf16[512,1024]{1,0:T(8,128)(2,1)S(1)} fusion(bf16[512,2048]{1,0:T(8,128)(2,1)S(1)} %copy-done, bf16[2048,1024]{1,0:T(8,128)(2,1)S(1)} %copy-done.12), kind=kOutput, calls=%fused_computation.3 | convolution fusion | flops 2148007936 | bytes 7340032 | tf_op jit(solution)/shard_map/dot_general | solution.py:479
  46.3 1.2 %fusion.1 = bf16[4,128,128]{2,1,0:T(8,128)(2,1)S(1)} fusion(bf16[4,128,128]{2,1,0:T(8,128)(2,1)} %collective-permute-done.3, bf16[4,128,256]{2,1,0:T(8,128)(2,1)} %copy-done.8, pred[]{:T(512)S(6)} %ne.11, pred[]{:T(512)S(6)} %ne.10, bf16[128,128]{1,0:T(8,128)(2,1)S(1)} %fusion.18), kind=kOutput, calls=%fused_computation.11 | convolution fusion | flops 17170432 | bytes 558592 | tf_op jit(solution)/shard_map/hij,hjf->hif/dot_general | solution.py:348
  47.5 0.9 broadcast_select_fusion.5
  48.4 1.5 %collective-permute-done.4.got_ref = bf16[4,128,128]{2,1,0:T(8,128)(2,1)S(1)} collective-permute-done((bf16[4,128,128]{2,1,0:T(8,128)(2,1)}, bf16[4,128,128]{2,1,0:T(8,128)(2,1)S(1)}, u32[]{:S(2)}, u32[]{:S(2)}) %collective-permute-start.4) | collective-permute-done | bytes 131104 | tf_op jit(solution)/shard_map/ppermute | solution.py:344
  49.9 2.0 %normed.3 = bf16[128,1024]{1,0:T(8,128)(2,1)S(1)} custom-call(s32[5]{0:T(128)S(1)} %stack.23.swap_ref, bf16[8,512,256]{2,1,0:T(8,128)(2,1)} %outputs.1.parts_ref, bf16[4,128,128]{2,1,0:T(8,128)(2,1)S(1)} %get-tuple-element.34.kept_ref, bf16[4,128,128]{2,1,0:T(8,128)(2,1)S(1)} %collective-permute-done.4.got_ref, ...), custom_call_target="tpu_custom_call" | custom-call | flops 33554432 | bytes 1048576 | tf_op jit(solution)/shard_map/normed/pallas_call | solution.py:318
  51.9 3.1 %convolution_convert_fusion.2 = bf16[128,2048]{1,0:T(8,128)(2,1)S(1)} fusion(bf16[128,1024]{1,0:T(8,128)(2,1)S(1)} %normed.3, bf16[1024,2048]{1,0:T(8,128)(2,1)} %param.21), kind=kOutput, calls=%fused_computation.2 | convolution fusion | flops 537133056 | bytes 4980736 | tf_op jit(solution)/shard_map/dot_general | solution.py:338
  55.1 1.6 %collective-permute-start.5 = (bf16[128,512]{1,0:T(8,128)(2,1)S(1)}, bf16[128,512]{1,0:T(8,128)(2,1)S(1)}, u32[]{:S(2)}, u32[]{:S(2)}) collective-permute-start(bf16[128,512]{1,0:T(8,128)(2,1)S(1)} %slice.130), channel_id=1, source_target_pairs={{0,1},{1,0},{2,3},{3,2},{4,5},{5,4},{6,7},{7,6},{8,9},{9,8},{10,11... | collective-permute-start | bytes 393224 | tf_op jit(solution)/shard_map/ppermute | solution.py:344
  56.7 2.0 %normed.4 = bf16[128,1024]{1,0:T(8,128)(2,1)S(1)} custom-call(s32[5]{0:T(128)S(1)} %stack.23.swap_ref, bf16[8,512,256]{2,1,0:T(8,128)(2,1)} %outputs.1.parts_ref, bf16[4,128,128]{2,1,0:T(8,128)(2,1)S(1)} %get-tuple-element.34.kept_ref, bf16[4,128,128]{2,1,0:T(8,128)(2,1)S(1)} %collective-permute-done.4.got_ref, ...), custom_call_target="tpu_custom_call" | custom-call | flops 33554432 | bytes 1048576 | tf_op jit(solution)/shard_map/normed/pallas_call | solution.py:318
  58.7 0.7 convolution_convert_fusion.1
  60.0 0.6 collective-permute-done.5
  60.7 2.7 %collective-permute-start.8 = (bf16[128,512]{1,0:T(8,128)(2,1)S(1)}, bf16[128,512]{1,0:T(8,128)(2,1)S(1)}, u32[]{:S(2)}, u32[]{:S(2)}) collective-permute-start(bf16[128,512]{1,0:T(8,128)(2,1)S(1)} %add_convert_fusion.3), channel_id=1, source_target_pairs={{0,2},{1,3},{2,0},{3,1},{4,6},{5,7},{6,4},{7,5},{8,10},{9,11},{10,... | collective-permute-start | bytes 393224 | tf_op jit(solution)/shard_map/ppermute | solution.py:344
  63.4 2.5 %normed.5 = bf16[256,1024]{1,0:T(8,128)(2,1)S(1)} custom-call(s32[5]{0:T(128)S(1)} %stack.23.swap_ref, bf16[8,512,256]{2,1,0:T(8,128)(2,1)} %outputs.1.parts_ref, bf16[4,128,128]{2,1,0:T(8,128)(2,1)S(1)} %get-tuple-element.34.kept_ref, bf16[4,128,128]{2,1,0:T(8,128)(2,1)S(1)} %collective-permute-done.4.got_ref, ...), custom_call_target="tpu_custom_call" | custom-call | flops 67108864 | bytes 2097152 | tf_op jit(solution)/shard_map/normed/pallas_call | solution.py:318
  65.9 1.3 %convolution_convert_fusion = bf16[256,2048]{1,0:T(8,128)(2,1)S(1)} fusion(bf16[256,1024]{1,0:T(8,128)(2,1)S(1)} %normed.5, bf16[1024,2048]{1,0:T(8,128)(2,1)S(1)} %copy-done.6), kind=kOutput, calls=%fused_computation | convolution fusion | flops 1074266112 | bytes 5767168 | tf_op jit(solution)/shard_map/dot_general | solution.py:338
  67.2 1.6 %collective-permute-start.6 = (bf16[128,2048]{1,0:T(8,128)(2,1)S(1)}, bf16[128,2048]{1,0:T(8,128)(2,1)S(1)}, u32[]{:S(2)}, u32[]{:S(2)}) collective-permute-start(bf16[128,2048]{1,0:T(8,128)(2,1)S(1)} %slice.132), channel_id=1, source_target_pairs={{0,1},{1,0},{2,3},{3,2},{4,5},{5,4},{6,7},{7,6},{8,9},{9,8},{10,11... | collective-permute-start | bytes 1572872 | tf_op jit(solution)/shard_map/ppermute | solution.py:344
  68.9 3.5 %collective-permute-done.8 = bf16[128,512]{1,0:T(8,128)(2,1)S(1)} collective-permute-done((bf16[128,512]{1,0:T(8,128)(2,1)S(1)}, bf16[128,512]{1,0:T(8,128)(2,1)S(1)}, u32[]{:S(2)}, u32[]{:S(2)}) %collective-permute-start.8) | collective-permute-done | bytes 131104 | tf_op jit(solution)/shard_map/ppermute | solution.py:344
  72.3 2.0 %collective-permute-done.7 = bf16[128,1536]{1,0:T(8,128)(2,1)S(1)} collective-permute-done((bf16[128,1536]{1,0:T(8,128)(2,1)S(1)}, bf16[128,1536]{1,0:T(8,128)(2,1)S(1)}, u32[]{:S(2)}, u32[]{:S(2)}) %collective-permute-start.7) | collective-permute-done | bytes 393248 | tf_op jit(solution)/shard_map/ppermute | solution.py:344
  74.5 1.4 %collective-permute-start.9 = (bf16[128,1536]{1,0:T(8,128)(2,1)S(1)}, bf16[128,1536]{1,0:T(8,128)(2,1)S(1)}, u32[]{:S(2)}, u32[]{:S(2)}) collective-permute-start(bf16[128,1536]{1,0:T(8,128)(2,1)S(1)} %add_convert_fusion.1), channel_id=1, source_target_pairs={{0,2},{1,3},{2,0},{3,1},{4,6},{5,7},{6,4},{7,5},{8,10},{9,11},{10,... | collective-permute-start | bytes 1179656 | tf_op jit(solution)/shard_map/ppermute | solution.py:344
  75.9 17.0 %collective-permute-done.6 = bf16[128,2048]{1,0:T(8,128)(2,1)S(1)} collective-permute-done((bf16[128,2048]{1,0:T(8,128)(2,1)S(1)}, bf16[128,2048]{1,0:T(8,128)(2,1)S(1)}, u32[]{:S(2)}, u32[]{:S(2)}) %collective-permute-start.6) | collective-permute-done | bytes 524320 | tf_op jit(solution)/shard_map/ppermute | solution.py:344
  93.2 0.9 pad_maximum_fusion
  (52 shorter events, 1.6 us)
Async XLA Ops:
  0.0 1.6 %copy-start = (bf16[512,2048]{1,0:T(8,128)(2,1)S(1)}, bf16[512,2048]{1,0:T(8,128)(2,1)}, u32[]{:S(2)}) copy-start(bf16[512,2048]{1,0:T(8,128)(2,1)} %param.11) | copy-start | bytes 6291460
  0.0 4.7 %copy-start.11 = (bf16[2048,1024]{1,0:T(8,128)(2,1)S(1)}, bf16[2048,1024]{1,0:T(8,128)(2,1)}, u32[]{:S(2)}) copy-start(bf16[2048,1024]{1,0:T(8,128)(2,1)} %param.14) | copy-start | bytes 12582916
  4.7 3.8 %copy-start.10 = (bf16[512,512]{1,0:T(8,128)(2,1)}, bf16[512,512]{1,0:T(8,128)(2,1)S(1)}, u32[]{:S(2)}) copy-start(bf16[512,512]{1,0:T(8,128)(2,1)S(1)} %convolution_convert_fusion.6.keys_ref) | copy-start | bytes 1572868
  4.7 2.4 %copy-start.13 = (bf16[2048,512]{1,0:T(8,128)(2,1)S(1)}, bf16[2048,512]{1,0:T(8,128)(2,1)}, u32[]{:S(2)}) copy-start(bf16[2048,512]{1,0:T(8,128)(2,1)} %param.12) | copy-start | bytes 6291460
  7.1 1.3 %copy-start.9 = (bf16[512,1024]{1,0:T(8,128)(2,1)}, bf16[512,1024]{1,0:T(8,128)(2,1)S(1)}, u32[]{:S(2)}) copy-start(bf16[512,1024]{1,0:T(8,128)(2,1)S(1)} %convolution_convert_fusion.4.values_ref) | copy-start | bytes 3145732
  7.1 4.6 %copy-start.1 = (f32[8,512]{1,0:T(8,128)S(1)}, f32[8,512]{1,0:T(8,128)}, u32[]{:S(2)}) copy-start(f32[8,512]{1,0:T(8,128)} %decay_ref.3) | copy-start | bytes 49156
  7.1 4.6 %copy-start.3 = (f32[4,1024]{1,0:T(4,128)S(1)}, f32[4,1024]{1,0:T(4,128)}, u32[]{:S(2)}) copy-start(f32[4,1024]{1,0:T(4,128)} %taps_v_ref.1) | copy-start | bytes 49156
  7.1 4.6 %copy-start.4 = (f32[8,512]{1,0:T(8,128)S(1)}, f32[8,512]{1,0:T(8,128)}, u32[]{:S(2)}) copy-start(f32[8,512]{1,0:T(8,128)} %write_ref.1) | copy-start | bytes 49156
  7.2 4.6 %copy-start.5 = (f32[4,512]{1,0:T(4,128)S(1)}, f32[4,512]{1,0:T(4,128)}, u32[]{:S(2)}) copy-start(f32[4,512]{1,0:T(4,128)} %taps_k_ref.1) | copy-start | bytes 24580
  8.4 15.3 %copy-start.7 = (bf16[512,512]{1,0:T(8,128)(2,1)}, bf16[512,512]{1,0:T(8,128)(2,1)S(1)}, u32[]{:S(2)}) copy-start(bf16[512,512]{1,0:T(8,128)(2,1)S(1)} %convolution_convert_fusion.5.query_ref) | copy-start | bytes 1572868
  8.5 3.2 %collective-permute-start = (bf16[16,2048]{1,0:T(8,128)(2,1)S(1)}, bf16[16,2048]{1,0:T(8,128)(2,1)S(1)}, u32[]{:S(2)}, u32[]{:S(2)}) collective-permute-start(bf16[16,2048]{1,0:T(8,128)(2,1)S(1)} %pad_maximum_fusion.2), channel_id=1, source_target_pairs={{0,4},{4,8},{8,12},{12,16},{16,20},{20,24},{24,28},{1,5},{5,9},{9,... | collective-permute-start | bytes 196616 | tf_op jit(solution)/shard_map/ppermute | solution.py:494
  23.8 7.4 %copy-start.2 = (f32[4,512]{1,0:T(4,128)S(1)}, f32[4,512]{1,0:T(4,128)}, u32[]{:S(2)}) copy-start(f32[4,512]{1,0:T(4,128)} %taps_ref.1) | copy-start | bytes 24580
  23.8 4.3 %collective-permute-start.1 = (bf16[4,128,256]{2,1,0:T(8,128)(2,1)S(1)}, bf16[4,128,256]{2,1,0:T(8,128)(2,1)S(1)}, u32[]{:S(2)}, u32[]{:S(2)}) collective-permute-start(bf16[4,128,256]{2,1,0:T(8,128)(2,1)S(1)} %broadcast_select_fusion.3), channel_id=1, source_target_pairs={{0,4},{4,0},{8,12},{12,8},{16,20},{20,16},{24,28},{28,24},{1,5},{5... | collective-permute-start | bytes 786440 | tf_op jit(solution)/shard_map/ppermute | solution.py:344
  28.5 9.5 %collective-permute-start.2 = (bf16[4,128,256]{2,1,0:T(8,128)(2,1)S(1)}, bf16[4,128,256]{2,1,0:T(8,128)(2,1)S(1)}, u32[]{:S(2)}, u32[]{:S(2)}) collective-permute-start(bf16[4,128,256]{2,1,0:T(8,128)(2,1)S(1)} %pad_maximum_fusion.1), channel_id=1, source_target_pairs={{0,8},{4,12},{8,0},{12,4},{16,24},{20,28},{24,16},{28,20},{1,9},{5... | collective-permute-start | bytes 786440 | tf_op jit(solution)/shard_map/ppermute | solution.py:344
  31.1 12.7 %copy-start.12 = (bf16[2048,1024]{1,0:T(8,128)(2,1)S(1)}, bf16[2048,1024]{1,0:T(8,128)(2,1)}, u32[]{:S(2)}) copy-start(bf16[2048,1024]{1,0:T(8,128)(2,1)} %param.15) | copy-start | bytes 12582916
  38.0 0.9 copy-start.8
  38.9 7.3 %collective-permute-start.3 = (bf16[4,128,128]{2,1,0:T(8,128)(2,1)}, bf16[4,128,128]{2,1,0:T(8,128)(2,1)}, u32[]{:S(2)}, u32[]{:S(2)}) collective-permute-start(bf16[4,128,128]{2,1,0:T(8,128)(2,1)} %fusion.3), channel_id=1, source_target_pairs={{0,16},{4,20},{8,24},{12,28},{1,17},{5,21},{9,25},{13,29},{2,18},{... | collective-permute-start | bytes 393224 | tf_op jit(solution)/shard_map/ppermute | solution.py:385
  48.3 1.6 %collective-permute-start.4 = (bf16[4,128,128]{2,1,0:T(8,128)(2,1)}, bf16[4,128,128]{2,1,0:T(8,128)(2,1)S(1)}, u32[]{:S(2)}, u32[]{:S(2)}) collective-permute-start(bf16[4,128,128]{2,1,0:T(8,128)(2,1)} %get-tuple-element.33), channel_id=1, source_target_pairs={{0,4},{4,0},{8,12},{12,8},{16,20},{20,16},{24,28},{28,24},{1,5},{5... | collective-permute-start | bytes 393224 | tf_op jit(solution)/shard_map/ppermute | solution.py:344
  51.9 6.8 %copy-start.6 = (bf16[1024,2048]{1,0:T(8,128)(2,1)S(1)}, bf16[1024,2048]{1,0:T(8,128)(2,1)}, u32[]{:S(2)}) copy-start(bf16[1024,2048]{1,0:T(8,128)(2,1)} %param.21) | copy-start | bytes 12582916
  55.1 5.6 %collective-permute-start.5 = (bf16[128,512]{1,0:T(8,128)(2,1)S(1)}, bf16[128,512]{1,0:T(8,128)(2,1)S(1)}, u32[]{:S(2)}, u32[]{:S(2)}) collective-permute-start(bf16[128,512]{1,0:T(8,128)(2,1)S(1)} %slice.130), channel_id=1, source_target_pairs={{0,1},{1,0},{2,3},{3,2},{4,5},{5,4},{6,7},{7,6},{8,9},{9,8},{10,11... | collective-permute-start | bytes 393224 | tf_op jit(solution)/shard_map/ppermute | solution.py:344
  59.5 14.9 %collective-permute-start.7 = (bf16[128,1536]{1,0:T(8,128)(2,1)S(1)}, bf16[128,1536]{1,0:T(8,128)(2,1)S(1)}, u32[]{:S(2)}, u32[]{:S(2)}) collective-permute-start(bf16[128,1536]{1,0:T(8,128)(2,1)S(1)} %slice.129), channel_id=1, source_target_pairs={{0,1},{1,0},{2,3},{3,2},{4,5},{5,4},{6,7},{7,6},{8,9},{9,8},{10,11... | collective-permute-start | bytes 1179656 | tf_op jit(solution)/shard_map/ppermute | solution.py:344
  60.7 11.6 %collective-permute-start.8 = (bf16[128,512]{1,0:T(8,128)(2,1)S(1)}, bf16[128,512]{1,0:T(8,128)(2,1)S(1)}, u32[]{:S(2)}, u32[]{:S(2)}) collective-permute-start(bf16[128,512]{1,0:T(8,128)(2,1)S(1)} %add_convert_fusion.3), channel_id=1, source_target_pairs={{0,2},{1,3},{2,0},{3,1},{4,6},{5,7},{6,4},{7,5},{8,10},{9,11},{10,... | collective-permute-start | bytes 393224 | tf_op jit(solution)/shard_map/ppermute | solution.py:344
  67.2 25.7 %collective-permute-start.6 = (bf16[128,2048]{1,0:T(8,128)(2,1)S(1)}, bf16[128,2048]{1,0:T(8,128)(2,1)S(1)}, u32[]{:S(2)}, u32[]{:S(2)}) collective-permute-start(bf16[128,2048]{1,0:T(8,128)(2,1)S(1)} %slice.132), channel_id=1, source_target_pairs={{0,1},{1,0},{2,3},{3,2},{4,5},{5,4},{6,7},{7,6},{8,9},{9,8},{10,11... | collective-permute-start | bytes 1572872 | tf_op jit(solution)/shard_map/ppermute | solution.py:344
  74.5 18.5 %collective-permute-start.9 = (bf16[128,1536]{1,0:T(8,128)(2,1)S(1)}, bf16[128,1536]{1,0:T(8,128)(2,1)S(1)}, u32[]{:S(2)}, u32[]{:S(2)}) collective-permute-start(bf16[128,1536]{1,0:T(8,128)(2,1)S(1)} %add_convert_fusion.1), channel_id=1, source_target_pairs={{0,2},{1,3},{2,0},{3,1},{4,6},{5,7},{6,4},{7,5},{8,10},{9,11},{10,... | collective-permute-start | bytes 1179656 | tf_op jit(solution)/shard_map/ppermute | solution.py:344

commit v4 on v3

--- a/solution.py
+++ b/solution.py
@@ -9,10 +9,11 @@
 
 HD = 128
 CHUNK = 128
-RIM = 16
+RIM = 8
 BF = jnp.bfloat16
 F32 = jnp.float32
 EXACT = lax.Precision.HIGHEST
+SCALAR = pl.BlockSpec(memory_space=pltpu.SMEM)
 WHOLE = pl.BlockSpec(memory_space=pltpu.VMEM)
 
 
@@ -44,8 +45,8 @@
     return values * (lax.rsqrt(jnp.sum(values * values, axis=-1, keepdims=True) + 1e-06) * factor)
 
 
-def stage_rows(stage, rims_ref, rows_ref):
-    stage[0:8] = rims_ref[RIM - 8 : RIM].astype(F32)
+def stage_rows(stage, at_ref, rims_ref, rows_ref):
+    stage[0:8] = jnp.where(at_ref[0] > 0, rims_ref[RIM - 8 : RIM].astype(F32), 0.0)
     stage[8:] = rows_ref[...].astype(F32)
 
 
@@ -133,6 +134,7 @@
     group,
     ratio,
     chunks,
+    at_ref,
     keys_ref,
     values_ref,
     rims_k_ref,
@@ -150,8 +152,8 @@
 ):
     row_ids, col_ids = grid_ids()
     eye = jnp.where(row_ids == col_ids, 1.0, 0.0)
-    stage_rows(stage_k, rims_k_ref, keys_ref)
-    stage_rows(stage_v, rims_v_ref, values_ref)
+    stage_rows(stage_k, at_ref, rims_k_ref, keys_ref)
+    stage_rows(stage_v, at_ref, rims_v_ref, values_ref)
     taps_k = taps_k_ref[...]
     taps_v = taps_v_ref[...]
     decays = []
@@ -242,6 +244,7 @@
     group,
     ratio,
     chunks,
+    at_ref,
     query_ref,
     rims_ref,
     taps_ref,
@@ -253,7 +256,7 @@
     stage,
 ):
     row_ids, col_ids = grid_ids()
-    stage_rows(stage, rims_ref, query_ref)
+    stage_rows(stage, at_ref, rims_ref, query_ref)
     decays = [
         cumulated(head_rows(decay_ref, ratio, chunks, group, member)) for member in range(group)
     ]
@@ -299,8 +302,7 @@
             parts_out[place, rows, HD:] = local.astype(BF)
 
 
-def norm_kernel(heads, swap_ref, parts_ref, kept_ref, got_ref, gate_ref, normed_ref):
-    swap = swap_ref[0] != 0
+def normed_heads(heads, swap, parts_ref, kept_ref, got_ref, gate_ref, normed_ref):
     half = heads // 2
     for head in range(heads):
         lanes = slice(head * HD, (head + 1) * HD)
@@ -311,6 +313,63 @@
         normed_ref[:, lanes] = (
             attended * spread * silu(gate_ref[:, lanes].astype(F32))
         ).astype(BF)
+
+
+def norm_kernel(heads, plan_ref, parts_ref, kept_ref, got_ref, gate_ref, normed_ref):
+    normed_heads(heads, plan_ref[0] != 0, parts_ref, kept_ref, got_ref, gate_ref, normed_ref)
+
+
+def far_kernel(
+    heads, plan_ref, parts_ref, kept_ref, got_ref, gate_ref, weight_hbm, out_ref, weight, normed, sems
+):
+    pieces = weight.shape[0]
+    depth = weight.shape[1]
+    copies = [
+        pltpu.make_async_copy(
+            weight_hbm.at[pl.ds(at * depth, depth)], weight.at[at], sems.at[at]
+        )
+        for at in range(pieces)
+    ]
+    for copy in copies:
+        copy.start()
+    normed_heads(heads, plan_ref[0] != 0, parts_ref, kept_ref, got_ref, gate_ref, normed)
+    total = None
+    for at, copy in enumerate(copies):
+        copy.wait()
+        part = jnp.dot(
+            normed[:, at * depth : (at + 1) * depth], weight[at], preferred_element_type=F32
+        )
+        total = part if total is None else total + part
+    out_ref[...] = total.astype(BF)
+
+
+def far_rows(plan, parts, kept, got, gate_in, w_out, length):
+    heads = parts.shape[0]
+    features, width = w_out.shape
+    pieces = 4
+    return pl.pallas_call(
+        functools.partial(far_kernel, heads),
+        grid_spec=pltpu.PrefetchScalarGridSpec(
+            num_scalar_prefetch=1,
+            grid=(1,),
+            in_specs=[
+                pl.BlockSpec((heads, length, 2 * HD), lambda c, plan: (0, plan[1], 0)),
+                WHOLE,
+                WHOLE,
+                pl.BlockSpec((length, heads * HD), lambda c, plan: (plan[1], 0)),
+                pl.BlockSpec(memory_space=pltpu.HBM),
+            ],
+            out_specs=pl.BlockSpec((length, width), lambda c, plan: (0, 0)),
+            scratch_shapes=[
+                pltpu.VMEM((pieces, features // pieces, width), BF),
+                pltpu.VMEM((length, features), BF),
+                pltpu.SemaphoreType.DMA((pieces,)),
+            ],
+        ),
+        out_shape=jax.ShapeDtypeStruct((length, width), BF),
+        compiler_params=pltpu.CompilerParams(vmem_limit_bytes=20 << 20),
+        name="far",
+    )(plan, in_hbm(parts), kept, got, gate_in, w_out)
 
 
 def final_rows(first, count, plan, parts, kept, got, gate_in, w_out, length):
@@ -350,24 +409,14 @@
     )
     if earlier.shape[-1] == HD:
         return moved + later[..., HD:].astype(F32)
-    return jnp.concatenate([moved[..., :HD], moved[..., HD:] + later[..., HD:].astype(F32)], axis=-1)
+    in_state = lax.broadcasted_iota(jnp.int32, later.shape, 2) >= HD
+    return moved + jnp.where(in_state, later.astype(F32), 0.0)
 
 
 def incoming_state(total, axis, covers):
-    covers = list(covers)
+    early, late = covers
     count = lax.axis_size(axis)
     index = lax.axis_index(axis)
-
-    def cover(value):
-        for at, work in enumerate(covers):
-            if work is not None:
-                value, work = lax.optimization_barrier((value, work))
-                done.append(work)
-                covers[at] = None
-                break
-        return value
-
-    done = []
     odd = (index & 1) != 0
     half = total.shape[0] // 2
     mine = jnp.where(odd, total[half:], total[:half])
@@ -375,39 +424,36 @@
     first = jnp.where(odd, other, mine)
     second = jnp.where(odd, mine, other)
     total = after(second, first).astype(BF)
-    before_map = before_state = None
+    eye = jnp.broadcast_to(jnp.eye(HD, dtype=BF), (half, HD, HD))
+    before = jnp.concatenate([eye, jnp.zeros_like(eye)], axis=-1)
     bit = 2
-    while bit < count:
+    while 2 * bit < count:
         high = (index & bit) != 0
-        last = 2 * bit >= count
-        if last and before_map is not None:
-            pairs = [(at, at ^ bit) for at in range(count) if not at & bit]
-            state = cover(lax.ppermute(total[..., HD:], axis, pairs))
-            moved = after(jnp.concatenate([before_map, before_state], axis=-1), state)
-            before_state = jnp.where(high, moved, before_state.astype(F32))
+        other = exchanged(total, axis, bit)
+        if bit == 2:
+            other, early = lax.optimization_barrier((other, early))
+        lower, upper = jnp.where(high, other, total), jnp.where(high, total, other)
+        if 4 * bit < count:
+            total = after(upper, lower).astype(BF)
         else:
-            other = cover(exchanged(total, axis, bit))
-            if before_map is None:
-                eye = jnp.broadcast_to(jnp.eye(HD, dtype=BF), (half, HD, HD))
-                before_map = jnp.where(high, other[..., :HD], eye)
-                before_state = jnp.where(high, other[..., HD:], jnp.zeros((), BF))
-            else:
-                before = jnp.concatenate([before_map, before_state], axis=-1)
-                moved = jnp.where(high, after(before, other), before.astype(F32)).astype(BF)
-                before_map, before_state = moved[..., :HD], moved[..., HD:]
-            if not last:
-                total = after(
-                    jnp.where(high, total, other), jnp.where(high, other, total)
-                ).astype(BF)
+            total = after(upper, lower[..., HD:]).astype(BF)
+        other, _ = lax.optimization_barrier((other, total))
+        if bit == 2:
+            before = jnp.where(high, other, before)
+        else:
+            before = jnp.where(high, after(before, other).astype(BF), before)
         bit *= 2
-    if before_state is None:
-        before_state = jnp.zeros((half, HD, HD), F32)
-    before_state = before_state.astype(BF)
-    passed = after(first, before_state).astype(BF)
-    kept = jnp.where(odd, passed, before_state)
-    got = exchanged(jnp.where(odd, before_state, passed), axis, 1)
-    done.extend(work for work in covers if work is not None)
-    return kept, got, done
+    high = (index & bit) != 0
+    state = exchanged(total[..., -HD:], axis, bit)
+    reach = jnp.where(high, before[..., :HD], jnp.zeros((), BF))
+    before = jnp.concatenate([reach, before[..., HD:]], axis=-1)
+    passed = after(first, before).astype(BF)
+    keep, send = jnp.where(odd, passed, before), jnp.where(odd, before, passed)
+    late = late(early)
+    state, keep, send, late = lax.optimization_barrier((state, keep, send, late))
+    got = exchanged(after(send, state).astype(BF), axis, 1)
+    kept = after(keep, state).astype(BF)
+    return kept, got, early, late
 
 
 def summed(*values):
@@ -438,8 +484,7 @@
     return summed(take(index), up, down)
 
 
-def swapped_sum(rows_of, axis):
-    far = rows_of(0, 1, None)[0]
+def swapped_sum(far, rows_of, axis):
     width = far.shape[-1] // 4
     early, late = slice(0, width), slice(width, 4 * width)
     first_in = exchanged(far[:, early], axis, 1)
@@ -475,12 +520,15 @@
     write_rate,
     w_out,
 ):
-    def project(weights):
-        return jnp.dot(inputs, weights, preferred_element_type=F32).astype(BF)
+    def project(weights, earlier=None):
+        tokens = inputs
+        if earlier is not None:
+            tokens, _ = lax.optimization_barrier((inputs, earlier))
+        return jnp.dot(tokens, weights, preferred_element_type=F32).astype(BF)
 
     proj_key = project(w_key)
     proj_value = project(w_value)
-    proj_query = project(w_query)
+    proj_query = project(w_query, (proj_key, proj_value))
     rows = inputs.shape[0]
     key_width = proj_key.shape[1]
     key_heads = key_width // HD
@@ -491,8 +539,9 @@
         [proj_key[-RIM:], proj_value[-RIM:], proj_query[-RIM:]], axis=1
     )
     count = lax.axis_size("ctx")
-    rims = lax.ppermute(tails, "ctx", [(at, at + 1) for at in range(count - 1)])
-    gate_in = project(w_gate_out)
+    rims = lax.ppermute(tails, "ctx", [(at, (at + 1) % count) for at in range(count)])
+    place_ctx = lax.axis_index("ctx").reshape(1)
+
     group = 2 if key_heads % 2 == 0 else 1
 
     def cols(length, width, start=0):
@@ -506,6 +555,7 @@
         functools.partial(local_kernel, group, ratio, chunks),
         grid=(key_heads // group,),
         in_specs=[
+            SCALAR,
             cols(rows, HD),
             cols(rows, ratio * HD),
             cols(RIM, HD),
@@ -534,11 +584,12 @@
         compiler_params=pltpu.CompilerParams(vmem_limit_bytes=32 << 20),
         cost_estimate=cost(16 * heads * rows, 4 * heads * rows * HD, 12 * heads * rows * HD),
         name="local",
-    )(in_hbm(proj_key), in_hbm(proj_value), rims, rims, conv_key, conv_value, decay_log, write_rate)
+    )(place_ctx, in_hbm(proj_key), in_hbm(proj_value), rims, rims, conv_key, conv_value, decay_log, write_rate)
     parts = pl.pallas_call(
         functools.partial(output_kernel, group, ratio, chunks),
         grid=(key_heads // group,),
         in_specs=[
+            SCALAR,
             cols(rows, HD),
             cols(RIM, HD, key_width + heads * HD),
             cols(taps_len, HD),
@@ -553,8 +604,8 @@
         compiler_params=pltpu.CompilerParams(vmem_limit_bytes=24 << 20),
         cost_estimate=cost(8 * heads * rows, 2 * heads * rows * HD, 12 * heads * rows * HD),
         name="outputs",
-    )(in_hbm(proj_query), rims, conv_query, in_hbm(keys), in_hbm(wy), in_hbm(starts), decay_log)
-    kept, got, (parts, gate_in) = incoming_state(total, "ctx", (parts, gate_in))
+    )(place_ctx, in_hbm(proj_query), rims, conv_query, in_hbm(keys), in_hbm(wy), in_hbm(starts), decay_log)
+    kept, got, parts, gate_in = incoming_state(total, "ctx", (parts, functools.partial(project, w_gate_out)))
     spread = lax.axis_size("head")
     place = lax.axis_index("head")
     length = rows // spread
@@ -572,7 +623,8 @@
         return final_rows(first, amount, steps, parts, kept, got, gate_in, w_out, length)
 
     if spread == 4:
-        return swapped_sum(rows_of, "head")
+        far = far_rows(plan, parts, kept, got, gate_in, w_out, length)
+        return swapped_sum(far, rows_of, "head")
     return line_sum(rows_of(0, spread, None), "head")
 
 

time: 94.5 us -> 86.4 us (0.914)
  starting transfers between devices: 21 us -> 12.2 us
  matrix products: 17.2 us -> 12.1 us
  waiting for transfers between devices: 26.7 us -> 31.4 us
  Pallas kernels: 25.4 us -> 26.8 us
    ppermute x2 -> x1, starting transfers between devices: 7.34 us -> 0.69 us  [shards(): lax.ppermute(tails, 'ctx', [(at, (at + 1) % count) for at in range(count)])]
    ppermute x2 -> x1, waiting for transfers between devices: 0.88 us -> 4.48 us  [shards(): lax.ppermute(tails, 'ctx', [(at, (at + 1) % count) for at in range(count)])]
    pallas_call x0 -> x1, Pallas kernels: none -> 3.48 us  [far_rows(): pl.pallas_call(functools.partial(far_kernel, heads), grid_spec=pltpu.Pref...]
    dot_general x3 -> x2, matrix products: 5.08 us -> 2.01 us  [final_rows(): mixed = jnp.dot(normed, w_out, preferred_element_type=F32).astype(BF)]
    ppermute x8 -> x9, starting transfers between devices: 13.7 us -> 11.5 us  [exchanged(): lax.ppermute(value, axis, [(source, source ^ bit) for source in range(cou...]
    dot_general x4 -> x5, matrix products: 3.13 us -> 0.99 us  [after(): jnp.einsum('hij,hjf->hif', later[..., :HD].astype(BF), earlier.astype(BF)...]
    pallas_call x3 -> x2, Pallas kernels: 6.56 us -> 4.54 us  [final_rows(): pl.pallas_call(functools.partial(norm_kernel, heads), grid_spec=pltpu.Pre...]
    ppermute x8 -> x9, waiting for transfers between devices: 25.8 us -> 26.9 us  [exchanged(): lax.ppermute(value, axis, [(source, source ^ bit) for source in range(cou...]
  transfers between devices with their start and end apart: 10 -> 10, of which waited for: 7 -> 9; matrix products, arithmetic and copies ran while one was open for 5% -> 6% of each run, Pallas kernels for 12% -> 13%
where the time goes in v4:
time: 86.4 us; the launch traced here: 86.1 us
  waiting for transfers between devices  31.4 us (36%)
  Pallas kernels  26.8 us (31%)
  starting transfers between devices  12.2 us (14%)
  matrix products  12.1 us (14%)
  local copies, waits for them, and re-layouts  1.84 us (2%)
  other arithmetic  1.43 us (2%)
    ppermute x9, waiting for transfers between devices, exchanged(): lax.ppermute(value, axis, [(source, source ^ bit) for source in range(cou...  26.9 us
    pallas_call x1, Pallas kernels, shards(): pl.pallas_call(functools.partial(local_kernel, group, ratio, chunks), gri...  12 us
    ppermute x9, starting transfers between devices, exchanged(): lax.ppermute(value, axis, [(source, source ^ bit) for source in range(cou...  11.5 us
    dot_general x4, matrix products, project(): return jnp.dot(tokens, weights, preferred_element_type=F32).astype(BF)  9.06 us
    pallas_call x1, Pallas kernels, shards(): pl.pallas_call(functools.partial(output_kernel, group, ratio, chunks), gr...  6.78 us
    pallas_call x2, Pallas kernels, final_rows(): pl.pallas_call(functools.partial(norm_kernel, heads), grid_spec=pltpu.Pre...  4.54 us
    ppermute x1, waiting for transfers between devices, shards(): lax.ppermute(tails, 'ctx', [(at, (at + 1) % count) for at in range(count)])  4.48 us
    pallas_call x1, Pallas kernels, far_rows(): pl.pallas_call(functools.partial(far_kernel, heads), grid_spec=pltpu.Pref...  3.48 us
  transfers between devices with their start and end apart: 10, of which 9 were waited for; matrix products, arithmetic and copies ran while one was open for 6% of the time, Pallas kernels for 13%

profile of v4, /device:TPU:0, one launch (start us, length us, event | category | flops | bytes accessed | tf_op | source)
XLA Modules:
  0.0 86.1 jit_solution(13663897511929888247)
XLA Ops:
  0.0 1.6 %copy-done = bf16[512,2048]{1,0:T(8,128)(2,1)S(1)} copy-done((bf16[512,2048]{1,0:T(8,128)(2,1)S(1)}, bf16[512,2048]{1,0:T(8,128)(2,1)}, u32[]{:S(2)}) %copy-start) | copy-done | bytes 2097176
  1.6 3.1 %convolution_convert_fusion.5.keys_ref = bf16[512,512]{1,0:T(8,128)(2,1)S(1)} fusion(bf16[512,2048]{1,0:T(8,128)(2,1)S(1)} %copy-done, bf16[2048,512]{1,0:T(8,128)(2,1)} %param.13), kind=kOutput, calls=%fused_computation.5 | convolution fusion | flops 1074003968 | bytes 4718592 | tf_op jit(solution)/shard_map/dot_general | solution.py:527
  4.7 2.4 %convolution_convert_fusion.3.values_ref = bf16[512,1024]{1,0:T(8,128)(2,1)S(1)} fusion(bf16[512,2048]{1,0:T(8,128)(2,1)S(1)} %copy-done, bf16[2048,1024]{1,0:T(8,128)(2,1)S(1)} %copy-done.10), kind=kOutput, calls=%fused_computation.3 | convolution fusion | flops 2148007936 | bytes 7340032 | tf_op jit(solution)/shard_map/dot_general | solution.py:527
  7.2 1.2 %convolution_convert_fusion.4.query_ref = bf16[512,512]{1,0:T(8,128)(2,1)S(1)} fusion(bf16[512,2048]{1,0:T(8,128)(2,1)S(1)} %copy-done, bf16[2048,512]{1,0:T(8,128)(2,1)S(1)} %copy-done.12), kind=kOutput, calls=%fused_computation.4 | convolution fusion | flops 1074003968 | bytes 4718592 | tf_op jit(solution)/shard_map/dot_general | solution.py:527
  8.5 0.7 collective-permute-start
  9.2 4.5 %collective-permute-done.rims_k_ref.rims_v_ref.rims_ref = bf16[8,2048]{1,0:T(8,128)(2,1)S(1)} collective-permute-done((bf16[8,2048]{1,0:T(8,128)(2,1)S(1)}, bf16[8,2048]{1,0:T(8,128)(2,1)S(1)}, u32[]{:S(2)}, u32[]{:S(2)}) %collective-permute-start) | collective-permute-done | bytes 32800 | tf_op jit(solution)/shard_map/ppermute | solution.py:542
  13.7 12.0 %local.1 = (bf16[512,512]{1,0:T(8,128)(2,1)}, bf16[8,512,256]{2,1,0:T(8,128)(2,1)}, bf16[8,3,128,256]{3,2,1,0:T(8,128)(2,1)}, bf16[8,128,256]{2,1,0:T(8,128)(2,1)S(1)}) custom-call(s32[1]{0:T(128)} %bitcast.5.at_ref, bf16[512,512]{1,0:T(8,128)(2,1)} %copy-done.8, bf16[512,1024]{1,0:T(8,128)(2,1)} %copy-done.9, ...), custom_call_target="tpu_custom_call" | custom-call | flops 2147483648 | bytes 6291456 | tf_op jit(solution)/shard_map/local/pallas_call | solution.py:554
  25.8 1.5 %collective-permute-done.1 = bf16[4,128,256]{2,1,0:T(8,128)(2,1)S(1)} collective-permute-done((bf16[4,128,256]{2,1,0:T(8,128)(2,1)S(1)}, bf16[4,128,256]{2,1,0:T(8,128)(2,1)S(1)}, u32[]{:S(2)}, u32[]{:S(2)}) %collective-permute-start.1) | collective-permute-done | bytes 262176 | tf_op jit(solution)/shard_map/ppermute | solution.py:403
  27.4 0.2 fusion
  27.6 1.4 %collective-permute-start.2 = (bf16[4,128,256]{2,1,0:T(8,128)(2,1)S(1)}, bf16[4,128,256]{2,1,0:T(8,128)(2,1)S(1)}, u32[]{:S(2)}, u32[]{:S(2)}) collective-permute-start(bf16[4,128,256]{2,1,0:T(8,128)(2,1)S(1)} %fusion), channel_id=1, source_target_pairs={{0,8},{4,12},{8,0},{12,4},{16,24},{20,28},{24,16},{28,20},{1,9},{5... | collective-permute-start | bytes 786440 | tf_op jit(solution)/shard_map/ppermute | solution.py:403
  29.2 6.8 %outputs.1.parts_ref = bf16[8,512,256]{2,1,0:T(8,128)(2,1)} custom-call(s32[1]{0:T(128)} %bitcast.5.at_ref, bf16[512,512]{1,0:T(8,128)(2,1)} %copy-done.7, bf16[8,2048]{1,0:T(8,128)(2,1)S(1)} %collective-permute-done.rims_k_ref.rims_v_ref.rims_ref, f32[4,512]{1,0:T(4,128)S(1)} %copy-done.3, bf16[512,512]{1,0:T(8,128)(2,1)} %get-tuple-element.25.keys_ref, ...), custom_call_target="tpu_custom_call" | custom-call | flops 1073741824 | bytes 6291456 | tf_op jit(solution)/shard_map/outputs/pallas_call | solution.py:588
  36.1 0.2 add_convert_fusion.4
  36.2 2.3 %collective-permute-start.3 = (bf16[4,128,128]{2,1,0:T(8,128)(2,1)S(1)}, bf16[4,128,128]{2,1,0:T(8,128)(2,1)S(1)}, u32[]{:S(2)}, u32[]{:S(2)}) collective-permute-start(bf16[4,128,128]{2,1,0:T(8,128)(2,1)S(1)} %add_convert_fusion.4), channel_id=1, source_target_pairs={{0,16},{4,20},{8,24},{12,28},{16,0},{20,4},{24,8},{28,12},{1,17},{... | collective-permute-start | bytes 393224 | tf_op jit(solution)/shard_map/ppermute | solution.py:403
  38.7 2.4 %convolution_convert_fusion.2.gate_ref = bf16[512,1024]{1,0:T(8,128)(2,1)S(1)} fusion(bf16[512,2048]{1,0:T(8,128)(2,1)S(1)} %copy-done, bf16[2048,1024]{1,0:T(8,128)(2,1)S(1)} %copy-done.11), kind=kOutput, calls=%fused_computation.2 | convolution fusion | flops 2148007936 | bytes 7340032 | tf_op jit(solution)/shard_map/dot_general | solution.py:527
  41.1 0.2 broadcast_select_fusion.1
  41.3 0.2 collective-permute-done.3
  41.5 0.2 fusion.3
  42.0 1.2 %collective-permute-done.4.got_ref = bf16[4,128,128]{2,1,0:T(8,128)(2,1)S(1)} collective-permute-done((bf16[4,128,128]{2,1,0:T(8,128)(2,1)S(1)}, bf16[4,128,128]{2,1,0:T(8,128)(2,1)S(1)}, u32[]{:S(2)}, u32[]{:S(2)}) %collective-permute-start.4) | collective-permute-done | bytes 131104 | tf_op jit(solution)/shard_map/ppermute | solution.py:403
  43.1 3.5 %far.1 = bf16[128,2048]{1,0:T(8,128)(2,1)S(1)} custom-call(s32[5]{0:T(128)S(1)} %stack.23.plan_ref, bf16[8,512,256]{2,1,0:T(8,128)(2,1)} %outputs.1.parts_ref, bf16[4,128,128]{2,1,0:T(8,128)(2,1)S(1)} %fusion.2.kept_ref, bf16[4,128,128]{2,1,0:T(8,128)(2,1)S(1)} %collective-permute-done.4.got_ref, bf16[512,1024]{1,0:T(8,128)(2,1)S(1)} %convolution_convert_fusion.2.gate_ref, ...), custom_call_target="tpu_custom_call" | custom-call | tf_op jit(solution)/shard_map/far/pallas_call | solution.py:350
  46.7 2.1 %collective-permute-start.5 = (bf16[128,512]{1,0:T(8,128)(2,1)S(1)}, bf16[128,512]{1,0:T(8,128)(2,1)S(1)}, u32[]{:S(2)}, u32[]{:S(2)}) collective-permute-start(bf16[128,512]{1,0:T(8,128)(2,1)S(1)} %slice.119), channel_id=1, source_target_pairs={{0,1},{1,0},{2,3},{3,2},{4,5},{5,4},{6,7},{7,6},{8,9},{9,8},{10,11... | collective-permute-start | bytes 393224 | tf_op jit(solution)/shard_map/ppermute | solution.py:403
  48.8 2.0 %normed.2 = bf16[128,1024]{1,0:T(8,128)(2,1)S(1)} custom-call(s32[5]{0:T(128)S(1)} %stack.23.plan_ref, bf16[8,512,256]{2,1,0:T(8,128)(2,1)} %outputs.1.parts_ref, bf16[4,128,128]{2,1,0:T(8,128)(2,1)S(1)} %fusion.2.kept_ref, bf16[4,128,128]{2,1,0:T(8,128)(2,1)S(1)} %collective-permute-done.4.got_ref, bf16[512,1024]{1,0:T(8,128)(2,1)S(1)} %convolution_convert_fusion.2.gate_ref), custom_call_target="tpu_custom_call" | custom-call | flops 33554432 | bytes 1048576 | tf_op jit(solution)/shard_map/normed/pallas_call | solution.py:377
  50.8 0.7 convolution_convert_fusion.1
  51.7 0.9 %collective-permute-done.5 = bf16[128,512]{1,0:T(8,128)(2,1)S(1)} collective-permute-done((bf16[128,512]{1,0:T(8,128)(2,1)S(1)}, bf16[128,512]{1,0:T(8,128)(2,1)S(1)}, u32[]{:S(2)}, u32[]{:S(2)}) %collective-permute-start.5) | collective-permute-done | bytes 131104 | tf_op jit(solution)/shard_map/ppermute | solution.py:403
  52.6 2.8 %collective-permute-start.8 = (bf16[128,512]{1,0:T(8,128)(2,1)S(1)}, bf16[128,512]{1,0:T(8,128)(2,1)S(1)}, u32[]{:S(2)}, u32[]{:S(2)}) collective-permute-start(bf16[128,512]{1,0:T(8,128)(2,1)S(1)} %add_convert_fusion.3), channel_id=1, source_target_pairs={{0,2},{1,3},{2,0},{3,1},{4,6},{5,7},{6,4},{7,5},{8,10},{9,11},{10,... | collective-permute-start | bytes 393224 | tf_op jit(solution)/shard_map/ppermute | solution.py:403
  55.5 2.5 %normed.3 = bf16[256,1024]{1,0:T(8,128)(2,1)S(1)} custom-call(s32[5]{0:T(128)S(1)} %stack.23.plan_ref, bf16[8,512,256]{2,1,0:T(8,128)(2,1)} %outputs.1.parts_ref, bf16[4,128,128]{2,1,0:T(8,128)(2,1)S(1)} %fusion.2.kept_ref, bf16[4,128,128]{2,1,0:T(8,128)(2,1)S(1)} %collective-permute-done.4.got_ref, bf16[512,1024]{1,0:T(8,128)(2,1)S(1)} %convolution_convert_fusion.2.gate_ref), custom_call_target="tpu_custom_call" | custom-call | flops 67108864 | bytes 2097152 | tf_op jit(solution)/shard_map/normed/pallas_call | solution.py:377
  58.0 1.3 %convolution_convert_fusion = bf16[256,2048]{1,0:T(8,128)(2,1)S(1)} fusion(bf16[256,1024]{1,0:T(8,128)(2,1)S(1)} %normed.3, bf16[1024,2048]{1,0:T(8,128)(2,1)S(1)} %copy-done.1), kind=kOutput, calls=%fused_computation | convolution fusion | flops 1074266112 | bytes 5767168 | tf_op jit(solution)/shard_map/dot_general | solution.py:397
  59.3 1.6 %collective-permute-start.6 = (bf16[128,2048]{1,0:T(8,128)(2,1)S(1)}, bf16[128,2048]{1,0:T(8,128)(2,1)S(1)}, u32[]{:S(2)}, u32[]{:S(2)}) collective-permute-start(bf16[128,2048]{1,0:T(8,128)(2,1)S(1)} %slice.121), channel_id=1, source_target_pairs={{0,1},{1,0},{2,3},{3,2},{4,5},{5,4},{6,7},{7,6},{8,9},{9,8},{10,11... | collective-permute-start | bytes 1572872 | tf_op jit(solution)/shard_map/ppermute | solution.py:403
  60.9 3.0 %collective-permute-done.8 = bf16[128,512]{1,0:T(8,128)(2,1)S(1)} collective-permute-done((bf16[128,512]{1,0:T(8,128)(2,1)S(1)}, bf16[128,512]{1,0:T(8,128)(2,1)S(1)}, u32[]{:S(2)}, u32[]{:S(2)}) %collective-permute-start.8) | collective-permute-done | bytes 131104 | tf_op jit(solution)/shard_map/ppermute | solution.py:403
  64.0 2.5 %collective-permute-done.7 = bf16[128,1536]{1,0:T(8,128)(2,1)S(1)} collective-permute-done((bf16[128,1536]{1,0:T(8,128)(2,1)S(1)}, bf16[128,1536]{1,0:T(8,128)(2,1)S(1)}, u32[]{:S(2)}, u32[]{:S(2)}) %collective-permute-start.7) | collective-permute-done | bytes 393248 | tf_op jit(solution)/shard_map/ppermute | solution.py:403
  66.6 0.9 %collective-permute-start.9 = (bf16[128,1536]{1,0:T(8,128)(2,1)S(1)}, bf16[128,1536]{1,0:T(8,128)(2,1)S(1)}, u32[]{:S(2)}, u32[]{:S(2)}) collective-permute-start(bf16[128,1536]{1,0:T(8,128)(2,1)S(1)} %add_convert_fusion.1), channel_id=1, source_target_pairs={{0,2},{1,3},{2,0},{3,1},{4,6},{5,7},{6,4},{7,5},{8,10},{9,11},{10,... | collective-permute-start | bytes 1179656 | tf_op jit(solution)/shard_map/ppermute | solution.py:403
  67.5 17.5 %collective-permute-done.6 = bf16[128,2048]{1,0:T(8,128)(2,1)S(1)} collective-permute-done((bf16[128,2048]{1,0:T(8,128)(2,1)S(1)}, bf16[128,2048]{1,0:T(8,128)(2,1)S(1)}, u32[]{:S(2)}, u32[]{:S(2)}) %collective-permute-start.6) | collective-permute-done | bytes 524320 | tf_op jit(solution)/shard_map/ppermute | solution.py:403
  85.3 0.8 pad_maximum_fusion
  (52 shorter events, 1.3 us)
Async XLA Ops:
  0.0 1.6 %copy-start = (bf16[512,2048]{1,0:T(8,128)(2,1)S(1)}, bf16[512,2048]{1,0:T(8,128)(2,1)}, u32[]{:S(2)}) copy-start(bf16[512,2048]{1,0:T(8,128)(2,1)} %param.11) | copy-start | bytes 6291460
  0.0 4.7 %copy-start.10 = (bf16[2048,1024]{1,0:T(8,128)(2,1)S(1)}, bf16[2048,1024]{1,0:T(8,128)(2,1)}, u32[]{:S(2)}) copy-start(bf16[2048,1024]{1,0:T(8,128)(2,1)} %param.14) | copy-start | bytes 12582916
  4.7 2.4 %copy-start.8 = (bf16[512,512]{1,0:T(8,128)(2,1)}, bf16[512,512]{1,0:T(8,128)(2,1)S(1)}, u32[]{:S(2)}) copy-start(bf16[512,512]{1,0:T(8,128)(2,1)S(1)} %convolution_convert_fusion.5.keys_ref) | copy-start | bytes 1572868
  4.7 2.4 %copy-start.12 = (bf16[2048,512]{1,0:T(8,128)(2,1)S(1)}, bf16[2048,512]{1,0:T(8,128)(2,1)}, u32[]{:S(2)}) copy-start(bf16[2048,512]{1,0:T(8,128)(2,1)} %param.12) | copy-start | bytes 6291460
  7.1 1.3 %copy-start.9 = (bf16[512,1024]{1,0:T(8,128)(2,1)}, bf16[512,1024]{1,0:T(8,128)(2,1)S(1)}, u32[]{:S(2)}) copy-start(bf16[512,1024]{1,0:T(8,128)(2,1)S(1)} %convolution_convert_fusion.3.values_ref) | copy-start | bytes 3145732
  7.1 1.3 %slice-start = ((bf16[512,512]{1,0:T(8,128)(2,1)}), bf16[8,512]{1,0:T(8,128)(2,1)S(1)}, s32[]{:S(2)}) async-start(bf16[512,512]{1,0:T(8,128)(2,1)} %copy-done.8), calls=%async_computation | async-start | bytes 16384 | tf_op jit(solution)/shard_map/slice | solution.py:539
  7.1 6.5 %copy-start.2 = (f32[8,512]{1,0:T(8,128)S(1)}, f32[8,512]{1,0:T(8,128)}, u32[]{:S(2)}) copy-start(f32[8,512]{1,0:T(8,128)} %decay_ref.3) | copy-start | bytes 49156
  7.2 6.5 %copy-start.4 = (f32[4,1024]{1,0:T(4,128)S(1)}, f32[4,1024]{1,0:T(4,128)}, u32[]{:S(2)}) copy-start(f32[4,1024]{1,0:T(4,128)} %taps_v_ref.1) | copy-start | bytes 49156
  7.2 6.5 %copy-start.5 = (f32[8,512]{1,0:T(8,128)S(1)}, f32[8,512]{1,0:T(8,128)}, u32[]{:S(2)}) copy-start(f32[8,512]{1,0:T(8,128)} %write_ref.1) | copy-start | bytes 49156
  7.2 6.5 %copy-start.6 = (f32[4,512]{1,0:T(4,128)S(1)}, f32[4,512]{1,0:T(4,128)}, u32[]{:S(2)}) copy-start(f32[4,512]{1,0:T(4,128)} %taps_k_ref.1) | copy-start | bytes 24580
  8.5 17.2 %copy-start.7 = (bf16[512,512]{1,0:T(8,128)(2,1)}, bf16[512,512]{1,0:T(8,128)(2,1)S(1)}, u32[]{:S(2)}) copy-start(bf16[512,512]{1,0:T(8,128)(2,1)S(1)} %convolution_convert_fusion.4.query_ref) | copy-start | bytes 1572868
  8.5 5.2 %collective-permute-start = (bf16[8,2048]{1,0:T(8,128)(2,1)S(1)}, bf16[8,2048]{1,0:T(8,128)(2,1)S(1)}, u32[]{:S(2)}, u32[]{:S(2)}) collective-permute-start(bf16[8,2048]{1,0:T(8,128)(2,1)S(1)} %pad_maximum_fusion.3), channel_id=1, source_target_pairs={{0,4},{4,8},{8,12},{12,16},{16,20},{20,24},{24,28},{28,0},{1,5},{5... | collective-permute-start | bytes 98312 | tf_op jit(solution)/shard_map/ppermute | solution.py:542
  25.7 3.4 %copy-start.3 = (f32[4,512]{1,0:T(4,128)S(1)}, f32[4,512]{1,0:T(4,128)}, u32[]{:S(2)}) copy-start(f32[4,512]{1,0:T(4,128)} %taps_ref.1) | copy-start | bytes 24580
  25.7 1.6 %collective-permute-start.1 = (bf16[4,128,256]{2,1,0:T(8,128)(2,1)S(1)}, bf16[4,128,256]{2,1,0:T(8,128)(2,1)S(1)}, u32[]{:S(2)}, u32[]{:S(2)}) collective-permute-start(bf16[4,128,256]{2,1,0:T(8,128)(2,1)S(1)} %broadcast_select_fusion.5), channel_id=1, source_target_pairs={{0,4},{4,0},{8,12},{12,8},{16,20},{20,16},{24,28},{28,24},{1,5},{5... | collective-permute-start | bytes 786440 | tf_op jit(solution)/shard_map/ppermute | solution.py:403
  27.6 8.4 %collective-permute-start.2 = (bf16[4,128,256]{2,1,0:T(8,128)(2,1)S(1)}, bf16[4,128,256]{2,1,0:T(8,128)(2,1)S(1)}, u32[]{:S(2)}, u32[]{:S(2)}) collective-permute-start(bf16[4,128,256]{2,1,0:T(8,128)(2,1)S(1)} %fusion), channel_id=1, source_target_pairs={{0,8},{4,12},{8,0},{12,4},{16,24},{20,28},{24,16},{28,20},{1,9},{5... | collective-permute-start | bytes 786440 | tf_op jit(solution)/shard_map/ppermute | solution.py:403
  29.1 9.6 %copy-start.11 = (bf16[2048,1024]{1,0:T(8,128)(2,1)S(1)}, bf16[2048,1024]{1,0:T(8,128)(2,1)}, u32[]{:S(2)}) copy-start(bf16[2048,1024]{1,0:T(8,128)(2,1)} %param.15) | copy-start | bytes 12582916
  36.2 5.3 %collective-permute-start.3 = (bf16[4,128,128]{2,1,0:T(8,128)(2,1)S(1)}, bf16[4,128,128]{2,1,0:T(8,128)(2,1)S(1)}, u32[]{:S(2)}, u32[]{:S(2)}) collective-permute-start(bf16[4,128,128]{2,1,0:T(8,128)(2,1)S(1)} %add_convert_fusion.4), channel_id=1, source_target_pairs={{0,16},{4,20},{8,24},{12,28},{16,0},{20,4},{24,8},{28,12},{1,17},{... | collective-permute-start | bytes 393224 | tf_op jit(solution)/shard_map/ppermute | solution.py:403
  38.7 4.4 %copy-start.1 = (bf16[1024,2048]{1,0:T(8,128)(2,1)S(1)}, bf16[1024,2048]{1,0:T(8,128)(2,1)}, u32[]{:S(2)}) copy-start(bf16[1024,2048]{1,0:T(8,128)(2,1)} %weight_hbm.1) | copy-start | bytes 12582916
  41.7 1.4 %collective-permute-start.4 = (bf16[4,128,128]{2,1,0:T(8,128)(2,1)S(1)}, bf16[4,128,128]{2,1,0:T(8,128)(2,1)S(1)}, u32[]{:S(2)}, u32[]{:S(2)}) collective-permute-start(bf16[4,128,128]{2,1,0:T(8,128)(2,1)S(1)} %fusion.3), channel_id=1, source_target_pairs={{0,4},{4,0},{8,12},{12,8},{16,20},{20,16},{24,28},{28,24},{1,5},{5... | collective-permute-start | bytes 393224 | tf_op jit(solution)/shard_map/ppermute | solution.py:403
  46.7 6.0 %collective-permute-start.5 = (bf16[128,512]{1,0:T(8,128)(2,1)S(1)}, bf16[128,512]{1,0:T(8,128)(2,1)S(1)}, u32[]{:S(2)}, u32[]{:S(2)}) collective-permute-start(bf16[128,512]{1,0:T(8,128)(2,1)S(1)} %slice.119), channel_id=1, source_target_pairs={{0,1},{1,0},{2,3},{3,2},{4,5},{5,4},{6,7},{7,6},{8,9},{9,8},{10,11... | collective-permute-start | bytes 393224 | tf_op jit(solution)/shard_map/ppermute | solution.py:403
  51.6 14.9 %collective-permute-start.7 = (bf16[128,1536]{1,0:T(8,128)(2,1)S(1)}, bf16[128,1536]{1,0:T(8,128)(2,1)S(1)}, u32[]{:S(2)}, u32[]{:S(2)}) collective-permute-start(bf16[128,1536]{1,0:T(8,128)(2,1)S(1)} %slice.118), channel_id=1, source_target_pairs={{0,1},{1,0},{2,3},{3,2},{4,5},{5,4},{6,7},{7,6},{8,9},{9,8},{10,11... | collective-permute-start | bytes 1179656 | tf_op jit(solution)/shard_map/ppermute | solution.py:403
  52.6 11.3 %collective-permute-start.8 = (bf16[128,512]{1,0:T(8,128)(2,1)S(1)}, bf16[128,512]{1,0:T(8,128)(2,1)S(1)}, u32[]{:S(2)}, u32[]{:S(2)}) collective-permute-start(bf16[128,512]{1,0:T(8,128)(2,1)S(1)} %add_convert_fusion.3), channel_id=1, source_target_pairs={{0,2},{1,3},{2,0},{3,1},{4,6},{5,7},{6,4},{7,5},{8,10},{9,11},{10,... | collective-permute-start | bytes 393224 | tf_op jit(solution)/shard_map/ppermute | solution.py:403
  59.3 25.7 %collective-permute-start.6 = (bf16[128,2048]{1,0:T(8,128)(2,1)S(1)}, bf16[128,2048]{1,0:T(8,128)(2,1)S(1)}, u32[]{:S(2)}, u32[]{:S(2)}) collective-permute-start(bf16[128,2048]{1,0:T(8,128)(2,1)S(1)} %slice.121), channel_id=1, source_target_pairs={{0,1},{1,0},{2,3},{3,2},{4,5},{5,4},{6,7},{7,6},{8,9},{9,8},{10,11... | collective-permute-start | bytes 1572872 | tf_op jit(solution)/shard_map/ppermute | solution.py:403
  66.6 18.5 %collective-permute-start.9 = (bf16[128,1536]{1,0:T(8,128)(2,1)S(1)}, bf16[128,1536]{1,0:T(8,128)(2,1)S(1)}, u32[]{:S(2)}, u32[]{:S(2)}) collective-permute-start(bf16[128,1536]{1,0:T(8,128)(2,1)S(1)} %add_convert_fusion.1), channel_id=1, source_target_pairs={{0,2},{1,3},{2,0},{3,1},{4,6},{5,7},{6,4},{7,5},{8,10},{9,11},{10,... | collective-permute-start | bytes 1179656 | tf_op jit(solution)/shard_map/ppermute | solution.py:403

commit v5 on v4

--- a/solution.py
+++ b/solution.py
@@ -320,32 +320,43 @@
 
 
 def far_kernel(
-    heads, plan_ref, parts_ref, kept_ref, got_ref, gate_ref, weight_hbm, out_ref, weight, normed, sems
+    heads,
+    plan_ref,
+    parts_ref,
+    kept_ref,
+    got_ref,
+    gate_ref,
+    weight_hbm,
+    out_ref,
+    normed_ref,
+    weight,
+    sems,
 ):
-    pieces = weight.shape[0]
-    depth = weight.shape[1]
+    pieces, depth, width = weight.shape
     copies = [
         pltpu.make_async_copy(
-            weight_hbm.at[pl.ds(at * depth, depth)], weight.at[at], sems.at[at]
+            weight_hbm.at[pl.ds(at * depth, depth), pl.ds(0, width)], weight.at[at], sems.at[at]
         )
         for at in range(pieces)
     ]
     for copy in copies:
         copy.start()
-    normed_heads(heads, plan_ref[0] != 0, parts_ref, kept_ref, got_ref, gate_ref, normed)
+    normed_heads(heads, plan_ref[0] != 0, parts_ref, kept_ref, got_ref, gate_ref, normed_ref)
     total = None
     for at, copy in enumerate(copies):
         copy.wait()
         part = jnp.dot(
-            normed[:, at * depth : (at + 1) * depth], weight[at], preferred_element_type=F32
+            normed_ref[:, at * depth : (at + 1) * depth],
+            weight[at],
+            preferred_element_type=F32,
         )
         total = part if total is None else total + part
     out_ref[...] = total.astype(BF)
 
 
-def far_rows(plan, parts, kept, got, gate_in, w_out, length):
+def far_rows(plan, parts, kept, got, gate_in, w_out, length, width):
     heads = parts.shape[0]
-    features, width = w_out.shape
+    features = w_out.shape[0]
     pieces = 4
     return pl.pallas_call(
         functools.partial(far_kernel, heads),
@@ -359,22 +370,27 @@
                 pl.BlockSpec((length, heads * HD), lambda c, plan: (plan[1], 0)),
                 pl.BlockSpec(memory_space=pltpu.HBM),
             ],
-            out_specs=pl.BlockSpec((length, width), lambda c, plan: (0, 0)),
+            out_specs=[
+                pl.BlockSpec((length, width), lambda c, plan: (0, 0)),
+                pl.BlockSpec((length, features), lambda c, plan: (0, 0)),
+            ],
             scratch_shapes=[
                 pltpu.VMEM((pieces, features // pieces, width), BF),
-                pltpu.VMEM((length, features), BF),
                 pltpu.SemaphoreType.DMA((pieces,)),
             ],
         ),
-        out_shape=jax.ShapeDtypeStruct((length, width), BF),
+        out_shape=[
+            jax.ShapeDtypeStruct((length, width), BF),
+            jax.ShapeDtypeStruct((length, features), BF),
+        ],
         compiler_params=pltpu.CompilerParams(vmem_limit_bytes=20 << 20),
         name="far",
     )(plan, in_hbm(parts), kept, got, gate_in, w_out)
 
 
-def final_rows(first, count, plan, parts, kept, got, gate_in, w_out, length):
+def normed_rows(first, count, plan, parts, kept, got, gate_in, length):
     heads = parts.shape[0]
-    normed = pl.pallas_call(
+    return pl.pallas_call(
         functools.partial(norm_kernel, heads),
         grid_spec=pltpu.PrefetchScalarGridSpec(
             num_scalar_prefetch=1,
@@ -394,8 +410,6 @@
         ),
         name="normed",
     )(plan, in_hbm(parts), kept, got, gate_in)
-    mixed = jnp.dot(normed, w_out, preferred_element_type=F32).astype(BF)
-    return mixed.reshape(count, length, w_out.shape[1])
 
 
 def exchanged(value, axis, bit):
@@ -484,16 +498,22 @@
     return summed(take(index), up, down)
 
 
-def swapped_sum(far, rows_of, axis):
-    width = far.shape[-1] // 4
-    early, late = slice(0, width), slice(width, 4 * width)
-    first_in = exchanged(far[:, early], axis, 1)
-    passed = rows_of(1, 1, None)[0]
-    far_late, passed = lax.optimization_barrier((far[:, late], passed))
+def mixed_rows(normed, w_out):
+    return jnp.dot(normed, w_out, preferred_element_type=F32).astype(BF)
+
+
+def swapped_sum(far, far_normed, w_out, rows_of, axis):
+    width = far.shape[-1]
+    early, late = slice(0, width), slice(width, w_out.shape[1])
+    first_in = exchanged(far, axis, 1)
+    far_normed, passed = lax.optimization_barrier((far_normed, rows_of(1, 1, far)))
+    far_late = mixed_rows(far_normed, w_out)[:, late]
     later_in = exchanged(far_late, axis, 1)
+    passed, _ = lax.optimization_barrier((passed, far_late))
+    passed = mixed_rows(passed, w_out)
     paired = summed(passed[:, early], first_in)
     first = exchanged(paired, axis, 2)
-    rest = rows_of(2, 2, paired)
+    rest = mixed_rows(rows_of(2, 2, paired), w_out).reshape(2, -1, w_out.shape[1])
     later_in, first = lax.optimization_barrier((later_in, first))
     later = exchanged(summed(passed[:, late], later_in), axis, 2)
     near = exchanged(rest[0], axis, 1)
@@ -620,12 +640,15 @@
         steps = plan
         if earlier is not None:
             steps, _ = lax.optimization_barrier((plan, earlier))
-        return final_rows(first, amount, steps, parts, kept, got, gate_in, w_out, length)
+        return normed_rows(first, amount, steps, parts, kept, got, gate_in, length)
 
     if spread == 4:
-        far = far_rows(plan, parts, kept, got, gate_in, w_out, length)
-        return swapped_sum(far, rows_of, "head")
-    return line_sum(rows_of(0, spread, None), "head")
+        far, far_normed = far_rows(
+            plan, parts, kept, got, gate_in, w_out, length, 3 * w_out.shape[1] // 8
+        )
+        return swapped_sum(far, far_normed, w_out, rows_of, "head")
+    whole = mixed_rows(rows_of(0, spread, None), w_out)
+    return line_sum(whole.reshape(spread, length, w_out.shape[1]), "head")
 
 
 def solution(mesh):

time: 86.4 us -> 84.5 us (0.978)
  waiting for transfers between devices: 31.4 us -> 27.2 us
  starting transfers between devices: 12.2 us -> 14.3 us
    ppermute x9, waiting for transfers between devices: 26.9 us -> 22.7 us  [exchanged(): lax.ppermute(value, axis, [(source, source ^ bit) for source in range(cou...]
    ppermute x9, starting transfers between devices: 11.5 us -> 13.6 us  [exchanged(): lax.ppermute(value, axis, [(source, source ^ bit) for source in range(cou...]
    dot_general x2 -> x3, matrix products: 2.01 us -> 2.73 us  [mixed_rows(): return jnp.dot(normed, w_out, preferred_element_type=F32).astype(BF)]
  transfers between devices with their start and end apart: 10 -> 10, of which waited for: 9 -> 9; matrix products, arithmetic and copies ran while one was open for 6% -> 7% of each run, Pallas kernels for 13% -> 13%
where the time goes in v5:
time: 84.5 us; the launch traced here: 84.3 us
  waiting for transfers between devices  27.2 us (32%)
  Pallas kernels  26.4 us (31%)
  starting transfers between devices  14.3 us (17%)
  matrix products  12.8 us (15%)
  local copies, waits for them, and re-layouts  1.83 us (2%)
  other arithmetic  1.43 us (2%)
    ppermute x9, waiting for transfers between devices, exchanged(): lax.ppermute(value, axis, [(source, source ^ bit) for source in range(cou...  22.7 us
    ppermute x9, starting transfers between devices, exchanged(): lax.ppermute(value, axis, [(source, source ^ bit) for source in range(cou...  13.6 us
    pallas_call x1, Pallas kernels, shards(): pl.pallas_call(functools.partial(local_kernel, group, ratio, chunks), gri...  12 us
    dot_general x4, matrix products, project(): return jnp.dot(tokens, weights, preferred_element_type=F32).astype(BF)  9.06 us
    pallas_call x1, Pallas kernels, shards(): pl.pallas_call(functools.partial(output_kernel, group, ratio, chunks), gr...  6.77 us
    pallas_call x2, Pallas kernels, normed_rows(): pl.pallas_call(functools.partial(norm_kernel, heads), grid_spec=pltpu.Pre...  4.54 us
    ppermute x1, waiting for transfers between devices, shards(): lax.ppermute(tails, 'ctx', [(at, (at + 1) % count) for at in range(count)])  4.48 us
    pallas_call x1, Pallas kernels, far_rows(): pl.pallas_call(functools.partial(far_kernel, heads), grid_spec=pltpu.Pref...  3.07 us
  transfers between devices with their start and end apart: 10, of which 9 were waited for; matrix products, arithmetic and copies ran while one was open for 7% of the time, Pallas kernels for 13%

profile of v5, /device:TPU:0, one launch (start us, length us, event | category | flops | bytes accessed | tf_op | source)
XLA Modules:
  0.0 84.3 jit_solution(623130713781548873)
XLA Ops:
  0.0 1.6 %copy-done = bf16[512,2048]{1,0:T(8,128)(2,1)S(1)} copy-done((bf16[512,2048]{1,0:T(8,128)(2,1)S(1)}, bf16[512,2048]{1,0:T(8,128)(2,1)}, u32[]{:S(2)}) %copy-start) | copy-done | bytes 2097176
  1.6 3.1 %convolution_convert_fusion.5.keys_ref = bf16[512,512]{1,0:T(8,128)(2,1)S(1)} fusion(bf16[512,2048]{1,0:T(8,128)(2,1)S(1)} %copy-done, bf16[2048,512]{1,0:T(8,128)(2,1)} %param.13), kind=kOutput, calls=%fused_computation.5 | convolution fusion | flops 1074003968 | bytes 4718592 | tf_op jit(solution)/shard_map/dot_general | solution.py:547
  4.7 2.4 %convolution_convert_fusion.3.values_ref = bf16[512,1024]{1,0:T(8,128)(2,1)S(1)} fusion(bf16[512,2048]{1,0:T(8,128)(2,1)S(1)} %copy-done, bf16[2048,1024]{1,0:T(8,128)(2,1)S(1)} %copy-done.10), kind=kOutput, calls=%fused_computation.3 | convolution fusion | flops 2148007936 | bytes 7340032 | tf_op jit(solution)/shard_map/dot_general | solution.py:547
  7.2 1.2 %convolution_convert_fusion.4.query_ref = bf16[512,512]{1,0:T(8,128)(2,1)S(1)} fusion(bf16[512,2048]{1,0:T(8,128)(2,1)S(1)} %copy-done, bf16[2048,512]{1,0:T(8,128)(2,1)S(1)} %copy-done.12), kind=kOutput, calls=%fused_computation.4 | convolution fusion | flops 1074003968 | bytes 4718592 | tf_op jit(solution)/shard_map/dot_general | solution.py:547
  8.5 0.7 collective-permute-start
  9.2 4.5 %collective-permute-done.rims_k_ref.rims_v_ref.rims_ref = bf16[8,2048]{1,0:T(8,128)(2,1)S(1)} collective-permute-done((bf16[8,2048]{1,0:T(8,128)(2,1)S(1)}, bf16[8,2048]{1,0:T(8,128)(2,1)S(1)}, u32[]{:S(2)}, u32[]{:S(2)}) %collective-permute-start) | collective-permute-done | bytes 32800 | tf_op jit(solution)/shard_map/ppermute | solution.py:562
  13.7 12.0 %local.1 = (bf16[512,512]{1,0:T(8,128)(2,1)}, bf16[8,512,256]{2,1,0:T(8,128)(2,1)}, bf16[8,3,128,256]{3,2,1,0:T(8,128)(2,1)}, bf16[8,128,256]{2,1,0:T(8,128)(2,1)S(1)}) custom-call(s32[1]{0:T(128)} %bitcast.5.at_ref, bf16[512,512]{1,0:T(8,128)(2,1)} %copy-done.8, bf16[512,1024]{1,0:T(8,128)(2,1)} %copy-done.9, ...), custom_call_target="tpu_custom_call" | custom-call | flops 2147483648 | bytes 6291456 | tf_op jit(solution)/shard_map/local/pallas_call | solution.py:574
  25.8 1.5 %collective-permute-done.1 = bf16[4,128,256]{2,1,0:T(8,128)(2,1)S(1)} collective-permute-done((bf16[4,128,256]{2,1,0:T(8,128)(2,1)S(1)}, bf16[4,128,256]{2,1,0:T(8,128)(2,1)S(1)}, u32[]{:S(2)}, u32[]{:S(2)}) %collective-permute-start.1) | collective-permute-done | bytes 262176 | tf_op jit(solution)/shard_map/ppermute | solution.py:417
  27.4 0.2 fusion
  27.6 1.4 %collective-permute-start.2 = (bf16[4,128,256]{2,1,0:T(8,128)(2,1)S(1)}, bf16[4,128,256]{2,1,0:T(8,128)(2,1)S(1)}, u32[]{:S(2)}, u32[]{:S(2)}) collective-permute-start(bf16[4,128,256]{2,1,0:T(8,128)(2,1)S(1)} %fusion), channel_id=1, source_target_pairs={{0,8},{4,12},{8,0},{12,4},{16,24},{20,28},{24,16},{28,20},{1,9},{5... | collective-permute-start | bytes 786440 | tf_op jit(solution)/shard_map/ppermute | solution.py:417
  29.1 6.8 %outputs.1.parts_ref = bf16[8,512,256]{2,1,0:T(8,128)(2,1)} custom-call(s32[1]{0:T(128)} %bitcast.5.at_ref, bf16[512,512]{1,0:T(8,128)(2,1)} %copy-done.7, bf16[8,2048]{1,0:T(8,128)(2,1)S(1)} %collective-permute-done.rims_k_ref.rims_v_ref.rims_ref, f32[4,512]{1,0:T(4,128)S(1)} %copy-done.3, bf16[512,512]{1,0:T(8,128)(2,1)} %get-tuple-element.29.keys_ref, ...), custom_call_target="tpu_custom_call" | custom-call | flops 1073741824 | bytes 6291456 | tf_op jit(solution)/shard_map/outputs/pallas_call | solution.py:608
  36.2 2.3 %collective-permute-start.3 = (bf16[4,128,128]{2,1,0:T(8,128)(2,1)S(1)}, bf16[4,128,128]{2,1,0:T(8,128)(2,1)S(1)}, u32[]{:S(2)}, u32[]{:S(2)}) collective-permute-start(bf16[4,128,128]{2,1,0:T(8,128)(2,1)S(1)} %add_convert_fusion.4), channel_id=1, source_target_pairs={{0,16},{4,20},{8,24},{12,28},{16,0},{20,4},{24,8},{28,12},{1,17},{... | collective-permute-start | bytes 393224 | tf_op jit(solution)/shard_map/ppermute | solution.py:417
  38.7 2.4 %convolution_convert_fusion.2.gate_ref = bf16[512,1024]{1,0:T(8,128)(2,1)S(1)} fusion(bf16[512,2048]{1,0:T(8,128)(2,1)S(1)} %copy-done, bf16[2048,1024]{1,0:T(8,128)(2,1)S(1)} %copy-done.11), kind=kOutput, calls=%fused_computation.2 | convolution fusion | flops 2148007936 | bytes 7340032 | tf_op jit(solution)/shard_map/dot_general | solution.py:547
  41.1 0.2 broadcast_select_fusion.1
  41.3 0.2 collective-permute-done.3
  41.5 0.2 fusion.3
  42.0 1.2 %collective-permute-done.4.got_ref = bf16[4,128,128]{2,1,0:T(8,128)(2,1)S(1)} collective-permute-done((bf16[4,128,128]{2,1,0:T(8,128)(2,1)S(1)}, bf16[4,128,128]{2,1,0:T(8,128)(2,1)S(1)}, u32[]{:S(2)}, u32[]{:S(2)}) %collective-permute-start.4) | collective-permute-done | bytes 131104 | tf_op jit(solution)/shard_map/ppermute | solution.py:417
  43.1 3.1 %far.1 = (bf16[128,768]{1,0:T(8,128)(2,1)S(1)}, bf16[128,1024]{1,0:T(8,128)(2,1)S(1)}) custom-call(s32[5]{0:T(128)S(1)} %stack.23.plan_ref, bf16[8,512,256]{2,1,0:T(8,128)(2,1)} %outputs.1.parts_ref, bf16[4,128,128]{2,1,0:T(8,128)(2,1)S(1)} %fusion.2.kept_ref, bf16[4,128,128]{2,1,0:T(8,128)(2,1)S(1)} %collective-permute-done.4.got_ref, ...), custom_call_target="tpu_custom_call" | custom-call | tf_op jit(solution)/shard_map/far/pallas_call | solution.py:361
  46.2 2.2 %collective-permute-start.5 = (bf16[128,768]{1,0:T(8,128)(2,1)S(1)}, bf16[128,768]{1,0:T(8,128)(2,1)S(1)}, u32[]{:S(2)}, u32[]{:S(2)}) collective-permute-start(bf16[128,768]{1,0:T(8,128)(2,1)S(1)} %get-tuple-element.41), channel_id=1, source_target_pairs={{0,1},{1,0},{2,3},{3,2},{4,5},{5,4},{6,7},{7,6},{8,9},{9,8},{10,11... | collective-permute-start | bytes 589832 | tf_op jit(solution)/shard_map/ppermute | solution.py:417
  48.4 2.0 %normed.2 = bf16[128,1024]{1,0:T(8,128)(2,1)S(1)} custom-call(s32[5]{0:T(128)S(1)} %stack.23.plan_ref, bf16[8,512,256]{2,1,0:T(8,128)(2,1)} %outputs.1.parts_ref, bf16[4,128,128]{2,1,0:T(8,128)(2,1)S(1)} %fusion.2.kept_ref, bf16[4,128,128]{2,1,0:T(8,128)(2,1)S(1)} %collective-permute-done.4.got_ref, bf16[512,1024]{1,0:T(8,128)(2,1)S(1)} %convolution_convert_fusion.2.gate_ref), custom_call_target="tpu_custom_call" | custom-call | flops 33554432 | bytes 1048576 | tf_op jit(solution)/shard_map/normed/pallas_call | solution.py:393
  50.4 0.7 fusion.14
  51.3 0.7 convolution_convert_fusion.1
  52.0 1.6 %collective-permute-done.5 = bf16[128,768]{1,0:T(8,128)(2,1)S(1)} collective-permute-done((bf16[128,768]{1,0:T(8,128)(2,1)S(1)}, bf16[128,768]{1,0:T(8,128)(2,1)S(1)}, u32[]{:S(2)}, u32[]{:S(2)}) %collective-permute-start.5) | collective-permute-done | bytes 196640 | tf_op jit(solution)/shard_map/ppermute | solution.py:417
  53.7 2.8 %collective-permute-start.8 = (bf16[128,768]{1,0:T(8,128)(2,1)S(1)}, bf16[128,768]{1,0:T(8,128)(2,1)S(1)}, u32[]{:S(2)}, u32[]{:S(2)}) collective-permute-start(bf16[128,768]{1,0:T(8,128)(2,1)S(1)} %add_convert_fusion.3), channel_id=1, source_target_pairs={{0,2},{1,3},{2,0},{3,1},{4,6},{5,7},{6,4},{7,5},{8,10},{9,11},{10,... | collective-permute-start | bytes 589832 | tf_op jit(solution)/shard_map/ppermute | solution.py:417
  56.5 2.5 %normed.3 = bf16[256,1024]{1,0:T(8,128)(2,1)S(1)} custom-call(s32[5]{0:T(128)S(1)} %stack.23.plan_ref, bf16[8,512,256]{2,1,0:T(8,128)(2,1)} %outputs.1.parts_ref, bf16[4,128,128]{2,1,0:T(8,128)(2,1)S(1)} %fusion.2.kept_ref, bf16[4,128,128]{2,1,0:T(8,128)(2,1)S(1)} %collective-permute-done.4.got_ref, bf16[512,1024]{1,0:T(8,128)(2,1)S(1)} %convolution_convert_fusion.2.gate_ref), custom_call_target="tpu_custom_call" | custom-call | flops 67108864 | bytes 2097152 | tf_op jit(solution)/shard_map/normed/pallas_call | solution.py:393
  59.0 1.3 %convolution_convert_fusion = bf16[256,2048]{1,0:T(8,128)(2,1)S(1)} fusion(bf16[256,1024]{1,0:T(8,128)(2,1)S(1)} %normed.3, bf16[1024,2048]{1,0:T(8,128)(2,1)S(1)} %copy-done.1), kind=kOutput, calls=%fused_computation | convolution fusion | flops 1074266112 | bytes 5767168 | tf_op jit(solution)/shard_map/dot_general | solution.py:502
  60.3 2.4 %collective-permute-start.6 = (bf16[128,2048]{1,0:T(8,128)(2,1)S(1)}, bf16[128,2048]{1,0:T(8,128)(2,1)S(1)}, u32[]{:S(2)}, u32[]{:S(2)}) collective-permute-start(bf16[128,2048]{1,0:T(8,128)(2,1)S(1)} %slice.117), channel_id=1, source_target_pairs={{0,1},{1,0},{2,3},{3,2},{4,5},{5,4},{6,7},{7,6},{8,9},{9,8},{10,11... | collective-permute-start | bytes 1572872 | tf_op jit(solution)/shard_map/ppermute | solution.py:417
  62.7 3.3 %collective-permute-done.7 = bf16[128,1280]{1,0:T(8,128)(2,1)S(1)} collective-permute-done((bf16[128,1280]{1,0:T(8,128)(2,1)S(1)}, bf16[128,1280]{1,0:T(8,128)(2,1)S(1)}, u32[]{:S(2)}, u32[]{:S(2)}) %collective-permute-start.7) | collective-permute-done | bytes 327712 | tf_op jit(solution)/shard_map/ppermute | solution.py:417
  66.1 2.3 %collective-permute-start.9 = (bf16[128,1280]{1,0:T(8,128)(2,1)S(1)}, bf16[128,1280]{1,0:T(8,128)(2,1)S(1)}, u32[]{:S(2)}, u32[]{:S(2)}) collective-permute-start(bf16[128,1280]{1,0:T(8,128)(2,1)S(1)} %add_convert_fusion.1), channel_id=1, source_target_pairs={{0,2},{1,3},{2,0},{3,1},{4,6},{5,7},{6,4},{7,5},{8,10},{9,11},{10,... | collective-permute-start | bytes 983048 | tf_op jit(solution)/shard_map/ppermute | solution.py:417
  68.5 13.9 %collective-permute-done.9 = bf16[128,1280]{1,0:T(8,128)(2,1)S(1)} collective-permute-done((bf16[128,1280]{1,0:T(8,128)(2,1)S(1)}, bf16[128,1280]{1,0:T(8,128)(2,1)S(1)}, u32[]{:S(2)}, u32[]{:S(2)}) %collective-permute-start.9) | collective-permute-done | bytes 327712 | tf_op jit(solution)/shard_map/ppermute | solution.py:417
  82.4 0.8 collective-permute-done.6
  83.4 0.8 %pad_maximum_fusion = bf16[128,2048]{1,0:T(8,128)(2,1)} fusion(bf16[128,1280]{1,0:T(8,128)(2,1)S(1)} %add_convert_fusion, bf16[128,768]{1,0:T(8,128)(2,1)S(1)} %add_convert_fusion.2), kind=kLoop, calls=%fused_computation.17 | loop fusion | flops 1048576 | bytes 1048576 | tf_op jit(solution)/shard_map/concatenate | solution.py:521
  (52 shorter events, 1.5 us)
Async XLA Ops:
  0.0 1.6 %copy-start = (bf16[512,2048]{1,0:T(8,128)(2,1)S(1)}, bf16[512,2048]{1,0:T(8,128)(2,1)}, u32[]{:S(2)}) copy-start(bf16[512,2048]{1,0:T(8,128)(2,1)} %param.11) | copy-start | bytes 6291460
  0.0 4.7 %copy-start.10 = (bf16[2048,1024]{1,0:T(8,128)(2,1)S(1)}, bf16[2048,1024]{1,0:T(8,128)(2,1)}, u32[]{:S(2)}) copy-start(bf16[2048,1024]{1,0:T(8,128)(2,1)} %param.14) | copy-start | bytes 12582916
  4.7 2.4 %copy-start.8 = (bf16[512,512]{1,0:T(8,128)(2,1)}, bf16[512,512]{1,0:T(8,128)(2,1)S(1)}, u32[]{:S(2)}) copy-start(bf16[512,512]{1,0:T(8,128)(2,1)S(1)} %convolution_convert_fusion.5.keys_ref) | copy-start | bytes 1572868
  4.7 2.4 %copy-start.12 = (bf16[2048,512]{1,0:T(8,128)(2,1)S(1)}, bf16[2048,512]{1,0:T(8,128)(2,1)}, u32[]{:S(2)}) copy-start(bf16[2048,512]{1,0:T(8,128)(2,1)} %param.12) | copy-start | bytes 6291460
  7.1 1.3 %copy-start.9 = (bf16[512,1024]{1,0:T(8,128)(2,1)}, bf16[512,1024]{1,0:T(8,128)(2,1)S(1)}, u32[]{:S(2)}) copy-start(bf16[512,1024]{1,0:T(8,128)(2,1)S(1)} %convolution_convert_fusion.3.values_ref) | copy-start | bytes 3145732
  7.1 1.3 %slice-start = ((bf16[512,512]{1,0:T(8,128)(2,1)}), bf16[8,512]{1,0:T(8,128)(2,1)S(1)}, s32[]{:S(2)}) async-start(bf16[512,512]{1,0:T(8,128)(2,1)} %copy-done.8), calls=%async_computation | async-start | bytes 16384 | tf_op jit(solution)/shard_map/slice | solution.py:559
  7.1 6.5 %copy-start.2 = (f32[8,512]{1,0:T(8,128)S(1)}, f32[8,512]{1,0:T(8,128)}, u32[]{:S(2)}) copy-start(f32[8,512]{1,0:T(8,128)} %decay_ref.3) | copy-start | bytes 49156
  7.2 6.5 %copy-start.4 = (f32[4,1024]{1,0:T(4,128)S(1)}, f32[4,1024]{1,0:T(4,128)}, u32[]{:S(2)}) copy-start(f32[4,1024]{1,0:T(4,128)} %taps_v_ref.1) | copy-start | bytes 49156
  7.2 6.5 %copy-start.5 = (f32[8,512]{1,0:T(8,128)S(1)}, f32[8,512]{1,0:T(8,128)}, u32[]{:S(2)}) copy-start(f32[8,512]{1,0:T(8,128)} %write_ref.1) | copy-start | bytes 49156
  7.2 6.5 %copy-start.6 = (f32[4,512]{1,0:T(4,128)S(1)}, f32[4,512]{1,0:T(4,128)}, u32[]{:S(2)}) copy-start(f32[4,512]{1,0:T(4,128)} %taps_k_ref.1) | copy-start | bytes 24580
  8.5 17.2 %copy-start.7 = (bf16[512,512]{1,0:T(8,128)(2,1)}, bf16[512,512]{1,0:T(8,128)(2,1)S(1)}, u32[]{:S(2)}) copy-start(bf16[512,512]{1,0:T(8,128)(2,1)S(1)} %convolution_convert_fusion.4.query_ref) | copy-start | bytes 1572868
  8.5 5.2 %collective-permute-start = (bf16[8,2048]{1,0:T(8,128)(2,1)S(1)}, bf16[8,2048]{1,0:T(8,128)(2,1)S(1)}, u32[]{:S(2)}, u32[]{:S(2)}) collective-permute-start(bf16[8,2048]{1,0:T(8,128)(2,1)S(1)} %pad_maximum_fusion.3), channel_id=1, source_target_pairs={{0,4},{4,8},{8,12},{12,16},{16,20},{20,24},{24,28},{28,0},{1,5},{5... | collective-permute-start | bytes 98312 | tf_op jit(solution)/shard_map/ppermute | solution.py:562
  25.7 3.4 %copy-start.3 = (f32[4,512]{1,0:T(4,128)S(1)}, f32[4,512]{1,0:T(4,128)}, u32[]{:S(2)}) copy-start(f32[4,512]{1,0:T(4,128)} %taps_ref.1) | copy-start | bytes 24580
  25.7 1.6 %collective-permute-start.1 = (bf16[4,128,256]{2,1,0:T(8,128)(2,1)S(1)}, bf16[4,128,256]{2,1,0:T(8,128)(2,1)S(1)}, u32[]{:S(2)}, u32[]{:S(2)}) collective-permute-start(bf16[4,128,256]{2,1,0:T(8,128)(2,1)S(1)} %broadcast_select_fusion.5), channel_id=1, source_target_pairs={{0,4},{4,0},{8,12},{12,8},{16,20},{20,16},{24,28},{28,24},{1,5},{5... | collective-permute-start | bytes 786440 | tf_op jit(solution)/shard_map/ppermute | solution.py:417
  27.6 8.4 %collective-permute-start.2 = (bf16[4,128,256]{2,1,0:T(8,128)(2,1)S(1)}, bf16[4,128,256]{2,1,0:T(8,128)(2,1)S(1)}, u32[]{:S(2)}, u32[]{:S(2)}) collective-permute-start(bf16[4,128,256]{2,1,0:T(8,128)(2,1)S(1)} %fusion), channel_id=1, source_target_pairs={{0,8},{4,12},{8,0},{12,4},{16,24},{20,28},{24,16},{28,20},{1,9},{5... | collective-permute-start | bytes 786440 | tf_op jit(solution)/shard_map/ppermute | solution.py:417
  29.1 9.6 %copy-start.11 = (bf16[2048,1024]{1,0:T(8,128)(2,1)S(1)}, bf16[2048,1024]{1,0:T(8,128)(2,1)}, u32[]{:S(2)}) copy-start(bf16[2048,1024]{1,0:T(8,128)(2,1)} %param.15) | copy-start | bytes 12582916
  36.2 5.3 %collective-permute-start.3 = (bf16[4,128,128]{2,1,0:T(8,128)(2,1)S(1)}, bf16[4,128,128]{2,1,0:T(8,128)(2,1)S(1)}, u32[]{:S(2)}, u32[]{:S(2)}) collective-permute-start(bf16[4,128,128]{2,1,0:T(8,128)(2,1)S(1)} %add_convert_fusion.4), channel_id=1, source_target_pairs={{0,16},{4,20},{8,24},{12,28},{16,0},{20,4},{24,8},{28,12},{1,17},{... | collective-permute-start | bytes 393224 | tf_op jit(solution)/shard_map/ppermute | solution.py:417
  38.7 4.4 %copy-start.1 = (bf16[1024,2048]{1,0:T(8,128)(2,1)S(1)}, bf16[1024,2048]{1,0:T(8,128)(2,1)}, u32[]{:S(2)}) copy-start(bf16[1024,2048]{1,0:T(8,128)(2,1)} %weight_hbm.1) | copy-start | bytes 12582916
  41.7 1.4 %collective-permute-start.4 = (bf16[4,128,128]{2,1,0:T(8,128)(2,1)S(1)}, bf16[4,128,128]{2,1,0:T(8,128)(2,1)S(1)}, u32[]{:S(2)}, u32[]{:S(2)}) collective-permute-start(bf16[4,128,128]{2,1,0:T(8,128)(2,1)S(1)} %fusion.3), channel_id=1, source_target_pairs={{0,4},{4,0},{8,12},{12,8},{16,20},{20,16},{24,28},{28,24},{1,5},{5... | collective-permute-start | bytes 393224 | tf_op jit(solution)/shard_map/ppermute | solution.py:417
  46.2 7.4 %collective-permute-start.5 = (bf16[128,768]{1,0:T(8,128)(2,1)S(1)}, bf16[128,768]{1,0:T(8,128)(2,1)S(1)}, u32[]{:S(2)}, u32[]{:S(2)}) collective-permute-start(bf16[128,768]{1,0:T(8,128)(2,1)S(1)} %get-tuple-element.41), channel_id=1, source_target_pairs={{0,1},{1,0},{2,3},{3,2},{4,5},{5,4},{6,7},{7,6},{8,9},{9,8},{10,11... | collective-permute-start | bytes 589832 | tf_op jit(solution)/shard_map/ppermute | solution.py:417
  51.2 14.9 %collective-permute-start.7 = (bf16[128,1280]{1,0:T(8,128)(2,1)S(1)}, bf16[128,1280]{1,0:T(8,128)(2,1)S(1)}, u32[]{:S(2)}, u32[]{:S(2)}) collective-permute-start(bf16[128,1280]{1,0:T(8,128)(2,1)S(1)} %slice.163), channel_id=1, source_target_pairs={{0,1},{1,0},{2,3},{3,2},{4,5},{5,4},{6,7},{7,6},{8,9},{9,8},{10,11... | collective-permute-start | bytes 983048 | tf_op jit(solution)/shard_map/ppermute | solution.py:417
  53.7 12.4 %collective-permute-start.8 = (bf16[128,768]{1,0:T(8,128)(2,1)S(1)}, bf16[128,768]{1,0:T(8,128)(2,1)S(1)}, u32[]{:S(2)}, u32[]{:S(2)}) collective-permute-start(bf16[128,768]{1,0:T(8,128)(2,1)S(1)} %add_convert_fusion.3), channel_id=1, source_target_pairs={{0,2},{1,3},{2,0},{3,1},{4,6},{5,7},{6,4},{7,5},{8,10},{9,11},{10,... | collective-permute-start | bytes 589832 | tf_op jit(solution)/shard_map/ppermute | solution.py:417
  60.3 22.9 %collective-permute-start.6 = (bf16[128,2048]{1,0:T(8,128)(2,1)S(1)}, bf16[128,2048]{1,0:T(8,128)(2,1)S(1)}, u32[]{:S(2)}, u32[]{:S(2)}) collective-permute-start(bf16[128,2048]{1,0:T(8,128)(2,1)S(1)} %slice.117), channel_id=1, source_target_pairs={{0,1},{1,0},{2,3},{3,2},{4,5},{5,4},{6,7},{7,6},{8,9},{9,8},{10,11... | collective-permute-start | bytes 1572872 | tf_op jit(solution)/shard_map/ppermute | solution.py:417
  66.1 16.2 %collective-permute-start.9 = (bf16[128,1280]{1,0:T(8,128)(2,1)S(1)}, bf16[128,1280]{1,0:T(8,128)(2,1)S(1)}, u32[]{:S(2)}, u32[]{:S(2)}) collective-permute-start(bf16[128,1280]{1,0:T(8,128)(2,1)S(1)} %add_convert_fusion.1), channel_id=1, source_target_pairs={{0,2},{1,3},{2,0},{3,1},{4,6},{5,7},{6,4},{7,5},{8,10},{9,11},{10,... | collective-permute-start | bytes 983048 | tf_op jit(solution)/shard_map/ppermute | solution.py:417

commit v6 on v5

--- a/solution.py
+++ b/solution.py
@@ -68,10 +68,10 @@
 def cumulated(decay):
     row_ids, col_ids = grid_ids()
     lower = jnp.where(row_ids >= col_ids, 1.0, 0.0)
-    dims = (((1,), (1,)), ((), ()))
-    as_rows = lax.dot_general(decay, lower, dims, precision=EXACT, preferred_element_type=F32)
-    as_cols = lax.dot_general(lower, decay, dims, precision=EXACT, preferred_element_type=F32)
-    return as_rows, as_cols
+    as_rows = lax.dot_general(
+        decay, lower, (((1,), (1,)), ((), ())), precision=EXACT, preferred_element_type=F32
+    )
+    return as_rows, as_rows.T
 
 
 def head_rows(ref, ratio, chunks, group=1, member=0):
@@ -160,15 +160,7 @@
     writes = []
     for member in range(group):
         decays.append(cumulated(head_rows(decay_ref, ratio, chunks, group, member)))
-        writes.append(
-            lax.dot_general(
-                eye,
-                head_rows(write_ref, ratio, chunks, group, member),
-                (((1,), (1,)), ((), ())),
-                precision=EXACT,
-                preferred_element_type=F32,
-            )
-        )
+        writes.append(head_rows(write_ref, ratio, chunks, group, member).T)
     keys = {}
     flipped = {}
     values = []
@@ -228,13 +220,12 @@
     for chunk in range(chunks):
         for place, state in enumerate(states):
             product, end = maps[place, chunk]
-            linear = eye * end - product[:, :HD]
-            added = product[:, HD:]
+            removed, added = product[:, :HD], product[:, HD:]
             if state is None:
-                states[place] = jnp.concatenate([linear, added], axis=1)
+                states[place] = jnp.concatenate([eye * end - removed, added], axis=1)
             else:
                 starts_out[place, chunk - 1] = state.astype(BF)
-                moved = mm(linear, state)
+                moved = end * state - mm(removed, state)
                 states[place] = jnp.concatenate([moved[:, :HD], moved[:, HD:] + added], axis=1)
     for place, state in enumerate(states):
         map_out[place] = state.astype(BF)
@@ -556,7 +547,7 @@
     ratio = heads // key_heads
     chunks = rows // CHUNK
     tails = jnp.concatenate(
-        [proj_key[-RIM:], proj_value[-RIM:], proj_query[-RIM:]], axis=1
+        [proj_value[-RIM:], proj_key[-RIM:], proj_query[-RIM:]], axis=1
     )
     count = lax.axis_size("ctx")
     rims = lax.ppermute(tails, "ctx", [(at, (at + 1) % count) for at in range(count)])
@@ -578,8 +569,8 @@
             SCALAR,
             cols(rows, HD),
             cols(rows, ratio * HD),
-            cols(RIM, HD),
-            cols(RIM, ratio * HD, key_width),
+            cols(RIM, HD, heads * HD),
+            cols(RIM, ratio * HD),
             cols(taps_len, HD),
             cols(taps_len, ratio * HD),
             gate_spec,

time: 84.5 us -> 84.8 us (level)
  transfers between devices with their start and end apart: 10 -> 10, of which waited for: 9 -> 8; matrix products, arithmetic and copies ran while one was open for 7% -> 7% of each run, Pallas kernels for 13% -> 13%
where the time goes in v6:
time: 84.8 us; the launch traced here: 84.5 us
  waiting for transfers between devices  27.1 us (32%)
  Pallas kernels  26.7 us (31%)
  starting transfers between devices  14.3 us (17%)
  matrix products  12.8 us (15%)
  local copies, waits for them, and re-layouts  1.83 us (2%)
  other arithmetic  1.43 us (2%)
    ppermute x9, waiting for transfers between devices, exchanged(): lax.ppermute(value, axis, [(source, source ^ bit) for source in range(cou...  22.6 us
    ppermute x9, starting transfers between devices, exchanged(): lax.ppermute(value, axis, [(source, source ^ bit) for source in range(cou...  13.6 us
    pallas_call x1, Pallas kernels, shards(): pl.pallas_call(functools.partial(local_kernel, group, ratio, chunks), gri...  12.2 us
    dot_general x4, matrix products, project(): return jnp.dot(tokens, weights, preferred_element_type=F32).astype(BF)  9.06 us
    pallas_call x1, Pallas kernels, shards(): pl.pallas_call(functools.partial(output_kernel, group, ratio, chunks), gr...  6.85 us
    pallas_call x2, Pallas kernels, normed_rows(): pl.pallas_call(functools.partial(norm_kernel, heads), grid_spec=pltpu.Pre...  4.54 us
    ppermute x1, waiting for transfers between devices, shards(): lax.ppermute(tails, 'ctx', [(at, (at + 1) % count) for at in range(count)])  4.48 us
    pallas_call x1, Pallas kernels, far_rows(): pl.pallas_call(functools.partial(far_kernel, heads), grid_spec=pltpu.Pref...  3.06 us
  transfers between devices with their start and end apart: 10, of which 8 were waited for; matrix products, arithmetic and copies ran while one was open for 7% of the time, Pallas kernels for 13%

profile of v6, /device:TPU:0, one launch (start us, length us, event | category | flops | bytes accessed | tf_op | source)
XLA Modules:
  0.0 84.5 jit_solution(13271448669775373917)
XLA Ops:
  0.0 1.6 %copy-done = bf16[512,2048]{1,0:T(8,128)(2,1)S(1)} copy-done((bf16[512,2048]{1,0:T(8,128)(2,1)S(1)}, bf16[512,2048]{1,0:T(8,128)(2,1)}, u32[]{:S(2)}) %copy-start) | copy-done | bytes 2097176
  1.6 3.1 %convolution_convert_fusion.5.keys_ref = bf16[512,512]{1,0:T(8,128)(2,1)S(1)} fusion(bf16[512,2048]{1,0:T(8,128)(2,1)S(1)} %copy-done, bf16[2048,512]{1,0:T(8,128)(2,1)} %param.13), kind=kOutput, calls=%fused_computation.5 | convolution fusion | flops 1074003968 | bytes 4718592 | tf_op jit(solution)/shard_map/dot_general | solution.py:538
  4.7 2.4 %convolution_convert_fusion.3.values_ref = bf16[512,1024]{1,0:T(8,128)(2,1)S(1)} fusion(bf16[512,2048]{1,0:T(8,128)(2,1)S(1)} %copy-done, bf16[2048,1024]{1,0:T(8,128)(2,1)S(1)} %copy-done.10), kind=kOutput, calls=%fused_computation.3 | convolution fusion | flops 2148007936 | bytes 7340032 | tf_op jit(solution)/shard_map/dot_general | solution.py:538
  7.2 1.2 %convolution_convert_fusion.4.query_ref = bf16[512,512]{1,0:T(8,128)(2,1)S(1)} fusion(bf16[512,2048]{1,0:T(8,128)(2,1)S(1)} %copy-done, bf16[2048,512]{1,0:T(8,128)(2,1)S(1)} %copy-done.12), kind=kOutput, calls=%fused_computation.4 | convolution fusion | flops 1074003968 | bytes 4718592 | tf_op jit(solution)/shard_map/dot_general | solution.py:538
  8.5 0.7 collective-permute-start
  9.2 4.5 %collective-permute-done.rims_k_ref.rims_v_ref.rims_ref = bf16[8,2048]{1,0:T(8,128)(2,1)S(1)} collective-permute-done((bf16[8,2048]{1,0:T(8,128)(2,1)S(1)}, bf16[8,2048]{1,0:T(8,128)(2,1)S(1)}, u32[]{:S(2)}, u32[]{:S(2)}) %collective-permute-start) | collective-permute-done | bytes 32800 | tf_op jit(solution)/shard_map/ppermute | solution.py:553
  13.7 12.2 %local.1 = (bf16[512,512]{1,0:T(8,128)(2,1)}, bf16[8,512,256]{2,1,0:T(8,128)(2,1)}, bf16[8,3,128,256]{3,2,1,0:T(8,128)(2,1)}, bf16[8,128,256]{2,1,0:T(8,128)(2,1)S(1)}) custom-call(s32[1]{0:T(128)} %bitcast.5.at_ref, bf16[512,512]{1,0:T(8,128)(2,1)} %copy-done.8, bf16[512,1024]{1,0:T(8,128)(2,1)} %copy-done.9, ...), custom_call_target="tpu_custom_call" | custom-call | flops 2147483648 | bytes 6291456 | tf_op jit(solution)/shard_map/local/pallas_call | solution.py:565
  26.1 1.5 %collective-permute-done.1 = bf16[4,128,256]{2,1,0:T(8,128)(2,1)S(1)} collective-permute-done((bf16[4,128,256]{2,1,0:T(8,128)(2,1)S(1)}, bf16[4,128,256]{2,1,0:T(8,128)(2,1)S(1)}, u32[]{:S(2)}, u32[]{:S(2)}) %collective-permute-start.1) | collective-permute-done | bytes 262176 | tf_op jit(solution)/shard_map/ppermute | solution.py:408
  27.6 0.2 fusion
  27.9 1.4 %collective-permute-start.2 = (bf16[4,128,256]{2,1,0:T(8,128)(2,1)S(1)}, bf16[4,128,256]{2,1,0:T(8,128)(2,1)S(1)}, u32[]{:S(2)}, u32[]{:S(2)}) collective-permute-start(bf16[4,128,256]{2,1,0:T(8,128)(2,1)S(1)} %fusion), channel_id=1, source_target_pairs={{0,8},{4,12},{8,0},{12,4},{16,24},{20,28},{24,16},{28,20},{1,9},{5... | collective-permute-start | bytes 786440 | tf_op jit(solution)/shard_map/ppermute | solution.py:408
  29.4 6.8 %outputs.1.parts_ref = bf16[8,512,256]{2,1,0:T(8,128)(2,1)} custom-call(s32[1]{0:T(128)} %bitcast.5.at_ref, bf16[512,512]{1,0:T(8,128)(2,1)} %copy-done.7, bf16[8,2048]{1,0:T(8,128)(2,1)S(1)} %collective-permute-done.rims_k_ref.rims_v_ref.rims_ref, f32[4,512]{1,0:T(4,128)S(1)} %copy-done.3, bf16[512,512]{1,0:T(8,128)(2,1)} %get-tuple-element.29.keys_ref, ...), custom_call_target="tpu_custom_call" | custom-call | flops 1073741824 | bytes 6291456 | tf_op jit(solution)/shard_map/outputs/pallas_call | solution.py:599
  36.3 0.2 add_convert_fusion.4
  36.5 2.3 %collective-permute-start.3 = (bf16[4,128,128]{2,1,0:T(8,128)(2,1)S(1)}, bf16[4,128,128]{2,1,0:T(8,128)(2,1)S(1)}, u32[]{:S(2)}, u32[]{:S(2)}) collective-permute-start(bf16[4,128,128]{2,1,0:T(8,128)(2,1)S(1)} %add_convert_fusion.4), channel_id=1, source_target_pairs={{0,16},{4,20},{8,24},{12,28},{16,0},{20,4},{24,8},{28,12},{1,17},{... | collective-permute-start | bytes 393224 | tf_op jit(solution)/shard_map/ppermute | solution.py:408
  39.0 2.4 %convolution_convert_fusion.2.gate_ref = bf16[512,1024]{1,0:T(8,128)(2,1)S(1)} fusion(bf16[512,2048]{1,0:T(8,128)(2,1)S(1)} %copy-done, bf16[2048,1024]{1,0:T(8,128)(2,1)S(1)} %copy-done.11), kind=kOutput, calls=%fused_computation.2 | convolution fusion | flops 2148007936 | bytes 7340032 | tf_op jit(solution)/shard_map/dot_general | solution.py:538
  41.4 0.2 broadcast_select_fusion.1
  41.6 0.2 collective-permute-done.3
  42.3 1.2 %collective-permute-done.4.got_ref = bf16[4,128,128]{2,1,0:T(8,128)(2,1)S(1)} collective-permute-done((bf16[4,128,128]{2,1,0:T(8,128)(2,1)S(1)}, bf16[4,128,128]{2,1,0:T(8,128)(2,1)S(1)}, u32[]{:S(2)}, u32[]{:S(2)}) %collective-permute-start.4) | collective-permute-done | bytes 131104 | tf_op jit(solution)/shard_map/ppermute | solution.py:408
  43.4 3.1 %far.1 = (bf16[128,768]{1,0:T(8,128)(2,1)S(1)}, bf16[128,1024]{1,0:T(8,128)(2,1)S(1)}) custom-call(s32[5]{0:T(128)S(1)} %stack.23.plan_ref, bf16[8,512,256]{2,1,0:T(8,128)(2,1)} %outputs.1.parts_ref, bf16[4,128,128]{2,1,0:T(8,128)(2,1)S(1)} %fusion.2.kept_ref, bf16[4,128,128]{2,1,0:T(8,128)(2,1)S(1)} %collective-permute-done.4.got_ref, ...), custom_call_target="tpu_custom_call" | custom-call | tf_op jit(solution)/shard_map/far/pallas_call | solution.py:352
  46.5 2.1 %collective-permute-start.5 = (bf16[128,768]{1,0:T(8,128)(2,1)S(1)}, bf16[128,768]{1,0:T(8,128)(2,1)S(1)}, u32[]{:S(2)}, u32[]{:S(2)}) collective-permute-start(bf16[128,768]{1,0:T(8,128)(2,1)S(1)} %get-tuple-element.41), channel_id=1, source_target_pairs={{0,1},{1,0},{2,3},{3,2},{4,5},{5,4},{6,7},{7,6},{8,9},{9,8},{10,11... | collective-permute-start | bytes 589832 | tf_op jit(solution)/shard_map/ppermute | solution.py:408
  48.6 2.0 %normed.2 = bf16[128,1024]{1,0:T(8,128)(2,1)S(1)} custom-call(s32[5]{0:T(128)S(1)} %stack.23.plan_ref, bf16[8,512,256]{2,1,0:T(8,128)(2,1)} %outputs.1.parts_ref, bf16[4,128,128]{2,1,0:T(8,128)(2,1)S(1)} %fusion.2.kept_ref, bf16[4,128,128]{2,1,0:T(8,128)(2,1)S(1)} %collective-permute-done.4.got_ref, bf16[512,1024]{1,0:T(8,128)(2,1)S(1)} %convolution_convert_fusion.2.gate_ref), custom_call_target="tpu_custom_call" | custom-call | flops 33554432 | bytes 1048576 | tf_op jit(solution)/shard_map/normed/pallas_call | solution.py:384
  50.6 0.7 fusion.14
  51.5 0.7 convolution_convert_fusion.1
  52.2 1.6 %collective-permute-done.5 = bf16[128,768]{1,0:T(8,128)(2,1)S(1)} collective-permute-done((bf16[128,768]{1,0:T(8,128)(2,1)S(1)}, bf16[128,768]{1,0:T(8,128)(2,1)S(1)}, u32[]{:S(2)}, u32[]{:S(2)}) %collective-permute-start.5) | collective-permute-done | bytes 196640 | tf_op jit(solution)/shard_map/ppermute | solution.py:408
  53.9 2.8 %collective-permute-start.8 = (bf16[128,768]{1,0:T(8,128)(2,1)S(1)}, bf16[128,768]{1,0:T(8,128)(2,1)S(1)}, u32[]{:S(2)}, u32[]{:S(2)}) collective-permute-start(bf16[128,768]{1,0:T(8,128)(2,1)S(1)} %add_convert_fusion.3), channel_id=1, source_target_pairs={{0,2},{1,3},{2,0},{3,1},{4,6},{5,7},{6,4},{7,5},{8,10},{9,11},{10,... | collective-permute-start | bytes 589832 | tf_op jit(solution)/shard_map/ppermute | solution.py:408
  56.7 2.5 %normed.3 = bf16[256,1024]{1,0:T(8,128)(2,1)S(1)} custom-call(s32[5]{0:T(128)S(1)} %stack.23.plan_ref, bf16[8,512,256]{2,1,0:T(8,128)(2,1)} %outputs.1.parts_ref, bf16[4,128,128]{2,1,0:T(8,128)(2,1)S(1)} %fusion.2.kept_ref, bf16[4,128,128]{2,1,0:T(8,128)(2,1)S(1)} %collective-permute-done.4.got_ref, bf16[512,1024]{1,0:T(8,128)(2,1)S(1)} %convolution_convert_fusion.2.gate_ref), custom_call_target="tpu_custom_call" | custom-call | flops 67108864 | bytes 2097152 | tf_op jit(solution)/shard_map/normed/pallas_call | solution.py:384
  59.2 1.3 %convolution_convert_fusion = bf16[256,2048]{1,0:T(8,128)(2,1)S(1)} fusion(bf16[256,1024]{1,0:T(8,128)(2,1)S(1)} %normed.3, bf16[1024,2048]{1,0:T(8,128)(2,1)S(1)} %copy-done.1), kind=kOutput, calls=%fused_computation | convolution fusion | flops 1074266112 | bytes 5767168 | tf_op jit(solution)/shard_map/dot_general | solution.py:493
  60.6 2.4 %collective-permute-start.6 = (bf16[128,2048]{1,0:T(8,128)(2,1)S(1)}, bf16[128,2048]{1,0:T(8,128)(2,1)S(1)}, u32[]{:S(2)}, u32[]{:S(2)}) collective-permute-start(bf16[128,2048]{1,0:T(8,128)(2,1)S(1)} %slice.117), channel_id=1, source_target_pairs={{0,1},{1,0},{2,3},{3,2},{4,5},{5,4},{6,7},{7,6},{8,9},{9,8},{10,11... | collective-permute-start | bytes 1572872 | tf_op jit(solution)/shard_map/ppermute | solution.py:408
  63.0 3.3 %collective-permute-done.7 = bf16[128,1280]{1,0:T(8,128)(2,1)S(1)} collective-permute-done((bf16[128,1280]{1,0:T(8,128)(2,1)S(1)}, bf16[128,1280]{1,0:T(8,128)(2,1)S(1)}, u32[]{:S(2)}, u32[]{:S(2)}) %collective-permute-start.7) | collective-permute-done | bytes 327712 | tf_op jit(solution)/shard_map/ppermute | solution.py:408
  66.4 2.3 %collective-permute-start.9 = (bf16[128,1280]{1,0:T(8,128)(2,1)S(1)}, bf16[128,1280]{1,0:T(8,128)(2,1)S(1)}, u32[]{:S(2)}, u32[]{:S(2)}) collective-permute-start(bf16[128,1280]{1,0:T(8,128)(2,1)S(1)} %add_convert_fusion.1), channel_id=1, source_target_pairs={{0,2},{1,3},{2,0},{3,1},{4,6},{5,7},{6,4},{7,5},{8,10},{9,11},{10,... | collective-permute-start | bytes 983048 | tf_op jit(solution)/shard_map/ppermute | solution.py:408
  68.7 13.9 %collective-permute-done.9 = bf16[128,1280]{1,0:T(8,128)(2,1)S(1)} collective-permute-done((bf16[128,1280]{1,0:T(8,128)(2,1)S(1)}, bf16[128,1280]{1,0:T(8,128)(2,1)S(1)}, u32[]{:S(2)}, u32[]{:S(2)}) %collective-permute-start.9) | collective-permute-done | bytes 327712 | tf_op jit(solution)/shard_map/ppermute | solution.py:408
  82.6 0.8 collective-permute-done.6
  83.7 0.8 %pad_maximum_fusion = bf16[128,2048]{1,0:T(8,128)(2,1)} fusion(bf16[128,1280]{1,0:T(8,128)(2,1)S(1)} %add_convert_fusion, bf16[128,768]{1,0:T(8,128)(2,1)S(1)} %add_convert_fusion.2), kind=kLoop, calls=%fused_computation.17 | loop fusion | flops 1048576 | bytes 1048576 | tf_op jit(solution)/shard_map/concatenate | solution.py:512
  (52 shorter events, 1.4 us)
Async XLA Ops:
  0.0 1.6 %copy-start = (bf16[512,2048]{1,0:T(8,128)(2,1)S(1)}, bf16[512,2048]{1,0:T(8,128)(2,1)}, u32[]{:S(2)}) copy-start(bf16[512,2048]{1,0:T(8,128)(2,1)} %param.11) | copy-start | bytes 6291460
  0.0 4.7 %copy-start.10 = (bf16[2048,1024]{1,0:T(8,128)(2,1)S(1)}, bf16[2048,1024]{1,0:T(8,128)(2,1)}, u32[]{:S(2)}) copy-start(bf16[2048,1024]{1,0:T(8,128)(2,1)} %param.14) | copy-start | bytes 12582916
  4.7 2.4 %copy-start.8 = (bf16[512,512]{1,0:T(8,128)(2,1)}, bf16[512,512]{1,0:T(8,128)(2,1)S(1)}, u32[]{:S(2)}) copy-start(bf16[512,512]{1,0:T(8,128)(2,1)S(1)} %convolution_convert_fusion.5.keys_ref) | copy-start | bytes 1572868
  4.7 2.4 %copy-start.12 = (bf16[2048,512]{1,0:T(8,128)(2,1)S(1)}, bf16[2048,512]{1,0:T(8,128)(2,1)}, u32[]{:S(2)}) copy-start(bf16[2048,512]{1,0:T(8,128)(2,1)} %param.12) | copy-start | bytes 6291460
  7.1 1.3 %copy-start.9 = (bf16[512,1024]{1,0:T(8,128)(2,1)}, bf16[512,1024]{1,0:T(8,128)(2,1)S(1)}, u32[]{:S(2)}) copy-start(bf16[512,1024]{1,0:T(8,128)(2,1)S(1)} %convolution_convert_fusion.3.values_ref) | copy-start | bytes 3145732
  7.1 1.3 %slice-start = ((bf16[512,512]{1,0:T(8,128)(2,1)}), bf16[8,512]{1,0:T(8,128)(2,1)S(1)}, s32[]{:S(2)}) async-start(bf16[512,512]{1,0:T(8,128)(2,1)} %copy-done.8), calls=%async_computation | async-start | bytes 16384 | tf_op jit(solution)/shard_map/slice | solution.py:550
  7.1 6.5 %copy-start.2 = (f32[8,512]{1,0:T(8,128)S(1)}, f32[8,512]{1,0:T(8,128)}, u32[]{:S(2)}) copy-start(f32[8,512]{1,0:T(8,128)} %decay_ref.3) | copy-start | bytes 49156
  7.2 6.5 %copy-start.4 = (f32[4,1024]{1,0:T(4,128)S(1)}, f32[4,1024]{1,0:T(4,128)}, u32[]{:S(2)}) copy-start(f32[4,1024]{1,0:T(4,128)} %taps_v_ref.1) | copy-start | bytes 49156
  7.2 6.5 %copy-start.5 = (f32[8,512]{1,0:T(8,128)S(1)}, f32[8,512]{1,0:T(8,128)}, u32[]{:S(2)}) copy-start(f32[8,512]{1,0:T(8,128)} %write_ref.1) | copy-start | bytes 49156
  7.2 6.5 %copy-start.6 = (f32[4,512]{1,0:T(4,128)S(1)}, f32[4,512]{1,0:T(4,128)}, u32[]{:S(2)}) copy-start(f32[4,512]{1,0:T(4,128)} %taps_k_ref.1) | copy-start | bytes 24580
  8.5 17.5 %copy-start.7 = (bf16[512,512]{1,0:T(8,128)(2,1)}, bf16[512,512]{1,0:T(8,128)(2,1)S(1)}, u32[]{:S(2)}) copy-start(bf16[512,512]{1,0:T(8,128)(2,1)S(1)} %convolution_convert_fusion.4.query_ref) | copy-start | bytes 1572868
  8.5 5.2 %collective-permute-start = (bf16[8,2048]{1,0:T(8,128)(2,1)S(1)}, bf16[8,2048]{1,0:T(8,128)(2,1)S(1)}, u32[]{:S(2)}, u32[]{:S(2)}) collective-permute-start(bf16[8,2048]{1,0:T(8,128)(2,1)S(1)} %pad_maximum_fusion.3), channel_id=1, source_target_pairs={{0,4},{4,8},{8,12},{12,16},{16,20},{20,24},{24,28},{28,0},{1,5},{5... | collective-permute-start | bytes 98312 | tf_op jit(solution)/shard_map/ppermute | solution.py:553
  25.9 3.4 %copy-start.3 = (f32[4,512]{1,0:T(4,128)S(1)}, f32[4,512]{1,0:T(4,128)}, u32[]{:S(2)}) copy-start(f32[4,512]{1,0:T(4,128)} %taps_ref.1) | copy-start | bytes 24580
  26.0 1.6 %collective-permute-start.1 = (bf16[4,128,256]{2,1,0:T(8,128)(2,1)S(1)}, bf16[4,128,256]{2,1,0:T(8,128)(2,1)S(1)}, u32[]{:S(2)}, u32[]{:S(2)}) collective-permute-start(bf16[4,128,256]{2,1,0:T(8,128)(2,1)S(1)} %broadcast_select_fusion.5), channel_id=1, source_target_pairs={{0,4},{4,0},{8,12},{12,8},{16,20},{20,16},{24,28},{28,24},{1,5},{5... | collective-permute-start | bytes 786440 | tf_op jit(solution)/shard_map/ppermute | solution.py:408
  27.9 8.4 %collective-permute-start.2 = (bf16[4,128,256]{2,1,0:T(8,128)(2,1)S(1)}, bf16[4,128,256]{2,1,0:T(8,128)(2,1)S(1)}, u32[]{:S(2)}, u32[]{:S(2)}) collective-permute-start(bf16[4,128,256]{2,1,0:T(8,128)(2,1)S(1)} %fusion), channel_id=1, source_target_pairs={{0,8},{4,12},{8,0},{12,4},{16,24},{20,28},{24,16},{28,20},{1,9},{5... | collective-permute-start | bytes 786440 | tf_op jit(solution)/shard_map/ppermute | solution.py:408
  29.4 9.6 %copy-start.11 = (bf16[2048,1024]{1,0:T(8,128)(2,1)S(1)}, bf16[2048,1024]{1,0:T(8,128)(2,1)}, u32[]{:S(2)}) copy-start(bf16[2048,1024]{1,0:T(8,128)(2,1)} %param.15) | copy-start | bytes 12582916
  36.5 5.3 %collective-permute-start.3 = (bf16[4,128,128]{2,1,0:T(8,128)(2,1)S(1)}, bf16[4,128,128]{2,1,0:T(8,128)(2,1)S(1)}, u32[]{:S(2)}, u32[]{:S(2)}) collective-permute-start(bf16[4,128,128]{2,1,0:T(8,128)(2,1)S(1)} %add_convert_fusion.4), channel_id=1, source_target_pairs={{0,16},{4,20},{8,24},{12,28},{16,0},{20,4},{24,8},{28,12},{1,17},{... | collective-permute-start | bytes 393224 | tf_op jit(solution)/shard_map/ppermute | solution.py:408
  39.0 4.4 %copy-start.1 = (bf16[1024,2048]{1,0:T(8,128)(2,1)S(1)}, bf16[1024,2048]{1,0:T(8,128)(2,1)}, u32[]{:S(2)}) copy-start(bf16[1024,2048]{1,0:T(8,128)(2,1)} %weight_hbm.1) | copy-start | bytes 12582916
  42.0 1.4 %collective-permute-start.4 = (bf16[4,128,128]{2,1,0:T(8,128)(2,1)S(1)}, bf16[4,128,128]{2,1,0:T(8,128)(2,1)S(1)}, u32[]{:S(2)}, u32[]{:S(2)}) collective-permute-start(bf16[4,128,128]{2,1,0:T(8,128)(2,1)S(1)} %fusion.3), channel_id=1, source_target_pairs={{0,4},{4,0},{8,12},{12,8},{16,20},{20,16},{24,28},{28,24},{1,5},{5... | collective-permute-start | bytes 393224 | tf_op jit(solution)/shard_map/ppermute | solution.py:408
  46.5 7.4 %collective-permute-start.5 = (bf16[128,768]{1,0:T(8,128)(2,1)S(1)}, bf16[128,768]{1,0:T(8,128)(2,1)S(1)}, u32[]{:S(2)}, u32[]{:S(2)}) collective-permute-start(bf16[128,768]{1,0:T(8,128)(2,1)S(1)} %get-tuple-element.41), channel_id=1, source_target_pairs={{0,1},{1,0},{2,3},{3,2},{4,5},{5,4},{6,7},{7,6},{8,9},{9,8},{10,11... | collective-permute-start | bytes 589832 | tf_op jit(solution)/shard_map/ppermute | solution.py:408
  51.4 14.9 %collective-permute-start.7 = (bf16[128,1280]{1,0:T(8,128)(2,1)S(1)}, bf16[128,1280]{1,0:T(8,128)(2,1)S(1)}, u32[]{:S(2)}, u32[]{:S(2)}) collective-permute-start(bf16[128,1280]{1,0:T(8,128)(2,1)S(1)} %slice.163), channel_id=1, source_target_pairs={{0,1},{1,0},{2,3},{3,2},{4,5},{5,4},{6,7},{7,6},{8,9},{9,8},{10,11... | collective-permute-start | bytes 983048 | tf_op jit(solution)/shard_map/ppermute | solution.py:408
  53.9 12.4 %collective-permute-start.8 = (bf16[128,768]{1,0:T(8,128)(2,1)S(1)}, bf16[128,768]{1,0:T(8,128)(2,1)S(1)}, u32[]{:S(2)}, u32[]{:S(2)}) collective-permute-start(bf16[128,768]{1,0:T(8,128)(2,1)S(1)} %add_convert_fusion.3), channel_id=1, source_target_pairs={{0,2},{1,3},{2,0},{3,1},{4,6},{5,7},{6,4},{7,5},{8,10},{9,11},{10,... | collective-permute-start | bytes 589832 | tf_op jit(solution)/shard_map/ppermute | solution.py:408
  60.6 22.9 %collective-permute-start.6 = (bf16[128,2048]{1,0:T(8,128)(2,1)S(1)}, bf16[128,2048]{1,0:T(8,128)(2,1)S(1)}, u32[]{:S(2)}, u32[]{:S(2)}) collective-permute-start(bf16[128,2048]{1,0:T(8,128)(2,1)S(1)} %slice.117), channel_id=1, source_target_pairs={{0,1},{1,0},{2,3},{3,2},{4,5},{5,4},{6,7},{7,6},{8,9},{9,8},{10,11... | collective-permute-start | bytes 1572872 | tf_op jit(solution)/shard_map/ppermute | solution.py:408
  66.4 16.2 %collective-permute-start.9 = (bf16[128,1280]{1,0:T(8,128)(2,1)S(1)}, bf16[128,1280]{1,0:T(8,128)(2,1)S(1)}, u32[]{:S(2)}, u32[]{:S(2)}) collective-permute-start(bf16[128,1280]{1,0:T(8,128)(2,1)S(1)} %add_convert_fusion.1), channel_id=1, source_target_pairs={{0,2},{1,3},{2,0},{3,1},{4,6},{5,7},{6,4},{7,5},{8,10},{9,11},{10,... | collective-permute-start | bytes 983048 | tf_op jit(solution)/shard_map/ppermute | solution.py:408

commit v7 on v6

--- a/solution.py
+++ b/solution.py
@@ -313,26 +313,33 @@
 def far_kernel(
     heads,
     plan_ref,
-    parts_ref,
+    parts_hbm,
     kept_ref,
     got_ref,
     gate_ref,
     weight_hbm,
     out_ref,
     normed_ref,
+    parts,
     weight,
     sems,
 ):
     pieces, depth, width = weight.shape
+    length = parts.shape[1]
+    rows = pl.ds(pl.multiple_of(plan_ref[1] * length, length), length)
+    inward = pltpu.make_async_copy(parts_hbm.at[:, rows], parts, sems.at[pieces])
     copies = [
         pltpu.make_async_copy(
             weight_hbm.at[pl.ds(at * depth, depth), pl.ds(0, width)], weight.at[at], sems.at[at]
         )
         for at in range(pieces)
     ]
-    for copy in copies:
+    for copy in [inward] + copies:
         copy.start()
-    normed_heads(heads, plan_ref[0] != 0, parts_ref, kept_ref, got_ref, gate_ref, normed_ref)
+    inward.wait()
+    normed_heads(
+        heads, plan_ref[0] != 0, parts, kept_ref, got_ref, gate_ref.at[rows], normed_ref
+    )
     total = None
     for at, copy in enumerate(copies):
         copy.wait()
@@ -349,30 +356,19 @@
     heads = parts.shape[0]
     features = w_out.shape[0]
     pieces = 4
+    hbm = pl.BlockSpec(memory_space=pltpu.HBM)
     return pl.pallas_call(
         functools.partial(far_kernel, heads),
-        grid_spec=pltpu.PrefetchScalarGridSpec(
-            num_scalar_prefetch=1,
-            grid=(1,),
-            in_specs=[
-                pl.BlockSpec((heads, length, 2 * HD), lambda c, plan: (0, plan[1], 0)),
-                WHOLE,
-                WHOLE,
-                pl.BlockSpec((length, heads * HD), lambda c, plan: (plan[1], 0)),
-                pl.BlockSpec(memory_space=pltpu.HBM),
-            ],
-            out_specs=[
-                pl.BlockSpec((length, width), lambda c, plan: (0, 0)),
-                pl.BlockSpec((length, features), lambda c, plan: (0, 0)),
-            ],
-            scratch_shapes=[
-                pltpu.VMEM((pieces, features // pieces, width), BF),
-                pltpu.SemaphoreType.DMA((pieces,)),
-            ],
-        ),
+        in_specs=[SCALAR, hbm, WHOLE, WHOLE, WHOLE, hbm],
+        out_specs=[WHOLE, WHOLE],
         out_shape=[
             jax.ShapeDtypeStruct((length, width), BF),
             jax.ShapeDtypeStruct((length, features), BF),
+        ],
+        scratch_shapes=[
+            pltpu.VMEM((heads, length, 2 * HD), BF),
+            pltpu.VMEM((pieces, features // pieces, width), BF),
+            pltpu.SemaphoreType.DMA((pieces + 1,)),
         ],
         compiler_params=pltpu.CompilerParams(vmem_limit_bytes=20 << 20),
         name="far",

time: 84.8 us -> 84.4 us (level)
  transfers between devices with their start and end apart: 10 -> 10, of which waited for: 8 -> 8; matrix products, arithmetic and copies ran while one was open for 7% -> 7% of each run, Pallas kernels for 13% -> 14%
where the time goes in v7:
time: 84.4 us; the launch traced here: 84.2 us
  waiting for transfers between devices  27.1 us (32%)
  Pallas kernels  26.3 us (31%)
  starting transfers between devices  14.3 us (17%)
  matrix products  12.8 us (15%)
  local copies, waits for them, and re-layouts  1.83 us (2%)
  other arithmetic  1.43 us (2%)
    ppermute x9, waiting for transfers between devices, exchanged(): lax.ppermute(value, axis, [(source, source ^ bit) for source in range(cou...  22.6 us
    ppermute x9, starting transfers between devices, exchanged(): lax.ppermute(value, axis, [(source, source ^ bit) for source in range(cou...  13.6 us
    pallas_call x1, Pallas kernels, shards(): pl.pallas_call(functools.partial(local_kernel, group, ratio, chunks), gri...  12.2 us
    dot_general x4, matrix products, project(): return jnp.dot(tokens, weights, preferred_element_type=F32).astype(BF)  9.06 us
    pallas_call x1, Pallas kernels, shards(): pl.pallas_call(functools.partial(output_kernel, group, ratio, chunks), gr...  6.85 us
    pallas_call x2, Pallas kernels, normed_rows(): pl.pallas_call(functools.partial(norm_kernel, heads), grid_spec=pltpu.Pre...  4.54 us
    ppermute x1, waiting for transfers between devices, shards(): lax.ppermute(tails, 'ctx', [(at, (at + 1) % count) for at in range(count)])  4.48 us
    dot_general x3, matrix products, mixed_rows(): return jnp.dot(normed, w_out, preferred_element_type=F32).astype(BF)  2.73 us
  transfers between devices with their start and end apart: 10, of which 8 were waited for; matrix products, arithmetic and copies ran while one was open for 7% of the time, Pallas kernels for 14%

profile of v7, /device:TPU:0, one launch (start us, length us, event | category | flops | bytes accessed | tf_op | source)
XLA Modules:
  0.0 84.2 jit_solution(13339965185366189165)
XLA Ops:
  0.0 1.6 %copy-done = bf16[512,2048]{1,0:T(8,128)(2,1)S(1)} copy-done((bf16[512,2048]{1,0:T(8,128)(2,1)S(1)}, bf16[512,2048]{1,0:T(8,128)(2,1)}, u32[]{:S(2)}) %copy-start) | copy-done | bytes 2097176
  1.6 3.1 %convolution_convert_fusion.5.keys_ref = bf16[512,512]{1,0:T(8,128)(2,1)S(1)} fusion(bf16[512,2048]{1,0:T(8,128)(2,1)S(1)} %copy-done, bf16[2048,512]{1,0:T(8,128)(2,1)} %param.13), kind=kOutput, calls=%fused_computation.5 | convolution fusion | flops 1074003968 | bytes 4718592 | tf_op jit(solution)/shard_map/dot_general | solution.py:534
  4.7 2.4 %convolution_convert_fusion.3.values_ref = bf16[512,1024]{1,0:T(8,128)(2,1)S(1)} fusion(bf16[512,2048]{1,0:T(8,128)(2,1)S(1)} %copy-done, bf16[2048,1024]{1,0:T(8,128)(2,1)S(1)} %copy-done.10), kind=kOutput, calls=%fused_computation.3 | convolution fusion | flops 2148007936 | bytes 7340032 | tf_op jit(solution)/shard_map/dot_general | solution.py:534
  7.2 1.2 %convolution_convert_fusion.4.query_ref = bf16[512,512]{1,0:T(8,128)(2,1)S(1)} fusion(bf16[512,2048]{1,0:T(8,128)(2,1)S(1)} %copy-done, bf16[2048,512]{1,0:T(8,128)(2,1)S(1)} %copy-done.12), kind=kOutput, calls=%fused_computation.4 | convolution fusion | flops 1074003968 | bytes 4718592 | tf_op jit(solution)/shard_map/dot_general | solution.py:534
  8.5 0.7 collective-permute-start
  9.2 4.5 %collective-permute-done.rims_k_ref.rims_v_ref.rims_ref = bf16[8,2048]{1,0:T(8,128)(2,1)S(1)} collective-permute-done((bf16[8,2048]{1,0:T(8,128)(2,1)S(1)}, bf16[8,2048]{1,0:T(8,128)(2,1)S(1)}, u32[]{:S(2)}, u32[]{:S(2)}) %collective-permute-start) | collective-permute-done | bytes 32800 | tf_op jit(solution)/shard_map/ppermute | solution.py:549
  13.7 12.2 %local.1 = (bf16[512,512]{1,0:T(8,128)(2,1)}, bf16[8,512,256]{2,1,0:T(8,128)(2,1)}, bf16[8,3,128,256]{3,2,1,0:T(8,128)(2,1)}, bf16[8,128,256]{2,1,0:T(8,128)(2,1)S(1)}) custom-call(s32[1]{0:T(128)} %bitcast.5.at_ref, bf16[512,512]{1,0:T(8,128)(2,1)} %copy-done.8, bf16[512,1024]{1,0:T(8,128)(2,1)} %copy-done.9, ...), custom_call_target="tpu_custom_call" | custom-call | flops 2147483648 | bytes 6291456 | tf_op jit(solution)/shard_map/local/pallas_call | solution.py:561
  26.1 1.5 %collective-permute-done.1 = bf16[4,128,256]{2,1,0:T(8,128)(2,1)S(1)} collective-permute-done((bf16[4,128,256]{2,1,0:T(8,128)(2,1)S(1)}, bf16[4,128,256]{2,1,0:T(8,128)(2,1)S(1)}, u32[]{:S(2)}, u32[]{:S(2)}) %collective-permute-start.1) | collective-permute-done | bytes 262176 | tf_op jit(solution)/shard_map/ppermute | solution.py:404
  27.6 0.2 fusion
  27.9 1.4 %collective-permute-start.2 = (bf16[4,128,256]{2,1,0:T(8,128)(2,1)S(1)}, bf16[4,128,256]{2,1,0:T(8,128)(2,1)S(1)}, u32[]{:S(2)}, u32[]{:S(2)}) collective-permute-start(bf16[4,128,256]{2,1,0:T(8,128)(2,1)S(1)} %fusion), channel_id=1, source_target_pairs={{0,8},{4,12},{8,0},{12,4},{16,24},{20,28},{24,16},{28,20},{1,9},{5... | collective-permute-start | bytes 786440 | tf_op jit(solution)/shard_map/ppermute | solution.py:404
  29.4 6.8 %outputs.1.parts_hbm.parts_ref = bf16[8,512,256]{2,1,0:T(8,128)(2,1)} custom-call(s32[1]{0:T(128)} %bitcast.5.at_ref, bf16[512,512]{1,0:T(8,128)(2,1)} %copy-done.7, bf16[8,2048]{1,0:T(8,128)(2,1)S(1)} %collective-permute-done.rims_k_ref.rims_v_ref.rims_ref, f32[4,512]{1,0:T(4,128)S(1)} %copy-done.3, bf16[512,512]{1,0:T(8,128)(2,1)} %get-tuple-element.29.keys_ref, ...), custom_call_target="tpu_custom_call" | custom-call | flops 1073741824 | bytes 6291456 | tf_op jit(solution)/shard_map/outputs/pallas_call | solution.py:595
  36.3 0.2 add_convert_fusion.4
  36.5 2.3 %collective-permute-start.3 = (bf16[4,128,128]{2,1,0:T(8,128)(2,1)S(1)}, bf16[4,128,128]{2,1,0:T(8,128)(2,1)S(1)}, u32[]{:S(2)}, u32[]{:S(2)}) collective-permute-start(bf16[4,128,128]{2,1,0:T(8,128)(2,1)S(1)} %add_convert_fusion.4), channel_id=1, source_target_pairs={{0,16},{4,20},{8,24},{12,28},{16,0},{20,4},{24,8},{28,12},{1,17},{... | collective-permute-start | bytes 393224 | tf_op jit(solution)/shard_map/ppermute | solution.py:404
  39.0 2.4 %convolution_convert_fusion.2.gate_ref = bf16[512,1024]{1,0:T(8,128)(2,1)S(1)} fusion(bf16[512,2048]{1,0:T(8,128)(2,1)S(1)} %copy-done, bf16[2048,1024]{1,0:T(8,128)(2,1)S(1)} %copy-done.11), kind=kOutput, calls=%fused_computation.2 | convolution fusion | flops 2148007936 | bytes 7340032 | tf_op jit(solution)/shard_map/dot_general | solution.py:534
  41.4 0.2 broadcast_select_fusion.1
  41.6 0.2 collective-permute-done.3
  42.3 1.2 %collective-permute-done.4.got_ref = bf16[4,128,128]{2,1,0:T(8,128)(2,1)S(1)} collective-permute-done((bf16[4,128,128]{2,1,0:T(8,128)(2,1)S(1)}, bf16[4,128,128]{2,1,0:T(8,128)(2,1)S(1)}, u32[]{:S(2)}, u32[]{:S(2)}) %collective-permute-start.4) | collective-permute-done | bytes 131104 | tf_op jit(solution)/shard_map/ppermute | solution.py:404
  43.4 2.7 %far.1 = (bf16[128,768]{1,0:T(8,128)(2,1)S(1)}, bf16[128,1024]{1,0:T(8,128)(2,1)S(1)}) custom-call(s32[5]{0:T(128)S(1)} %stack.23.plan_ref, bf16[8,512,256]{2,1,0:T(8,128)(2,1)} %outputs.1.parts_hbm.parts_ref, bf16[4,128,128]{2,1,0:T(8,128)(2,1)S(1)} %fusion.2.kept_ref, bf16[4,128,128]{2,1,0:T(8,128)(2,1)S(1)} %collective-permute-done.4.got_ref, ...), custom_call_target="tpu_custom_call" | custom-call | tf_op jit(solution)/shard_map/far/pallas_call | solution.py:360
  46.1 2.1 %collective-permute-start.5 = (bf16[128,768]{1,0:T(8,128)(2,1)S(1)}, bf16[128,768]{1,0:T(8,128)(2,1)S(1)}, u32[]{:S(2)}, u32[]{:S(2)}) collective-permute-start(bf16[128,768]{1,0:T(8,128)(2,1)S(1)} %get-tuple-element.41), channel_id=1, source_target_pairs={{0,1},{1,0},{2,3},{3,2},{4,5},{5,4},{6,7},{7,6},{8,9},{9,8},{10,11... | collective-permute-start | bytes 589832 | tf_op jit(solution)/shard_map/ppermute | solution.py:404
  48.2 2.0 %normed.2 = bf16[128,1024]{1,0:T(8,128)(2,1)S(1)} custom-call(s32[5]{0:T(128)S(1)} %stack.23.plan_ref, bf16[8,512,256]{2,1,0:T(8,128)(2,1)} %outputs.1.parts_hbm.parts_ref, bf16[4,128,128]{2,1,0:T(8,128)(2,1)S(1)} %fusion.2.kept_ref, bf16[4,128,128]{2,1,0:T(8,128)(2,1)S(1)} %collective-permute-done.4.got_ref, ...), custom_call_target="tpu_custom_call" | custom-call | flops 33554432 | bytes 1048576 | tf_op jit(solution)/shard_map/normed/pallas_call | solution.py:380
  50.3 0.7 fusion.14
  51.1 0.7 convolution_convert_fusion.1
  51.9 1.6 %collective-permute-done.5 = bf16[128,768]{1,0:T(8,128)(2,1)S(1)} collective-permute-done((bf16[128,768]{1,0:T(8,128)(2,1)S(1)}, bf16[128,768]{1,0:T(8,128)(2,1)S(1)}, u32[]{:S(2)}, u32[]{:S(2)}) %collective-permute-start.5) | collective-permute-done | bytes 196640 | tf_op jit(solution)/shard_map/ppermute | solution.py:404
  53.6 2.8 %collective-permute-start.8 = (bf16[128,768]{1,0:T(8,128)(2,1)S(1)}, bf16[128,768]{1,0:T(8,128)(2,1)S(1)}, u32[]{:S(2)}, u32[]{:S(2)}) collective-permute-start(bf16[128,768]{1,0:T(8,128)(2,1)S(1)} %add_convert_fusion.3), channel_id=1, source_target_pairs={{0,2},{1,3},{2,0},{3,1},{4,6},{5,7},{6,4},{7,5},{8,10},{9,11},{10,... | collective-permute-start | bytes 589832 | tf_op jit(solution)/shard_map/ppermute | solution.py:404
  56.3 2.5 %normed.3 = bf16[256,1024]{1,0:T(8,128)(2,1)S(1)} custom-call(s32[5]{0:T(128)S(1)} %stack.23.plan_ref, bf16[8,512,256]{2,1,0:T(8,128)(2,1)} %outputs.1.parts_hbm.parts_ref, bf16[4,128,128]{2,1,0:T(8,128)(2,1)S(1)} %fusion.2.kept_ref, bf16[4,128,128]{2,1,0:T(8,128)(2,1)S(1)} %collective-permute-done.4.got_ref, ...), custom_call_target="tpu_custom_call" | custom-call | flops 67108864 | bytes 2097152 | tf_op jit(solution)/shard_map/normed/pallas_call | solution.py:380
  58.9 1.3 %convolution_convert_fusion = bf16[256,2048]{1,0:T(8,128)(2,1)S(1)} fusion(bf16[256,1024]{1,0:T(8,128)(2,1)S(1)} %normed.3, bf16[1024,2048]{1,0:T(8,128)(2,1)S(1)} %copy-done.1), kind=kOutput, calls=%fused_computation | convolution fusion | flops 1074266112 | bytes 5767168 | tf_op jit(solution)/shard_map/dot_general | solution.py:489
  60.2 2.4 %collective-permute-start.6 = (bf16[128,2048]{1,0:T(8,128)(2,1)S(1)}, bf16[128,2048]{1,0:T(8,128)(2,1)S(1)}, u32[]{:S(2)}, u32[]{:S(2)}) collective-permute-start(bf16[128,2048]{1,0:T(8,128)(2,1)S(1)} %slice.117), channel_id=1, source_target_pairs={{0,1},{1,0},{2,3},{3,2},{4,5},{5,4},{6,7},{7,6},{8,9},{9,8},{10,11... | collective-permute-start | bytes 1572872 | tf_op jit(solution)/shard_map/ppermute | solution.py:404
  62.6 3.3 %collective-permute-done.7 = bf16[128,1280]{1,0:T(8,128)(2,1)S(1)} collective-permute-done((bf16[128,1280]{1,0:T(8,128)(2,1)S(1)}, bf16[128,1280]{1,0:T(8,128)(2,1)S(1)}, u32[]{:S(2)}, u32[]{:S(2)}) %collective-permute-start.7) | collective-permute-done | bytes 327712 | tf_op jit(solution)/shard_map/ppermute | solution.py:404
  66.0 2.3 %collective-permute-start.9 = (bf16[128,1280]{1,0:T(8,128)(2,1)S(1)}, bf16[128,1280]{1,0:T(8,128)(2,1)S(1)}, u32[]{:S(2)}, u32[]{:S(2)}) collective-permute-start(bf16[128,1280]{1,0:T(8,128)(2,1)S(1)} %add_convert_fusion.1), channel_id=1, source_target_pairs={{0,2},{1,3},{2,0},{3,1},{4,6},{5,7},{6,4},{7,5},{8,10},{9,11},{10,... | collective-permute-start | bytes 983048 | tf_op jit(solution)/shard_map/ppermute | solution.py:404
  68.3 13.9 %collective-permute-done.9 = bf16[128,1280]{1,0:T(8,128)(2,1)S(1)} collective-permute-done((bf16[128,1280]{1,0:T(8,128)(2,1)S(1)}, bf16[128,1280]{1,0:T(8,128)(2,1)S(1)}, u32[]{:S(2)}, u32[]{:S(2)}) %collective-permute-start.9) | collective-permute-done | bytes 327712 | tf_op jit(solution)/shard_map/ppermute | solution.py:404
  82.3 0.8 collective-permute-done.6
  83.3 0.8 %pad_maximum_fusion = bf16[128,2048]{1,0:T(8,128)(2,1)} fusion(bf16[128,1280]{1,0:T(8,128)(2,1)S(1)} %add_convert_fusion, bf16[128,768]{1,0:T(8,128)(2,1)S(1)} %add_convert_fusion.2), kind=kLoop, calls=%fused_computation.17 | loop fusion | flops 1048576 | bytes 1048576 | tf_op jit(solution)/shard_map/concatenate | solution.py:508
  (52 shorter events, 1.4 us)
Async XLA Ops:
  0.0 1.6 %copy-start = (bf16[512,2048]{1,0:T(8,128)(2,1)S(1)}, bf16[512,2048]{1,0:T(8,128)(2,1)}, u32[]{:S(2)}) copy-start(bf16[512,2048]{1,0:T(8,128)(2,1)} %param.11) | copy-start | bytes 6291460
  0.0 4.7 %copy-start.10 = (bf16[2048,1024]{1,0:T(8,128)(2,1)S(1)}, bf16[2048,1024]{1,0:T(8,128)(2,1)}, u32[]{:S(2)}) copy-start(bf16[2048,1024]{1,0:T(8,128)(2,1)} %param.14) | copy-start | bytes 12582916
  4.7 2.4 %copy-start.8 = (bf16[512,512]{1,0:T(8,128)(2,1)}, bf16[512,512]{1,0:T(8,128)(2,1)S(1)}, u32[]{:S(2)}) copy-start(bf16[512,512]{1,0:T(8,128)(2,1)S(1)} %convolution_convert_fusion.5.keys_ref) | copy-start | bytes 1572868
  4.7 2.4 %copy-start.12 = (bf16[2048,512]{1,0:T(8,128)(2,1)S(1)}, bf16[2048,512]{1,0:T(8,128)(2,1)}, u32[]{:S(2)}) copy-start(bf16[2048,512]{1,0:T(8,128)(2,1)} %param.12) | copy-start | bytes 6291460
  7.1 1.3 %copy-start.9 = (bf16[512,1024]{1,0:T(8,128)(2,1)}, bf16[512,1024]{1,0:T(8,128)(2,1)S(1)}, u32[]{:S(2)}) copy-start(bf16[512,1024]{1,0:T(8,128)(2,1)S(1)} %convolution_convert_fusion.3.values_ref) | copy-start | bytes 3145732
  7.1 1.3 %slice-start = ((bf16[512,512]{1,0:T(8,128)(2,1)}), bf16[8,512]{1,0:T(8,128)(2,1)S(1)}, s32[]{:S(2)}) async-start(bf16[512,512]{1,0:T(8,128)(2,1)} %copy-done.8), calls=%async_computation | async-start | bytes 16384 | tf_op jit(solution)/shard_map/slice | solution.py:546
  7.1 6.5 %copy-start.2 = (f32[8,512]{1,0:T(8,128)S(1)}, f32[8,512]{1,0:T(8,128)}, u32[]{:S(2)}) copy-start(f32[8,512]{1,0:T(8,128)} %decay_ref.3) | copy-start | bytes 49156
  7.2 6.5 %copy-start.4 = (f32[4,1024]{1,0:T(4,128)S(1)}, f32[4,1024]{1,0:T(4,128)}, u32[]{:S(2)}) copy-start(f32[4,1024]{1,0:T(4,128)} %taps_v_ref.1) | copy-start | bytes 49156
  7.2 6.5 %copy-start.5 = (f32[8,512]{1,0:T(8,128)S(1)}, f32[8,512]{1,0:T(8,128)}, u32[]{:S(2)}) copy-start(f32[8,512]{1,0:T(8,128)} %write_ref.1) | copy-start | bytes 49156
  7.2 6.5 %copy-start.6 = (f32[4,512]{1,0:T(4,128)S(1)}, f32[4,512]{1,0:T(4,128)}, u32[]{:S(2)}) copy-start(f32[4,512]{1,0:T(4,128)} %taps_k_ref.1) | copy-start | bytes 24580
  8.5 17.5 %copy-start.7 = (bf16[512,512]{1,0:T(8,128)(2,1)}, bf16[512,512]{1,0:T(8,128)(2,1)S(1)}, u32[]{:S(2)}) copy-start(bf16[512,512]{1,0:T(8,128)(2,1)S(1)} %convolution_convert_fusion.4.query_ref) | copy-start | bytes 1572868
  8.5 5.2 %collective-permute-start = (bf16[8,2048]{1,0:T(8,128)(2,1)S(1)}, bf16[8,2048]{1,0:T(8,128)(2,1)S(1)}, u32[]{:S(2)}, u32[]{:S(2)}) collective-permute-start(bf16[8,2048]{1,0:T(8,128)(2,1)S(1)} %pad_maximum_fusion.3), channel_id=1, source_target_pairs={{0,4},{4,8},{8,12},{12,16},{16,20},{20,24},{24,28},{28,0},{1,5},{5... | collective-permute-start | bytes 98312 | tf_op jit(solution)/shard_map/ppermute | solution.py:549
  25.9 3.4 %copy-start.3 = (f32[4,512]{1,0:T(4,128)S(1)}, f32[4,512]{1,0:T(4,128)}, u32[]{:S(2)}) copy-start(f32[4,512]{1,0:T(4,128)} %taps_ref.1) | copy-start | bytes 24580
  26.0 1.6 %collective-permute-start.1 = (bf16[4,128,256]{2,1,0:T(8,128)(2,1)S(1)}, bf16[4,128,256]{2,1,0:T(8,128)(2,1)S(1)}, u32[]{:S(2)}, u32[]{:S(2)}) collective-permute-start(bf16[4,128,256]{2,1,0:T(8,128)(2,1)S(1)} %broadcast_select_fusion.5), channel_id=1, source_target_pairs={{0,4},{4,0},{8,12},{12,8},{16,20},{20,16},{24,28},{28,24},{1,5},{5... | collective-permute-start | bytes 786440 | tf_op jit(solution)/shard_map/ppermute | solution.py:404
  27.9 8.4 %collective-permute-start.2 = (bf16[4,128,256]{2,1,0:T(8,128)(2,1)S(1)}, bf16[4,128,256]{2,1,0:T(8,128)(2,1)S(1)}, u32[]{:S(2)}, u32[]{:S(2)}) collective-permute-start(bf16[4,128,256]{2,1,0:T(8,128)(2,1)S(1)} %fusion), channel_id=1, source_target_pairs={{0,8},{4,12},{8,0},{12,4},{16,24},{20,28},{24,16},{28,20},{1,9},{5... | collective-permute-start | bytes 786440 | tf_op jit(solution)/shard_map/ppermute | solution.py:404
  29.4 9.6 %copy-start.11 = (bf16[2048,1024]{1,0:T(8,128)(2,1)S(1)}, bf16[2048,1024]{1,0:T(8,128)(2,1)}, u32[]{:S(2)}) copy-start(bf16[2048,1024]{1,0:T(8,128)(2,1)} %param.15) | copy-start | bytes 12582916
  36.5 5.3 %collective-permute-start.3 = (bf16[4,128,128]{2,1,0:T(8,128)(2,1)S(1)}, bf16[4,128,128]{2,1,0:T(8,128)(2,1)S(1)}, u32[]{:S(2)}, u32[]{:S(2)}) collective-permute-start(bf16[4,128,128]{2,1,0:T(8,128)(2,1)S(1)} %add_convert_fusion.4), channel_id=1, source_target_pairs={{0,16},{4,20},{8,24},{12,28},{16,0},{20,4},{24,8},{28,12},{1,17},{... | collective-permute-start | bytes 393224 | tf_op jit(solution)/shard_map/ppermute | solution.py:404
  39.0 4.4 %copy-start.1 = (bf16[1024,2048]{1,0:T(8,128)(2,1)S(1)}, bf16[1024,2048]{1,0:T(8,128)(2,1)}, u32[]{:S(2)}) copy-start(bf16[1024,2048]{1,0:T(8,128)(2,1)} %weight_hbm.1) | copy-start | bytes 12582916
  42.0 1.4 %collective-permute-start.4 = (bf16[4,128,128]{2,1,0:T(8,128)(2,1)S(1)}, bf16[4,128,128]{2,1,0:T(8,128)(2,1)S(1)}, u32[]{:S(2)}, u32[]{:S(2)}) collective-permute-start(bf16[4,128,128]{2,1,0:T(8,128)(2,1)S(1)} %fusion.3), channel_id=1, source_target_pairs={{0,4},{4,0},{8,12},{12,8},{16,20},{20,16},{24,28},{28,24},{1,5},{5... | collective-permute-start | bytes 393224 | tf_op jit(solution)/shard_map/ppermute | solution.py:404
  46.1 7.4 %collective-permute-start.5 = (bf16[128,768]{1,0:T(8,128)(2,1)S(1)}, bf16[128,768]{1,0:T(8,128)(2,1)S(1)}, u32[]{:S(2)}, u32[]{:S(2)}) collective-permute-start(bf16[128,768]{1,0:T(8,128)(2,1)S(1)} %get-tuple-element.41), channel_id=1, source_target_pairs={{0,1},{1,0},{2,3},{3,2},{4,5},{5,4},{6,7},{7,6},{8,9},{9,8},{10,11... | collective-permute-start | bytes 589832 | tf_op jit(solution)/shard_map/ppermute | solution.py:404
  51.1 14.9 %collective-permute-start.7 = (bf16[128,1280]{1,0:T(8,128)(2,1)S(1)}, bf16[128,1280]{1,0:T(8,128)(2,1)S(1)}, u32[]{:S(2)}, u32[]{:S(2)}) collective-permute-start(bf16[128,1280]{1,0:T(8,128)(2,1)S(1)} %slice.163), channel_id=1, source_target_pairs={{0,1},{1,0},{2,3},{3,2},{4,5},{5,4},{6,7},{7,6},{8,9},{9,8},{10,11... | collective-permute-start | bytes 983048 | tf_op jit(solution)/shard_map/ppermute | solution.py:404
  53.6 12.4 %collective-permute-start.8 = (bf16[128,768]{1,0:T(8,128)(2,1)S(1)}, bf16[128,768]{1,0:T(8,128)(2,1)S(1)}, u32[]{:S(2)}, u32[]{:S(2)}) collective-permute-start(bf16[128,768]{1,0:T(8,128)(2,1)S(1)} %add_convert_fusion.3), channel_id=1, source_target_pairs={{0,2},{1,3},{2,0},{3,1},{4,6},{5,7},{6,4},{7,5},{8,10},{9,11},{10,... | collective-permute-start | bytes 589832 | tf_op jit(solution)/shard_map/ppermute | solution.py:404
  60.2 22.9 %collective-permute-start.6 = (bf16[128,2048]{1,0:T(8,128)(2,1)S(1)}, bf16[128,2048]{1,0:T(8,128)(2,1)S(1)}, u32[]{:S(2)}, u32[]{:S(2)}) collective-permute-start(bf16[128,2048]{1,0:T(8,128)(2,1)S(1)} %slice.117), channel_id=1, source_target_pairs={{0,1},{1,0},{2,3},{3,2},{4,5},{5,4},{6,7},{7,6},{8,9},{9,8},{10,11... | collective-permute-start | bytes 1572872 | tf_op jit(solution)/shard_map/ppermute | solution.py:404
  66.0 16.2 %collective-permute-start.9 = (bf16[128,1280]{1,0:T(8,128)(2,1)S(1)}, bf16[128,1280]{1,0:T(8,128)(2,1)S(1)}, u32[]{:S(2)}, u32[]{:S(2)}) collective-permute-start(bf16[128,1280]{1,0:T(8,128)(2,1)S(1)} %add_convert_fusion.1), channel_id=1, source_target_pairs={{0,2},{1,3},{2,0},{3,1},{4,6},{5,7},{6,4},{7,5},{8,10},{9,11},{10,... | collective-permute-start | bytes 983048 | tf_op jit(solution)/shard_map/ppermute | solution.py:404

commit v8 on v7

--- a/solution.py
+++ b/solution.py
@@ -502,13 +502,16 @@
     first = exchanged(paired, axis, 2)
     rest = mixed_rows(rows_of(2, 2, paired), w_out).reshape(2, -1, w_out.shape[1])
     later_in, first = lax.optimization_barrier((later_in, first))
-    later = exchanged(summed(passed[:, late], later_in), axis, 2)
-    near = exchanged(rest[0], axis, 1)
+    later = summed(passed[:, late], later_in)
+    near_early = exchanged(rest[0][:, early], axis, 1)
+    near_rows, _ = lax.optimization_barrier((rest[0][:, late], later))
+    later = exchanged(later, axis, 2)
+    near_late = exchanged(near_rows, axis, 1)
     own = rest[1]
     return jnp.concatenate(
         [
-            summed(own[:, early], near[:, early], first),
-            summed(own[:, late], near[:, late], later),
+            summed(own[:, early], near_early, first),
+            summed(own[:, late], near_late, later),
         ],
         axis=-1,
     )

time: 84.4 us -> 84.3 us (level)
  waiting for transfers between devices: 27.1 us -> 25.3 us
  starting transfers between devices: 14.3 us -> 15.9 us
    ppermute x9 -> x10, waiting for transfers between devices: 22.6 us -> 20.8 us  [exchanged(): lax.ppermute(value, axis, [(source, source ^ bit) for source in range(cou...]
    ppermute x9 -> x10, starting transfers between devices: 13.6 us -> 15.2 us  [exchanged(): lax.ppermute(value, axis, [(source, source ^ bit) for source in range(cou...]
  transfers between devices with their start and end apart: 10 -> 11, of which waited for: 8 -> 9; matrix products, arithmetic and copies ran while one was open for 7% -> 7% of each run, Pallas kernels for 14% -> 14%
where the time goes in v8:
time: 84.3 us; the launch traced here: 84.1 us
  Pallas kernels  26.4 us (31%)
  waiting for transfers between devices  25.3 us (30%)
  starting transfers between devices  15.9 us (19%)
  matrix products  12.8 us (15%)
  local copies, waits for them, and re-layouts  1.84 us (2%)
  other arithmetic  1.42 us (2%)
    ppermute x10, waiting for transfers between devices, exchanged(): lax.ppermute(value, axis, [(source, source ^ bit) for source in range(cou...  20.8 us
    ppermute x10, starting transfers between devices, exchanged(): lax.ppermute(value, axis, [(source, source ^ bit) for source in range(cou...  15.2 us
    pallas_call x1, Pallas kernels, shards(): pl.pallas_call(functools.partial(local_kernel, group, ratio, chunks), gri...  12.2 us
    dot_general x4, matrix products, project(): return jnp.dot(tokens, weights, preferred_element_type=F32).astype(BF)  9.06 us
    pallas_call x1, Pallas kernels, shards(): pl.pallas_call(functools.partial(output_kernel, group, ratio, chunks), gr...  6.86 us
    pallas_call x2, Pallas kernels, normed_rows(): pl.pallas_call(functools.partial(norm_kernel, heads), grid_spec=pltpu.Pre...  4.54 us
    ppermute x1, waiting for transfers between devices, shards(): lax.ppermute(tails, 'ctx', [(at, (at + 1) % count) for at in range(count)])  4.48 us
    dot_general x3, matrix products, mixed_rows(): return jnp.dot(normed, w_out, preferred_element_type=F32).astype(BF)  2.73 us
  transfers between devices with their start and end apart: 11, of which 9 were waited for; matrix products, arithmetic and copies ran while one was open for 7% of the time, Pallas kernels for 14%

profile of v8, /device:TPU:0, one launch (start us, length us, event | category | flops | bytes accessed | tf_op | source)
XLA Modules:
  0.0 84.1 jit_solution(15953104543160610569)
XLA Ops:
  0.0 1.6 %copy-done = bf16[512,2048]{1,0:T(8,128)(2,1)S(1)} copy-done((bf16[512,2048]{1,0:T(8,128)(2,1)S(1)}, bf16[512,2048]{1,0:T(8,128)(2,1)}, u32[]{:S(2)}) %copy-start) | copy-done | bytes 2097176
  1.6 3.1 %convolution_convert_fusion.5.keys_ref = bf16[512,512]{1,0:T(8,128)(2,1)S(1)} fusion(bf16[512,2048]{1,0:T(8,128)(2,1)S(1)} %copy-done, bf16[2048,512]{1,0:T(8,128)(2,1)} %param.13), kind=kOutput, calls=%fused_computation.5 | convolution fusion | flops 1074003968 | bytes 4718592 | tf_op jit(solution)/shard_map/dot_general | solution.py:537
  4.7 2.4 %convolution_convert_fusion.3.values_ref = bf16[512,1024]{1,0:T(8,128)(2,1)S(1)} fusion(bf16[512,2048]{1,0:T(8,128)(2,1)S(1)} %copy-done, bf16[2048,1024]{1,0:T(8,128)(2,1)S(1)} %copy-done.10), kind=kOutput, calls=%fused_computation.3 | convolution fusion | flops 2148007936 | bytes 7340032 | tf_op jit(solution)/shard_map/dot_general | solution.py:537
  7.2 1.2 %convolution_convert_fusion.4.query_ref = bf16[512,512]{1,0:T(8,128)(2,1)S(1)} fusion(bf16[512,2048]{1,0:T(8,128)(2,1)S(1)} %copy-done, bf16[2048,512]{1,0:T(8,128)(2,1)S(1)} %copy-done.12), kind=kOutput, calls=%fused_computation.4 | convolution fusion | flops 1074003968 | bytes 4718592 | tf_op jit(solution)/shard_map/dot_general | solution.py:537
  8.5 0.7 collective-permute-start
  9.2 4.5 %collective-permute-done.rims_k_ref.rims_v_ref.rims_ref = bf16[8,2048]{1,0:T(8,128)(2,1)S(1)} collective-permute-done((bf16[8,2048]{1,0:T(8,128)(2,1)S(1)}, bf16[8,2048]{1,0:T(8,128)(2,1)S(1)}, u32[]{:S(2)}, u32[]{:S(2)}) %collective-permute-start) | collective-permute-done | bytes 32800 | tf_op jit(solution)/shard_map/ppermute | solution.py:552
  13.7 12.2 %local.1 = (bf16[512,512]{1,0:T(8,128)(2,1)}, bf16[8,512,256]{2,1,0:T(8,128)(2,1)}, bf16[8,3,128,256]{3,2,1,0:T(8,128)(2,1)}, bf16[8,128,256]{2,1,0:T(8,128)(2,1)S(1)}) custom-call(s32[1]{0:T(128)} %bitcast.5.at_ref, bf16[512,512]{1,0:T(8,128)(2,1)} %copy-done.8, bf16[512,1024]{1,0:T(8,128)(2,1)} %copy-done.9, ...), custom_call_target="tpu_custom_call" | custom-call | flops 2147483648 | bytes 6291456 | tf_op jit(solution)/shard_map/local/pallas_call | solution.py:564
  26.1 1.5 %collective-permute-done.1 = bf16[4,128,256]{2,1,0:T(8,128)(2,1)S(1)} collective-permute-done((bf16[4,128,256]{2,1,0:T(8,128)(2,1)S(1)}, bf16[4,128,256]{2,1,0:T(8,128)(2,1)S(1)}, u32[]{:S(2)}, u32[]{:S(2)}) %collective-permute-start.1) | collective-permute-done | bytes 262176 | tf_op jit(solution)/shard_map/ppermute | solution.py:404
  27.6 0.2 fusion
  27.9 1.4 %collective-permute-start.2 = (bf16[4,128,256]{2,1,0:T(8,128)(2,1)S(1)}, bf16[4,128,256]{2,1,0:T(8,128)(2,1)S(1)}, u32[]{:S(2)}, u32[]{:S(2)}) collective-permute-start(bf16[4,128,256]{2,1,0:T(8,128)(2,1)S(1)} %fusion), channel_id=1, source_target_pairs={{0,8},{4,12},{8,0},{12,4},{16,24},{20,28},{24,16},{28,20},{1,9},{5... | collective-permute-start | bytes 786440 | tf_op jit(solution)/shard_map/ppermute | solution.py:404
  29.4 6.9 %outputs.1.parts_hbm.parts_ref = bf16[8,512,256]{2,1,0:T(8,128)(2,1)} custom-call(s32[1]{0:T(128)} %bitcast.5.at_ref, bf16[512,512]{1,0:T(8,128)(2,1)} %copy-done.7, bf16[8,2048]{1,0:T(8,128)(2,1)S(1)} %collective-permute-done.rims_k_ref.rims_v_ref.rims_ref, f32[4,512]{1,0:T(4,128)S(1)} %copy-done.3, bf16[512,512]{1,0:T(8,128)(2,1)} %get-tuple-element.30.keys_ref, ...), custom_call_target="tpu_custom_call" | custom-call | flops 1073741824 | bytes 6291456 | tf_op jit(solution)/shard_map/outputs/pallas_call | solution.py:598
  36.5 2.3 %collective-permute-start.3 = (bf16[4,128,128]{2,1,0:T(8,128)(2,1)S(1)}, bf16[4,128,128]{2,1,0:T(8,128)(2,1)S(1)}, u32[]{:S(2)}, u32[]{:S(2)}) collective-permute-start(bf16[4,128,128]{2,1,0:T(8,128)(2,1)S(1)} %add_convert_fusion.4), channel_id=1, source_target_pairs={{0,16},{4,20},{8,24},{12,28},{16,0},{20,4},{24,8},{28,12},{1,17},{... | collective-permute-start | bytes 393224 | tf_op jit(solution)/shard_map/ppermute | solution.py:404
  39.0 2.4 %convolution_convert_fusion.2.gate_ref = bf16[512,1024]{1,0:T(8,128)(2,1)S(1)} fusion(bf16[512,2048]{1,0:T(8,128)(2,1)S(1)} %copy-done, bf16[2048,1024]{1,0:T(8,128)(2,1)S(1)} %copy-done.11), kind=kOutput, calls=%fused_computation.2 | convolution fusion | flops 2148007936 | bytes 7340032 | tf_op jit(solution)/shard_map/dot_general | solution.py:537
  41.3 0.2 broadcast_select_fusion.1
  42.2 1.2 %collective-permute-done.4.got_ref = bf16[4,128,128]{2,1,0:T(8,128)(2,1)S(1)} collective-permute-done((bf16[4,128,128]{2,1,0:T(8,128)(2,1)S(1)}, bf16[4,128,128]{2,1,0:T(8,128)(2,1)S(1)}, u32[]{:S(2)}, u32[]{:S(2)}) %collective-permute-start.4) | collective-permute-done | bytes 131104 | tf_op jit(solution)/shard_map/ppermute | solution.py:404
  43.4 2.7 %far.1 = (bf16[128,768]{1,0:T(8,128)(2,1)S(1)}, bf16[128,1024]{1,0:T(8,128)(2,1)S(1)}) custom-call(s32[5]{0:T(128)S(1)} %stack.23.plan_ref, bf16[8,512,256]{2,1,0:T(8,128)(2,1)} %outputs.1.parts_hbm.parts_ref, bf16[4,128,128]{2,1,0:T(8,128)(2,1)S(1)} %fusion.2.kept_ref, bf16[4,128,128]{2,1,0:T(8,128)(2,1)S(1)} %collective-permute-done.4.got_ref, ...), custom_call_target="tpu_custom_call" | custom-call | tf_op jit(solution)/shard_map/far/pallas_call | solution.py:360
  46.1 2.1 %collective-permute-start.5 = (bf16[128,768]{1,0:T(8,128)(2,1)S(1)}, bf16[128,768]{1,0:T(8,128)(2,1)S(1)}, u32[]{:S(2)}, u32[]{:S(2)}) collective-permute-start(bf16[128,768]{1,0:T(8,128)(2,1)S(1)} %get-tuple-element.42), channel_id=1, source_target_pairs={{0,1},{1,0},{2,3},{3,2},{4,5},{5,4},{6,7},{7,6},{8,9},{9,8},{10,11... | collective-permute-start | bytes 589832 | tf_op jit(solution)/shard_map/ppermute | solution.py:404
  48.2 2.0 %normed.2 = bf16[128,1024]{1,0:T(8,128)(2,1)S(1)} custom-call(s32[5]{0:T(128)S(1)} %stack.23.plan_ref, bf16[8,512,256]{2,1,0:T(8,128)(2,1)} %outputs.1.parts_hbm.parts_ref, bf16[4,128,128]{2,1,0:T(8,128)(2,1)S(1)} %fusion.2.kept_ref, bf16[4,128,128]{2,1,0:T(8,128)(2,1)S(1)} %collective-permute-done.4.got_ref, ...), custom_call_target="tpu_custom_call" | custom-call | flops 33554432 | bytes 1048576 | tf_op jit(solution)/shard_map/normed/pallas_call | solution.py:380
  50.3 0.7 fusion.14
  51.1 0.7 convolution_convert_fusion.1
  51.9 1.6 %collective-permute-done.5 = bf16[128,768]{1,0:T(8,128)(2,1)S(1)} collective-permute-done((bf16[128,768]{1,0:T(8,128)(2,1)S(1)}, bf16[128,768]{1,0:T(8,128)(2,1)S(1)}, u32[]{:S(2)}, u32[]{:S(2)}) %collective-permute-start.5) | collective-permute-done | bytes 196640 | tf_op jit(solution)/shard_map/ppermute | solution.py:404
  53.6 2.8 %collective-permute-start.8 = (bf16[128,768]{1,0:T(8,128)(2,1)S(1)}, bf16[128,768]{1,0:T(8,128)(2,1)S(1)}, u32[]{:S(2)}, u32[]{:S(2)}) collective-permute-start(bf16[128,768]{1,0:T(8,128)(2,1)S(1)} %add_convert_fusion.3), channel_id=1, source_target_pairs={{0,2},{1,3},{2,0},{3,1},{4,6},{5,7},{6,4},{7,5},{8,10},{9,11},{10,... | collective-permute-start | bytes 589832 | tf_op jit(solution)/shard_map/ppermute | solution.py:404
  56.3 2.5 %normed.3 = bf16[256,1024]{1,0:T(8,128)(2,1)S(1)} custom-call(s32[5]{0:T(128)S(1)} %stack.23.plan_ref, bf16[8,512,256]{2,1,0:T(8,128)(2,1)} %outputs.1.parts_hbm.parts_ref, bf16[4,128,128]{2,1,0:T(8,128)(2,1)S(1)} %fusion.2.kept_ref, bf16[4,128,128]{2,1,0:T(8,128)(2,1)S(1)} %collective-permute-done.4.got_ref, ...), custom_call_target="tpu_custom_call" | custom-call | flops 67108864 | bytes 2097152 | tf_op jit(solution)/shard_map/normed/pallas_call | solution.py:380
  58.9 1.3 %convolution_convert_fusion = bf16[256,2048]{1,0:T(8,128)(2,1)S(1)} fusion(bf16[256,1024]{1,0:T(8,128)(2,1)S(1)} %normed.3, bf16[1024,2048]{1,0:T(8,128)(2,1)S(1)} %copy-done.1), kind=kOutput, calls=%fused_computation | convolution fusion | flops 1074266112 | bytes 5767168 | tf_op jit(solution)/shard_map/dot_general | solution.py:489
  60.2 2.4 %collective-permute-start.6 = (bf16[128,768]{1,0:T(8,128)(2,1)S(1)}, bf16[128,768]{1,0:T(8,128)(2,1)S(1)}, u32[]{:S(2)}, u32[]{:S(2)}) collective-permute-start(bf16[128,768]{1,0:T(8,128)(2,1)S(1)} %slice.117), channel_id=1, source_target_pairs={{0,1},{1,0},{2,3},{3,2},{4,5},{5,4},{6,7},{7,6},{8,9},{9,8},{10,11... | collective-permute-start | bytes 589832 | tf_op jit(solution)/shard_map/ppermute | solution.py:404
  62.6 3.3 %collective-permute-done.7 = bf16[128,1280]{1,0:T(8,128)(2,1)S(1)} collective-permute-done((bf16[128,1280]{1,0:T(8,128)(2,1)S(1)}, bf16[128,1280]{1,0:T(8,128)(2,1)S(1)}, u32[]{:S(2)}, u32[]{:S(2)}) %collective-permute-start.7) | collective-permute-done | bytes 327712 | tf_op jit(solution)/shard_map/ppermute | solution.py:404
  66.0 2.3 %collective-permute-start.10 = (bf16[128,1280]{1,0:T(8,128)(2,1)S(1)}, bf16[128,1280]{1,0:T(8,128)(2,1)S(1)}, u32[]{:S(2)}, u32[]{:S(2)}) collective-permute-start(bf16[128,1280]{1,0:T(8,128)(2,1)S(1)} %add_convert_fusion.1), channel_id=1, source_target_pairs={{0,2},{1,3},{2,0},{3,1},{4,6},{5,7},{6,4},{7,5},{8,10},{9,11},{10,... | collective-permute-start | bytes 983048 | tf_op jit(solution)/shard_map/ppermute | solution.py:404
  68.3 1.6 %collective-permute-start.9 = (bf16[128,1280]{1,0:T(8,128)(2,1)S(1)}, bf16[128,1280]{1,0:T(8,128)(2,1)S(1)}, u32[]{:S(2)}, u32[]{:S(2)}) collective-permute-start(bf16[128,1280]{1,0:T(8,128)(2,1)S(1)} %slice.119), channel_id=1, source_target_pairs={{0,1},{1,0},{2,3},{3,2},{4,5},{5,4},{6,7},{7,6},{8,9},{9,8},{10,11... | collective-permute-start | bytes 983048 | tf_op jit(solution)/shard_map/ppermute | solution.py:404
  70.0 3.4 %collective-permute-done.6 = bf16[128,768]{1,0:T(8,128)(2,1)S(1)} collective-permute-done((bf16[128,768]{1,0:T(8,128)(2,1)S(1)}, bf16[128,768]{1,0:T(8,128)(2,1)S(1)}, u32[]{:S(2)}, u32[]{:S(2)}) %collective-permute-start.6) | collective-permute-done | bytes 196640 | tf_op jit(solution)/shard_map/ppermute | solution.py:404
  73.5 8.5 %collective-permute-done.10 = bf16[128,1280]{1,0:T(8,128)(2,1)S(1)} collective-permute-done((bf16[128,1280]{1,0:T(8,128)(2,1)S(1)}, bf16[128,1280]{1,0:T(8,128)(2,1)S(1)}, u32[]{:S(2)}, u32[]{:S(2)}) %collective-permute-start.10) | collective-permute-done | bytes 327712 | tf_op jit(solution)/shard_map/ppermute | solution.py:404
  82.0 1.0 %collective-permute-done.9 = bf16[128,1280]{1,0:T(8,128)(2,1)S(1)} collective-permute-done((bf16[128,1280]{1,0:T(8,128)(2,1)S(1)}, bf16[128,1280]{1,0:T(8,128)(2,1)S(1)}, u32[]{:S(2)}, u32[]{:S(2)}) %collective-permute-start.9) | collective-permute-done | bytes 327712 | tf_op jit(solution)/shard_map/ppermute | solution.py:404
  83.2 0.8 %pad_maximum_fusion = bf16[128,2048]{1,0:T(8,128)(2,1)} fusion(bf16[128,1280]{1,0:T(8,128)(2,1)S(1)} %add_convert_fusion, bf16[128,768]{1,0:T(8,128)(2,1)S(1)} %add_convert_fusion.2), kind=kLoop, calls=%fused_computation.17 | loop fusion | flops 1048576 | bytes 1048576 | tf_op jit(solution)/shard_map/concatenate | solution.py:511
  (55 shorter events, 1.8 us)
Async XLA Ops:
  0.0 1.6 %copy-start = (bf16[512,2048]{1,0:T(8,128)(2,1)S(1)}, bf16[512,2048]{1,0:T(8,128)(2,1)}, u32[]{:S(2)}) copy-start(bf16[512,2048]{1,0:T(8,128)(2,1)} %param.11) | copy-start | bytes 6291460
  0.0 4.7 %copy-start.10 = (bf16[2048,1024]{1,0:T(8,128)(2,1)S(1)}, bf16[2048,1024]{1,0:T(8,128)(2,1)}, u32[]{:S(2)}) copy-start(bf16[2048,1024]{1,0:T(8,128)(2,1)} %param.14) | copy-start | bytes 12582916
  4.7 2.4 %copy-start.8 = (bf16[512,512]{1,0:T(8,128)(2,1)}, bf16[512,512]{1,0:T(8,128)(2,1)S(1)}, u32[]{:S(2)}) copy-start(bf16[512,512]{1,0:T(8,128)(2,1)S(1)} %convolution_convert_fusion.5.keys_ref) | copy-start | bytes 1572868
  4.7 2.4 %copy-start.12 = (bf16[2048,512]{1,0:T(8,128)(2,1)S(1)}, bf16[2048,512]{1,0:T(8,128)(2,1)}, u32[]{:S(2)}) copy-start(bf16[2048,512]{1,0:T(8,128)(2,1)} %param.12) | copy-start | bytes 6291460
  7.1 1.3 %copy-start.9 = (bf16[512,1024]{1,0:T(8,128)(2,1)}, bf16[512,1024]{1,0:T(8,128)(2,1)S(1)}, u32[]{:S(2)}) copy-start(bf16[512,1024]{1,0:T(8,128)(2,1)S(1)} %convolution_convert_fusion.3.values_ref) | copy-start | bytes 3145732
  7.1 1.3 %slice-start = ((bf16[512,512]{1,0:T(8,128)(2,1)}), bf16[8,512]{1,0:T(8,128)(2,1)S(1)}, s32[]{:S(2)}) async-start(bf16[512,512]{1,0:T(8,128)(2,1)} %copy-done.8), calls=%async_computation | async-start | bytes 16384 | tf_op jit(solution)/shard_map/slice | solution.py:549
  7.1 6.5 %copy-start.2 = (f32[8,512]{1,0:T(8,128)S(1)}, f32[8,512]{1,0:T(8,128)}, u32[]{:S(2)}) copy-start(f32[8,512]{1,0:T(8,128)} %decay_ref.3) | copy-start | bytes 49156
  7.2 6.5 %copy-start.4 = (f32[4,1024]{1,0:T(4,128)S(1)}, f32[4,1024]{1,0:T(4,128)}, u32[]{:S(2)}) copy-start(f32[4,1024]{1,0:T(4,128)} %taps_v_ref.1) | copy-start | bytes 49156
  7.2 6.5 %copy-start.5 = (f32[8,512]{1,0:T(8,128)S(1)}, f32[8,512]{1,0:T(8,128)}, u32[]{:S(2)}) copy-start(f32[8,512]{1,0:T(8,128)} %write_ref.1) | copy-start | bytes 49156
  7.2 6.5 %copy-start.6 = (f32[4,512]{1,0:T(4,128)S(1)}, f32[4,512]{1,0:T(4,128)}, u32[]{:S(2)}) copy-start(f32[4,512]{1,0:T(4,128)} %taps_k_ref.1) | copy-start | bytes 24580
  8.5 17.5 %copy-start.7 = (bf16[512,512]{1,0:T(8,128)(2,1)}, bf16[512,512]{1,0:T(8,128)(2,1)S(1)}, u32[]{:S(2)}) copy-start(bf16[512,512]{1,0:T(8,128)(2,1)S(1)} %convolution_convert_fusion.4.query_ref) | copy-start | bytes 1572868
  8.5 5.2 %collective-permute-start = (bf16[8,2048]{1,0:T(8,128)(2,1)S(1)}, bf16[8,2048]{1,0:T(8,128)(2,1)S(1)}, u32[]{:S(2)}, u32[]{:S(2)}) collective-permute-start(bf16[8,2048]{1,0:T(8,128)(2,1)S(1)} %pad_maximum_fusion.3), channel_id=1, source_target_pairs={{0,4},{4,8},{8,12},{12,16},{16,20},{20,24},{24,28},{28,0},{1,5},{5... | collective-permute-start | bytes 98312 | tf_op jit(solution)/shard_map/ppermute | solution.py:552
  25.9 3.4 %copy-start.3 = (f32[4,512]{1,0:T(4,128)S(1)}, f32[4,512]{1,0:T(4,128)}, u32[]{:S(2)}) copy-start(f32[4,512]{1,0:T(4,128)} %taps_ref.1) | copy-start | bytes 24580
  26.0 1.6 %collective-permute-start.1 = (bf16[4,128,256]{2,1,0:T(8,128)(2,1)S(1)}, bf16[4,128,256]{2,1,0:T(8,128)(2,1)S(1)}, u32[]{:S(2)}, u32[]{:S(2)}) collective-permute-start(bf16[4,128,256]{2,1,0:T(8,128)(2,1)S(1)} %broadcast_select_fusion.5), channel_id=1, source_target_pairs={{0,4},{4,0},{8,12},{12,8},{16,20},{20,16},{24,28},{28,24},{1,5},{5... | collective-permute-start | bytes 786440 | tf_op jit(solution)/shard_map/ppermute | solution.py:404
  27.9 8.4 %collective-permute-start.2 = (bf16[4,128,256]{2,1,0:T(8,128)(2,1)S(1)}, bf16[4,128,256]{2,1,0:T(8,128)(2,1)S(1)}, u32[]{:S(2)}, u32[]{:S(2)}) collective-permute-start(bf16[4,128,256]{2,1,0:T(8,128)(2,1)S(1)} %fusion), channel_id=1, source_target_pairs={{0,8},{4,12},{8,0},{12,4},{16,24},{20,28},{24,16},{28,20},{1,9},{5... | collective-permute-start | bytes 786440 | tf_op jit(solution)/shard_map/ppermute | solution.py:404
  29.4 9.6 %copy-start.11 = (bf16[2048,1024]{1,0:T(8,128)(2,1)S(1)}, bf16[2048,1024]{1,0:T(8,128)(2,1)}, u32[]{:S(2)}) copy-start(bf16[2048,1024]{1,0:T(8,128)(2,1)} %param.15) | copy-start | bytes 12582916
  36.5 5.3 %collective-permute-start.3 = (bf16[4,128,128]{2,1,0:T(8,128)(2,1)S(1)}, bf16[4,128,128]{2,1,0:T(8,128)(2,1)S(1)}, u32[]{:S(2)}, u32[]{:S(2)}) collective-permute-start(bf16[4,128,128]{2,1,0:T(8,128)(2,1)S(1)} %add_convert_fusion.4), channel_id=1, source_target_pairs={{0,16},{4,20},{8,24},{12,28},{16,0},{20,4},{24,8},{28,12},{1,17},{... | collective-permute-start | bytes 393224 | tf_op jit(solution)/shard_map/ppermute | solution.py:404
  39.0 4.4 %copy-start.1 = (bf16[1024,2048]{1,0:T(8,128)(2,1)S(1)}, bf16[1024,2048]{1,0:T(8,128)(2,1)}, u32[]{:S(2)}) copy-start(bf16[1024,2048]{1,0:T(8,128)(2,1)} %weight_hbm.1) | copy-start | bytes 12582916
  42.0 1.4 %collective-permute-start.4 = (bf16[4,128,128]{2,1,0:T(8,128)(2,1)S(1)}, bf16[4,128,128]{2,1,0:T(8,128)(2,1)S(1)}, u32[]{:S(2)}, u32[]{:S(2)}) collective-permute-start(bf16[4,128,128]{2,1,0:T(8,128)(2,1)S(1)} %fusion.3), channel_id=1, source_target_pairs={{0,4},{4,0},{8,12},{12,8},{16,20},{20,16},{24,28},{28,24},{1,5},{5... | collective-permute-start | bytes 393224 | tf_op jit(solution)/shard_map/ppermute | solution.py:404
  46.1 7.4 %collective-permute-start.5 = (bf16[128,768]{1,0:T(8,128)(2,1)S(1)}, bf16[128,768]{1,0:T(8,128)(2,1)S(1)}, u32[]{:S(2)}, u32[]{:S(2)}) collective-permute-start(bf16[128,768]{1,0:T(8,128)(2,1)S(1)} %get-tuple-element.42), channel_id=1, source_target_pairs={{0,1},{1,0},{2,3},{3,2},{4,5},{5,4},{6,7},{7,6},{8,9},{9,8},{10,11... | collective-permute-start | bytes 589832 | tf_op jit(solution)/shard_map/ppermute | solution.py:404
  51.0 14.9 %collective-permute-start.7 = (bf16[128,1280]{1,0:T(8,128)(2,1)S(1)}, bf16[128,1280]{1,0:T(8,128)(2,1)S(1)}, u32[]{:S(2)}, u32[]{:S(2)}) collective-permute-start(bf16[128,1280]{1,0:T(8,128)(2,1)S(1)} %slice.160), channel_id=1, source_target_pairs={{0,1},{1,0},{2,3},{3,2},{4,5},{5,4},{6,7},{7,6},{8,9},{9,8},{10,11... | collective-permute-start | bytes 983048 | tf_op jit(solution)/shard_map/ppermute | solution.py:404
  53.6 12.4 %collective-permute-start.8 = (bf16[128,768]{1,0:T(8,128)(2,1)S(1)}, bf16[128,768]{1,0:T(8,128)(2,1)S(1)}, u32[]{:S(2)}, u32[]{:S(2)}) collective-permute-start(bf16[128,768]{1,0:T(8,128)(2,1)S(1)} %add_convert_fusion.3), channel_id=1, source_target_pairs={{0,2},{1,3},{2,0},{3,1},{4,6},{5,7},{6,4},{7,5},{8,10},{9,11},{10,... | collective-permute-start | bytes 589832 | tf_op jit(solution)/shard_map/ppermute | solution.py:404
  60.2 13.2 %collective-permute-start.6 = (bf16[128,768]{1,0:T(8,128)(2,1)S(1)}, bf16[128,768]{1,0:T(8,128)(2,1)S(1)}, u32[]{:S(2)}, u32[]{:S(2)}) collective-permute-start(bf16[128,768]{1,0:T(8,128)(2,1)S(1)} %slice.117), channel_id=1, source_target_pairs={{0,1},{1,0},{2,3},{3,2},{4,5},{5,4},{6,7},{7,6},{8,9},{9,8},{10,11... | collective-permute-start | bytes 589832 | tf_op jit(solution)/shard_map/ppermute | solution.py:404
  66.0 16.0 %collective-permute-start.10 = (bf16[128,1280]{1,0:T(8,128)(2,1)S(1)}, bf16[128,1280]{1,0:T(8,128)(2,1)S(1)}, u32[]{:S(2)}, u32[]{:S(2)}) collective-permute-start(bf16[128,1280]{1,0:T(8,128)(2,1)S(1)} %add_convert_fusion.1), channel_id=1, source_target_pairs={{0,2},{1,3},{2,0},{3,1},{4,6},{5,7},{6,4},{7,5},{8,10},{9,11},{10,... | collective-permute-start | bytes 983048 | tf_op jit(solution)/shard_map/ppermute | solution.py:404
  68.3 14.7 %collective-permute-start.9 = (bf16[128,1280]{1,0:T(8,128)(2,1)S(1)}, bf16[128,1280]{1,0:T(8,128)(2,1)S(1)}, u32[]{:S(2)}, u32[]{:S(2)}) collective-permute-start(bf16[128,1280]{1,0:T(8,128)(2,1)S(1)} %slice.119), channel_id=1, source_target_pairs={{0,1},{1,0},{2,3},{3,2},{4,5},{5,4},{6,7},{7,6},{8,9},{9,8},{10,11... | collective-permute-start | bytes 983048 | tf_op jit(solution)/shard_map/ppermute | solution.py:404
